TPU v7x, 128 devices: a whole 4x4x4 slice. The times are simulated.
128 devices in a mesh: freq: 8 (over x, core), space: 16 (over y, z).
Axes of the slice: x: 4, y: 4, z: 4, core: 2. Of those that a mesh axis runs over, the one named last changes fastest.
Arguments:
- traces: float32 [128, 128, 2048], P('space', 'freq'), may hold values from -6 to 6
- kept_bins: int32 [8], replicated, may hold values from 8 to 1015, as said below
- start_basis: float32 [8, 2, 40, 256], P('freq'), may hold values from -6 to 6
Outputs:
- denoised: float32 [128, 128, 2048], P('space', 'freq')
Inputs may be any that keep to these rules, and one draw needn't show every extreme that they name: `kept_bins`: 8 distinct bins in rising order; the first is the band's lower limit and the last its upper limit.
All inputs are finite; a program needn't handle non-finite values.
Results may differ from a plain program's by a relative error of at most 0.00019.
Values sent between devices are 32-bit elements; how exact they have to be, the bound alone decides.
A program may use at most 128 MiB of HBM per device.

v0:
```python
import math

import jax
import jax.numpy as jnp
from jax import lax
from jax.experimental import pallas as pl
from jax.experimental.pallas import tpu as pltpu
from jax.sharding import PartitionSpec as P

NT = 2048
LX = 8
LY = 32
RANK = 40
POWER = 4
CADZOW = 2


exact_mode = lax.Precision.HIGHEST


def shifted(x, axis, by):
    count = lax.axis_size(axis)
    pairs = [(i, i + by) for i in range(count) if 0 <= i + by < count]
    return lax.ppermute(x, axis, pairs)


def all_sum(x, axis):
    count = lax.axis_size(axis)
    chunks = x.reshape(count, -1)
    mine = lax.all_to_all(chunks, axis, 0, 0, tiled=True).sum(axis=0)
    copies = jnp.broadcast_to(mine[None], (count, mine.shape[0]))
    return lax.all_to_all(copies, axis, 0, 0, tiled=True).reshape(x.shape)


def product(form, left, right, precision=exact_mode):
    return jnp.einsum(form, left, right, precision=precision, preferred_element_type=jnp.float32)


def tables(kept_bins):
    samples = jnp.arange(NT, dtype=jnp.int32)
    phases = samples[:, None] * kept_bins[None, :] % NT
    angles = phases.astype(jnp.float32) * (2.0 * math.pi / NT)
    return (jnp.cos(angles), jnp.sin(angles))


def paired(start):
    real_rows = jnp.concatenate([start[:, 0], -start[:, 1]], axis=1)
    imag_rows = jnp.concatenate([start[:, 1], start[:, 0]], axis=1)
    return jnp.concatenate([real_rows, imag_rows], axis=2)


def shift_matrix(length, lags, limit):
    shape = (length, lags, length)
    z = lax.broadcasted_iota(jnp.int32, shape, 0)
    b = lax.broadcasted_iota(jnp.int32, shape, 1)
    y = lax.broadcasted_iota(jnp.int32, shape, 2)
    return ((z == y + b) & (y < limit)).astype(jnp.float32)


def realified(real_part, imag_part):
    top = jnp.concatenate([real_part, -imag_part], axis=-1)
    bottom = jnp.concatenate([imag_part, real_part], axis=-1)
    return jnp.concatenate([top, bottom], axis=-2)


def packed(real_part, imag_part):
    upper = lax.broadcasted_iota(jnp.int32, real_part.shape, real_part.ndim - 2) <= lax.broadcasted_iota(
        jnp.int32, real_part.shape, real_part.ndim - 1
    )
    return jnp.where(upper, real_part, imag_part)


def unpacked(square):
    row_id = lax.broadcasted_iota(jnp.int32, square.shape, square.ndim - 2)
    col_id = lax.broadcasted_iota(jnp.int32, square.shape, square.ndim - 1)
    mirrored = jnp.swapaxes(square, -1, -2)
    real_part = jnp.where(row_id <= col_id, square, mirrored)
    imag_part = jnp.where(row_id > col_id, square, jnp.where(row_id == col_id, 0.0, -mirrored))
    return real_part, imag_part


def inverse_factor(left):
    count, width = left.shape
    half = width // 2
    row_id = lax.broadcasted_iota(jnp.int32, left.shape, 0)
    lane_id = lax.broadcasted_iota(jnp.int32, left.shape, 1)
    sign = jnp.where(lane_id[:1] < half, -1.0, 1.0)
    rows_only = row_id[:, :1]

    def body(k, carry):
        left, inverse, pivots = carry
        at_row = row_id == k
        col_real = jnp.sum(jnp.where(lane_id == k, left, 0.0), axis=1, keepdims=True)
        col_imag = jnp.sum(jnp.where(lane_id == k + half, left, 0.0), axis=1, keepdims=True)
        row_left = jnp.sum(jnp.where(at_row, left, 0.0), axis=0, keepdims=True)
        row_inverse = jnp.sum(jnp.where(at_row, inverse, 0.0), axis=0, keepdims=True)
        pivot = jnp.sum(jnp.where(rows_only == k, col_real, 0.0), axis=0, keepdims=True)
        scale = 1.0 / pivot
        below = rows_only > k
        by_real = jnp.where(below, col_real, 0.0) * scale
        by_imag = jnp.where(below, col_imag, 0.0) * scale
        left = left - (by_real * row_left + by_imag * (pltpu.roll(row_left, half, 1) * sign))
        inverse = inverse - (
            by_real * row_inverse + by_imag * (pltpu.roll(row_inverse, half, 1) * sign)
        )
        pivots = jnp.where(rows_only == k, pivot, pivots)
        return left, inverse, pivots

    eye = (row_id == lane_id).astype(jnp.float32)
    start = (left, eye, jnp.zeros((count, 1), jnp.float32))
    _, inverse, pivots = lax.fori_loop(0, count, body, start)
    return inverse * lax.rsqrt(pivots)


def turned(rows):
    width = rows.shape[1] // 2
    return jnp.concatenate([-rows[:, width:], rows[:, :width]], axis=1)


def dot(left, right):
    return jnp.dot(left, right, precision=exact_mode, preferred_element_type=jnp.float32)


def power_kernel(cov_ref, start_ref, out_ref):
    square = cov_ref[0]
    mirrored = square.T
    row_id = lax.broadcasted_iota(jnp.int32, square.shape, 0)
    col_id = lax.broadcasted_iota(jnp.int32, square.shape, 1)
    cov_real = jnp.where(row_id <= col_id, square, mirrored)
    cov_imag = jnp.where(row_id > col_id, square, jnp.where(row_id == col_id, 0.0, -mirrored))
    half = start_ref.shape[1] // 2
    width = square.shape[0]
    subspace = start_ref[0, :half, :]
    pad = jnp.zeros((64 - half, 2 * width), jnp.float32)
    contract = (((1,), (1,)), ((), ()))
    for power_step in range(POWER):
        sub_real = subspace[:, :width]
        sub_imag = subspace[:, width:]
        summed = jnp.concatenate(
            [
                dot(sub_real, cov_real) + dot(sub_imag, cov_imag),
                dot(sub_imag, cov_real) - dot(sub_real, cov_imag),
            ],
            axis=1,
        )
        stacked = jnp.concatenate([summed, pad, turned(summed), pad], axis=0)
        gram_matrix = lax.dot_general(
            summed, stacked, contract, precision=exact_mode, preferred_element_type=jnp.float32
        )
        subspace = dot(inverse_factor(gram_matrix), stacked)
    out_ref[0, :half, :] = subspace
    out_ref[0, half:, :] = turned(subspace)


def power_steps(cov_square, subspace):
    freq_count, basis, width = subspace.shape
    rows = cov_square.shape[1]
    return pl.pallas_call(
        power_kernel,
        out_shape=jax.ShapeDtypeStruct(subspace.shape, jnp.float32),
        grid=(freq_count,),
        in_specs=[
            pl.BlockSpec((1, rows, rows), lambda i: (i, 0, 0)),
            pl.BlockSpec((1, basis, width), lambda i: (i, 0, 0)),
        ],
        out_specs=pl.BlockSpec((1, basis, width), lambda i: (i, 0, 0)),
    )(cov_square, subspace)


def counts_along(places, lags, limit):
    total = jnp.zeros(places.shape, jnp.float32)
    for shift_by in range(lags):
        inside = (places - shift_by >= 0) & (places - shift_by < limit)
        total = total + inside.astype(jnp.float32)
    return total


def on_device(traces, kept_bins, start_basis):
    space_count = lax.axis_size("space")
    cosines, sines = tables(kept_bins)
    dft_scale = 1.0 / math.sqrt(NT)
    waves = jnp.stack([cosines * dft_scale, -sines * dft_scale], axis=1)
    spectra_tile = product("xyt,tcf->fcxy", traces, waves)
    slices = lax.all_to_all(spectra_tile, "freq", split_axis=0, concat_axis=3, tiled=True)
    freq_count = slices.shape[0]
    strip_width = slices.shape[2]
    trace_cols = slices.shape[3]
    rows = LX * LY
    x_offset = lax.axis_index("space") * strip_width
    places = x_offset + jnp.arange(strip_width, dtype=jnp.int32)
    columns = jnp.arange(trace_cols, dtype=jnp.int32)
    limit_x = strip_width * space_count - LX + 1
    limit_y = trace_cols - LY + 1
    valid_x = (places < limit_x).astype(jnp.float32)
    counts = (
        counts_along(places, LX, limit_x)[:, None] * counts_along(columns, LY, limit_y)[None, :]
    )
    lag_shift = shift_matrix(trace_cols, LY, limit_y)
    subspace = paired(start_basis)
    next_counts = (
        counts_along(places + strip_width, LX, limit_x)[:, None]
        * counts_along(columns, LY, limit_y)[None, :]
    )[: LX - 1]
    next_counts = jnp.maximum(next_counts, 1.0)
    rim_rows = shifted(slices[:, :, : LX - 1, :], "space", -1)
    for cadzow_step in range(CADZOW):
        extended = jnp.concatenate([slices, rim_rows], axis=2)
        lagged = product("fcpz,zby->fcbpy", extended, lag_shift)
        matrix = jnp.stack(
            [lagged[:, :, :, lag_x : lag_x + strip_width, :] for lag_x in range(LX)], axis=2
        )
        matrix = matrix * valid_x[:, None]
        matrix = matrix.reshape(freq_count, 2 * rows, strip_width * trace_cols)
        gram_h = product("fik,fjk->fij", matrix, matrix, lax.Precision.HIGH)
        cov_real = gram_h[:, :rows, :rows] + gram_h[:, rows:, rows:]
        cov_imag = gram_h[:, rows:, :rows] - gram_h[:, :rows, rows:]
        cov = all_sum(packed(cov_real, cov_imag), "space")
        subspace = power_steps(cov, subspace)
        half = subspace.shape[1] // 2
        signs = jnp.where(jnp.arange(2 * half) < half, 1.0, -1.0)[:, None]
        weights = subspace * signs
        coeffs = product("fjk,fkc->fjc", weights, matrix, lax.Precision.HIGH)
        projected = product("fjk,fjc->fkc", weights, coeffs, lax.Precision.HIGH)
        projected = projected.reshape(freq_count, 2, LX, LY, strip_width, trace_cols)
        along_y = product("fcabxy,vby->fcaxv", projected, lag_shift)
        full = sum(
            jnp.pad(along_y[:, :, lag_x], ((0, 0), (0, 0), (lag_x, LX - 1 - lag_x), (0, 0)))
            for lag_x in range(LX)
        )
        tail = full[:, :, strip_width:, :]
        spill = shifted(tail, "space", 1)
        if cadzow_step + 1 < CADZOW:
            next_head = shifted(full[:, :, : LX - 1, :], "space", -1)
            rim_rows = (next_head + tail) / next_counts
        spill = jnp.pad(spill, ((0, 0), (0, 0), (0, strip_width - (LX - 1)), (0, 0)))
        slices = (full[:, :, :strip_width, :] + spill) / counts
    out_scale = math.sqrt(2.0 / kept_bins.shape[0])
    received = lax.all_to_all(slices, "freq", split_axis=3, concat_axis=0, tiled=True)
    synth = product("fxy,tf->xyt", received[:, 0], cosines)
    synth = synth - product("fxy,tf->xyt", received[:, 1], sines)
    return out_scale * synth


def solution(mesh):
    placed = (P("space", "freq", None), P(), P("freq", None, None, None))
    return jax.shard_map(
        on_device, mesh=mesh, in_specs=placed, out_specs=P("space", "freq", None), check_vma=False
    )
```

profile of v0, /device:TPU:8, one launch (start us, length us, event | category | flops | bytes accessed | tf_op | source)
XLA Modules:
  0.0 185.3 jit_solution(12091315989710284242)
XLA Ops:
  0.0 1.1 cosine_multiply_fusion
  1.2 3.8 %convolution_bitcast_fusion.2 = f32[8,2,8,16]{3,0,2,1:T(8,128)S(1)} fusion(f32[8,16,2048]{2,1,0:T(8,128)S(1)} %copy-done, f32[2048,1,8]{0,2,1:T(8,128)S(1)} %get-tuple-element.28, f32[2048,1,8]{0,2,1:T(8,128)S(1)} %get-tuple-element.27), kind=kOutput, calls=%fused_computation.28 | convolution fusion | flops 50364416 | bytes 1187840 | tf_op jit(solution)/shard_map/xyt,tcf->fcxy/dot_general | solution.py:36
  5.0 0.7 reshape.996
  5.7 4.3 %all-to-all-start = ((f32[8,1,256]{2,1,0:T(1,128)}), f32[8,1,256]{2,1,0:T(1,128)S(1)}, u32[]{:S(2)}, u32[]{:S(2)}) async-start(f32[8,1,256]{2,1,0:T(1,128)} %reshape.996), calls=%async_computation | async-start | bytes 16384 | tf_op jit(solution)/shard_map/all_to_all | solution.py:184
  10.0 0.8 slice_bitcast_fusion.16
  10.8 0.8 fusion.156
  11.7 0.7 maximum_maximum_fusion.start_ref
  12.4 3.0 %all-to-all-done = f32[8,1,256]{2,1,0:T(1,128)S(1)} async-done(((f32[8,1,256]{2,1,0:T(1,128)}), f32[8,1,256]{2,1,0:T(1,128)S(1)}, u32[]{:S(2)}, u32[]{:S(2)}) %all-to-all-start) | async-done | bytes 8224 | tf_op jit(solution)/shard_map/all_to_all | solution.py:184
  15.3 0.5 broadcast.1219
  15.9 0.7 reduce.4
  16.7 5.8 %collective-permute-start = (f32[1,2,7,128]{3,2,1,0:T(8,128)S(1)}, f32[1,2,7,128]{3,2,1,0:T(8,128)S(1)}, u32[]{:S(2)}, u32[]{:S(2)}) collective-permute-start(f32[1,2,7,128]{3,2,1,0:T(8,128)S(1)} %bitcast.286), channel_id=1, source_target_pairs={{1,0},{2,1},{3,2},{4,3},{5,4},{6,5},{7,6},{8,7},{9,8},{10,9},{11,1... | collective-permute-start | bytes 21512 | tf_op jit(solution)/shard_map/ppermute | solution.py:24
  22.6 1.3 collective-permute-done
  23.9 0.9 fusion.28
  25.1 0.2 broadcast_multiply_fusion.1
  25.4 0.2 copy.28
  25.6 2.1 %fusion.22 = f32[1,512,512]{2,1,0:T(8,128)S(1)} fusion(f32[64,8,8,128]{3,2,1,0:T(8,128)S(1)} %bitcast.276), kind=kOutput, calls=%fused_computation.22 | convolution fusion | flops 1610612736 | bytes 3145728 | tf_op jit(solution)/shard_map/fik,fjk->fij/dot_general | solution.py:36
  27.8 1.0 all_to_all.60
  28.7 8.9 %all-to-all-start.1 = ((f32[16,1,4096]{2,1,0:T(1,128)}), f32[16,1,4096]{2,1,0:T(1,128)S(1)}, u32[]{:S(2)}, u32[]{:S(2)}) async-start(f32[16,1,4096]{2,1,0:T(1,128)} %all_to_all.60), calls=%async_computation.1 | async-start | bytes 524288 | tf_op jit(solution)/shard_map/all_to_all | solution.py:30
  37.7 1.6 copy.31
  39.3 5.1 %all-to-all-done.1 = f32[16,1,4096]{2,1,0:T(1,128)S(1)} async-done(((f32[16,1,4096]{2,1,0:T(1,128)}), f32[16,1,4096]{2,1,0:T(1,128)S(1)}, u32[]{:S(2)}, u32[]{:S(2)}) %all-to-all-start.1) | async-done | bytes 262176 | tf_op jit(solution)/shard_map/all_to_all | solution.py:30
  44.6 0.9 broadcast_in_dim.14
  45.5 5.3 %all-to-all-start.2 = ((f32[16,1,4096]{2,1,0:T(1,128)}), f32[16,1,4096]{2,1,0:T(1,128)S(1)}, u32[]{:S(2)}, u32[]{:S(2)}) async-start(f32[16,1,4096]{2,1,0:T(1,128)} %broadcast_in_dim.14), calls=%async_computation.2 | async-start | bytes 524288 | tf_op jit(solution)/shard_map/all_to_all | solution.py:32
  50.9 2.1 %fusion.5 = f32[1024,512]{0,1:T(8,128)S(1)} fusion(f32[64,8,8,128]{3,2,1,0:T(8,128)} %bitcast.273, f32[1024]{0:T(1024)S(1)} %broadcast_bitcast_fusion), kind=kLoop, calls=%fused_computation.8 | loop fusion | flops 524288 | bytes 4198400 | tf_op jit(solution)/shard_map/fjk,fkc->fjc/dot_general | solution.py:36
  52.9 1.9 %copy.59 = f32[1024,512]{1,0:T(8,128)} copy(f32[1024,512]{0,1:T(8,128)S(1)} %fusion.5) | data formatting | bytes 4194304 | tf_op jit(solution)/shard_map/fjk,fkc->fjc/dot_general | solution.py:36
  54.8 2.9 %all-to-all-done.2 = f32[16,1,4096]{2,1,0:T(1,128)S(1)} async-done(((f32[16,1,4096]{2,1,0:T(1,128)}), f32[16,1,4096]{2,1,0:T(1,128)S(1)}, u32[]{:S(2)}, u32[]{:S(2)}) %all-to-all-start.2) | async-done | bytes 262176 | tf_op jit(solution)/shard_map/all_to_all | solution.py:32
  57.7 0.6 reduce.2
  58.3 0.7 reshape.973.cov_ref
  59.0 23.7 %shard_map.37.start_ref = f32[1,80,512]{2,1,0:T(8,128)} custom-call(f32[1,256,256]{2,1,0:T(8,128)} %reshape.973.cov_ref, f32[1,80,512]{2,1,0:T(8,128)} %maximum_maximum_fusion.start_ref), custom_call_target="tpu_custom_call" | custom-call | tf_op jit(solution)/shard_map/pallas_call | solution.py:158
  82.8 1.0 multiply_bitcast_fusion.1
  83.8 2.7 %convolution_bitcast_fusion.1 = f32[8,128,80,1,1]{1,2,0,4,3:T(8,128)S(1)} fusion(f32[8,128,512]{2,1,0:T(8,128)} %bitcast.275, f32[1,80,512]{2,1,0:T(8,128)} %shard_map.37.start_ref, f32[80]{0:T(128)S(1)} %compare_select_fusion), kind=kOutput, calls=%fused_computation.27 | convolution fusion | flops 251699200 | bytes 2588992 | tf_op jit(solution)/shard_map/fjk,fkc->fjc/dot_general | solution.py:36
  86.6 1.0 fusion.158
  87.5 2.3 %fusion.34 = f32[1,2,8,8,128]{4,3,2,1,0:T(8,128)S(1)} fusion(f32[2,8,32,8,128]{4,2,3,1,0:T(8,128)S(1)} %fusion.158, pred[128]{0:T(512)(128)(4,1)S(1)} %iota_compare_fusion.1), kind=kOutput, calls=%fused_computation.29 | convolution fusion | flops 806879232 | bytes 2162816 | tf_op jit(solution)/shard_map/fcabxy,vby->fcaxv/dot_general | solution.py:36
  89.9 4.1 %collective-permute-start.2 = (f32[1,2,7,128]{3,2,1,0:T(8,128)S(1)}, f32[1,2,7,128]{3,2,1,0:T(8,128)S(1)}, u32[]{:S(2)}, u32[]{:S(2)}) collective-permute-start(f32[1,2,7,128]{3,2,1,0:T(8,128)S(1)} %slice.229), channel_id=1, source_target_pairs={{1,0},{2,1},{3,2},{4,3},{5,4},{6,5},{7,6},{8,7},{9,8},{10,9},{11,1... | collective-permute-start | bytes 21512 | tf_op jit(solution)/shard_map/ppermute | solution.py:24
  94.1 1.4 collective-permute-done.2
  95.5 2.3 %collective-permute-start.1 = (f32[1,2,7,128]{3,2,1,0:T(8,128)S(1)}, f32[1,2,7,128]{3,2,1,0:T(8,128)S(1)}, u32[]{:S(2)}, u32[]{:S(2)}) collective-permute-start(f32[1,2,7,128]{3,2,1,0:T(8,128)S(1)} %get-tuple-element.23), channel_id=1, source_target_pairs={{0,1},{1,2},{2,3},{3,4},{4,5},{5,6},{6,7},{7,8},{8,9},{9,10},{10,1... | collective-permute-start | bytes 21512 | tf_op jit(solution)/shard_map/ppermute | solution.py:24
  97.8 5.5 %collective-permute-done.1 = f32[1,2,7,128]{3,2,1,0:T(8,128)S(1)} collective-permute-done((f32[1,2,7,128]{3,2,1,0:T(8,128)S(1)}, f32[1,2,7,128]{3,2,1,0:T(8,128)S(1)}, u32[]{:S(2)}, u32[]{:S(2)}) %collective-permute-start.1) | collective-permute-done | bytes 7200 | tf_op jit(solution)/shard_map/ppermute | solution.py:24
  103.4 0.9 fusion.31
  104.6 0.2 broadcast_multiply_fusion
  104.8 0.2 copy.41
  105.1 2.1 %fusion.25 = f32[1,512,512]{2,1,0:T(8,128)S(1)} fusion(f32[64,8,8,128]{3,2,1,0:T(8,128)S(1)} %bitcast.277), kind=kOutput, calls=%fused_computation.23 | convolution fusion | flops 1610612736 | bytes 3145728 | tf_op jit(solution)/shard_map/fik,fjk->fij/dot_general | solution.py:36
  107.2 1.0 all_to_all.61
  108.2 4.5 %all-to-all-start.3 = ((f32[16,1,4096]{2,1,0:T(1,128)}), f32[16,1,4096]{2,1,0:T(1,128)S(1)}, u32[]{:S(2)}, u32[]{:S(2)}) async-start(f32[16,1,4096]{2,1,0:T(1,128)} %all_to_all.61), calls=%async_computation.3 | async-start | bytes 524288 | tf_op jit(solution)/shard_map/all_to_all | solution.py:30
  112.7 1.6 copy.44
  114.3 5.2 %all-to-all-done.3 = f32[16,1,4096]{2,1,0:T(1,128)S(1)} async-done(((f32[16,1,4096]{2,1,0:T(1,128)}), f32[16,1,4096]{2,1,0:T(1,128)S(1)}, u32[]{:S(2)}, u32[]{:S(2)}) %all-to-all-start.3) | async-done | bytes 262176 | tf_op jit(solution)/shard_map/all_to_all | solution.py:30
  119.7 0.9 broadcast_in_dim.17
  120.6 5.3 %all-to-all-start.4 = ((f32[16,1,4096]{2,1,0:T(1,128)}), f32[16,1,4096]{2,1,0:T(1,128)S(1)}, u32[]{:S(2)}, u32[]{:S(2)}) async-start(f32[16,1,4096]{2,1,0:T(1,128)} %broadcast_in_dim.17), calls=%async_computation.4 | async-start | bytes 524288 | tf_op jit(solution)/shard_map/all_to_all | solution.py:32
  126.0 2.1 %fusion.1 = f32[1024,512]{0,1:T(8,128)S(1)} fusion(f32[64,8,8,128]{3,2,1,0:T(8,128)} %bitcast.272, f32[1024]{0:T(1024)S(1)} %broadcast_bitcast_fusion), kind=kLoop, calls=%fused_computation.3 | loop fusion | flops 524288 | bytes 4198400 | tf_op jit(solution)/shard_map/fjk,fkc->fjc/dot_general | solution.py:36
  128.0 1.9 %copy.60 = f32[1024,512]{1,0:T(8,128)} copy(f32[1024,512]{0,1:T(8,128)S(1)} %fusion.1) | data formatting | bytes 4194304 | tf_op jit(solution)/shard_map/fjk,fkc->fjc/dot_general | solution.py:36
  129.9 2.9 %all-to-all-done.4 = f32[16,1,4096]{2,1,0:T(1,128)S(1)} async-done(((f32[16,1,4096]{2,1,0:T(1,128)}), f32[16,1,4096]{2,1,0:T(1,128)S(1)}, u32[]{:S(2)}, u32[]{:S(2)}) %all-to-all-start.4) | async-done | bytes 262176 | tf_op jit(solution)/shard_map/all_to_all | solution.py:32
  132.8 0.6 reduce.3
  133.4 0.7 reshape.976.cov_ref
  134.1 23.7 %shard_map.38 = f32[1,80,512]{2,1,0:T(8,128)} custom-call(f32[1,256,256]{2,1,0:T(8,128)} %reshape.976.cov_ref, f32[1,80,512]{2,1,0:T(8,128)} %shard_map.37.start_ref), custom_call_target="tpu_custom_call" | custom-call | tf_op jit(solution)/shard_map/pallas_call | solution.py:158
  157.9 1.0 multiply_bitcast_fusion
  158.9 2.7 %convolution_bitcast_fusion = f32[8,128,80,1,1]{1,2,0,4,3:T(8,128)S(1)} fusion(f32[8,128,512]{2,1,0:T(8,128)} %bitcast.274, f32[1,80,512]{2,1,0:T(8,128)} %shard_map.38, f32[80]{0:T(128)S(1)} %compare_select_fusion), kind=kOutput, calls=%fused_computation.26 | convolution fusion | flops 251699200 | bytes 2588992 | tf_op jit(solution)/shard_map/fjk,fkc->fjc/dot_general | solution.py:36
  161.7 1.0 fusion.159
  162.7 2.3 %fusion.39 = f32[2,8,8,128]{3,2,1,0:T(8,128)S(1)} fusion(f32[2,8,32,8,128]{4,2,3,1,0:T(8,128)S(1)} %fusion.159, pred[128]{0:T(512)(128)(4,1)S(1)} %iota_compare_fusion.1), kind=kOutput, calls=%fused_computation.30 | convolution fusion | flops 806879232 | bytes 2162816 | tf_op jit(solution)/shard_map/fcabxy,vby->fcaxv/dot_general | solution.py:36
  165.1 2.3 %collective-permute-start.3 = (f32[1,2,7,128]{3,2,1,0:T(8,128)S(1)}, f32[1,2,7,128]{3,2,1,0:T(8,128)S(1)}, u32[]{:S(2)}, u32[]{:S(2)}) collective-permute-start(f32[1,2,7,128]{3,2,1,0:T(8,128)S(1)} %slice.251), channel_id=1, source_target_pairs={{0,1},{1,2},{2,3},{3,4},{4,5},{5,6},{6,7},{7,8},{8,9},{9,10},{10,1... | collective-permute-start | bytes 21512 | tf_op jit(solution)/shard_map/ppermute | solution.py:24
  167.4 5.3 %collective-permute-done.3 = f32[1,2,7,128]{3,2,1,0:T(8,128)S(1)} collective-permute-done((f32[1,2,7,128]{3,2,1,0:T(8,128)S(1)}, f32[1,2,7,128]{3,2,1,0:T(8,128)S(1)}, u32[]{:S(2)}, u32[]{:S(2)}) %collective-permute-start.3) | collective-permute-done | bytes 7200 | tf_op jit(solution)/shard_map/ppermute | solution.py:24
  172.9 0.2 reshape.998
  173.1 7.7 %all_to_all.68 = f32[8,1,256]{2,1,0:T(1,128)S(1)} all-to-all(f32[8,1,256]{2,1,0:T(1,128)S(1)} %reshape.998), channel_id=1, replica_groups=mesh['freq'=8,'space'=16] {'freq'}, dimensions={0} | all-to-all | bytes 16384 | tf_op jit(solution)/shard_map/all_to_all | solution.py:238
  180.8 0.7 reduce.5
  181.4 0.2 reshape.999
  181.8 1.2 fusion.82
  183.0 2.2 %fusion = f32[8,16,2048]{2,1,0:T(8,128)} fusion(f32[8,16,2048]{2,1,0:T(8,128)S(1)} %fusion.82, f32[8,2,8,16]{3,0,2,1:T(8,128)S(1)} %bitcast.283, s32[8]{0:T(128)S(1)} %copy-done.1), kind=kOutput, calls=%fused_computation.1 | convolution fusion | flops 25919488 | bytes 2130432 | tf_op jit(solution)/shard_map/fxy,tf->xyt/dot_general | solution.py:36
  (50 shorter events, 2.1 us)
Async XLA Ops:
  0.0 1.2 copy-start
  5.7 9.6 %all-to-all-start = ((f32[8,1,256]{2,1,0:T(1,128)}), f32[8,1,256]{2,1,0:T(1,128)S(1)}, u32[]{:S(2)}, u32[]{:S(2)}) async-start(f32[8,1,256]{2,1,0:T(1,128)} %reshape.996), calls=%async_computation | async-start | bytes 16384 | tf_op jit(solution)/shard_map/all_to_all | solution.py:184
  16.7 7.2 %collective-permute-start = (f32[1,2,7,128]{3,2,1,0:T(8,128)S(1)}, f32[1,2,7,128]{3,2,1,0:T(8,128)S(1)}, u32[]{:S(2)}, u32[]{:S(2)}) collective-permute-start(f32[1,2,7,128]{3,2,1,0:T(8,128)S(1)} %bitcast.286), channel_id=1, source_target_pairs={{1,0},{2,1},{3,2},{4,3},{5,4},{6,5},{7,6},{8,7},{9,8},{10,9},{11,1... | collective-permute-start | bytes 21512 | tf_op jit(solution)/shard_map/ppermute | solution.py:24
  28.7 15.7 %all-to-all-start.1 = ((f32[16,1,4096]{2,1,0:T(1,128)}), f32[16,1,4096]{2,1,0:T(1,128)S(1)}, u32[]{:S(2)}, u32[]{:S(2)}) async-start(f32[16,1,4096]{2,1,0:T(1,128)} %all_to_all.60), calls=%async_computation.1 | async-start | bytes 524288 | tf_op jit(solution)/shard_map/all_to_all | solution.py:30
  45.5 12.1 %all-to-all-start.2 = ((f32[16,1,4096]{2,1,0:T(1,128)}), f32[16,1,4096]{2,1,0:T(1,128)S(1)}, u32[]{:S(2)}, u32[]{:S(2)}) async-start(f32[16,1,4096]{2,1,0:T(1,128)} %broadcast_in_dim.14), calls=%async_computation.2 | async-start | bytes 524288 | tf_op jit(solution)/shard_map/all_to_all | solution.py:32
  89.9 5.5 %collective-permute-start.2 = (f32[1,2,7,128]{3,2,1,0:T(8,128)S(1)}, f32[1,2,7,128]{3,2,1,0:T(8,128)S(1)}, u32[]{:S(2)}, u32[]{:S(2)}) collective-permute-start(f32[1,2,7,128]{3,2,1,0:T(8,128)S(1)} %slice.229), channel_id=1, source_target_pairs={{1,0},{2,1},{3,2},{4,3},{5,4},{6,5},{7,6},{8,7},{9,8},{10,9},{11,1... | collective-permute-start | bytes 21512 | tf_op jit(solution)/shard_map/ppermute | solution.py:24
  95.5 7.9 %collective-permute-start.1 = (f32[1,2,7,128]{3,2,1,0:T(8,128)S(1)}, f32[1,2,7,128]{3,2,1,0:T(8,128)S(1)}, u32[]{:S(2)}, u32[]{:S(2)}) collective-permute-start(f32[1,2,7,128]{3,2,1,0:T(8,128)S(1)} %get-tuple-element.23), channel_id=1, source_target_pairs={{0,1},{1,2},{2,3},{3,4},{4,5},{5,6},{6,7},{7,8},{8,9},{9,10},{10,1... | collective-permute-start | bytes 21512 | tf_op jit(solution)/shard_map/ppermute | solution.py:24
  108.2 11.3 %all-to-all-start.3 = ((f32[16,1,4096]{2,1,0:T(1,128)}), f32[16,1,4096]{2,1,0:T(1,128)S(1)}, u32[]{:S(2)}, u32[]{:S(2)}) async-start(f32[16,1,4096]{2,1,0:T(1,128)} %all_to_all.61), calls=%async_computation.3 | async-start | bytes 524288 | tf_op jit(solution)/shard_map/all_to_all | solution.py:30
  120.6 12.1 %all-to-all-start.4 = ((f32[16,1,4096]{2,1,0:T(1,128)}), f32[16,1,4096]{2,1,0:T(1,128)S(1)}, u32[]{:S(2)}, u32[]{:S(2)}) async-start(f32[16,1,4096]{2,1,0:T(1,128)} %broadcast_in_dim.17), calls=%async_computation.4 | async-start | bytes 524288 | tf_op jit(solution)/shard_map/all_to_all | solution.py:32
  162.6 19.1 %copy-start.1 = (s32[8]{0:T(128)S(1)}, s32[8]{0:T(128)}, u32[]{:S(2)}) copy-start(s32[8]{0:T(128)} %param.4) | copy-start | bytes 100
  165.1 7.7 %collective-permute-start.3 = (f32[1,2,7,128]{3,2,1,0:T(8,128)S(1)}, f32[1,2,7,128]{3,2,1,0:T(8,128)S(1)}, u32[]{:S(2)}, u32[]{:S(2)}) collective-permute-start(f32[1,2,7,128]{3,2,1,0:T(8,128)S(1)} %slice.251), channel_id=1, source_target_pairs={{0,1},{1,2},{2,3},{3,4},{4,5},{5,6},{6,7},{7,8},{8,9},{9,10},{10,1... | collective-permute-start | bytes 21512 | tf_op jit(solution)/shard_map/ppermute | solution.py:24
where the time goes:
time: 186 us; the launch traced here: 185 us
  Pallas kernels  47.5 us (26%)
  starting transfers between devices  43 us (23%)
  waiting for transfers between devices  32.6 us (18%)
  matrix products  25.2 us (14%)
  local copies, waits for them, and re-layouts  16.5 us (9%)
  other arithmetic  12.4 us (7%)
  blocking collectives  7.67 us (4%)
    pallas_call x2, Pallas kernels, power_steps(): pl.pallas_call(power_kernel, out_shape=jax.ShapeDtypeStruct(subspace.shap...  47.5 us
    dot_general x13, matrix products, product(): jnp.einsum(form, left, right, precision=precision, preferred_element_type...  25.2 us
    ppermute x4, starting transfers between devices, shifted(): return lax.ppermute(x, axis, pairs)  14.6 us
    ppermute x4, waiting for transfers between devices, shifted(): return lax.ppermute(x, axis, pairs)  13.6 us
    all_to_all x2, starting transfers between devices, all_sum(): mine = lax.all_to_all(chunks, axis, 0, 0, tiled=True).sum(axis=0)  13.4 us
    all_to_all x2, starting transfers between devices, all_sum(): return lax.all_to_all(copies, axis, 0, 0, tiled=True).reshape(x.shape)  10.7 us
    all_to_all x2, waiting for transfers between devices, all_sum(): mine = lax.all_to_all(chunks, axis, 0, 0, tiled=True).sum(axis=0)  10.4 us
    all_to_all x1, blocking collectives, on_device(): lax.all_to_all(slices, 'freq', split_axis=3, concat_axis=0, tiled=True)  7.67 us
  transfers between devices with their start and end apart: 9, of which 9 were waited for; matrix products, arithmetic and copies ran while one was open for 7% of the time, Pallas kernels for 0%

commit v1 on v0

--- a/solution.py
+++ b/solution.py
@@ -211,7 +211,7 @@
         )
         matrix = matrix * valid_x[:, None]
         matrix = matrix.reshape(freq_count, 2 * rows, strip_width * trace_cols)
-        gram_h = product("fik,fjk->fij", matrix, matrix, lax.Precision.HIGH)
+        gram_h = product("fik,fjk->fij", matrix, matrix)
         cov_real = gram_h[:, :rows, :rows] + gram_h[:, rows:, rows:]
         cov_imag = gram_h[:, rows:, :rows] - gram_h[:, :rows, rows:]
         cov = all_sum(packed(cov_real, cov_imag), "space")

time: 186 us -> 190 us (1.022)
  matrix products: 25.2 us -> 28.8 us
    dot_general x13, matrix products: 25.2 us -> 28.8 us  [product(): jnp.einsum(form, left, right, precision=precision, preferred_element_type...]
where the time goes in v1:
time: 190 us; the launch traced here: 189 us
  Pallas kernels  47.5 us (25%)
  starting transfers between devices  43 us (23%)
  waiting for transfers between devices  32.6 us (17%)
  matrix products  28.8 us (15%)
  local copies, waits for them, and re-layouts  16.5 us (9%)
  other arithmetic  12.4 us (7%)
  blocking collectives  7.67 us (4%)
    pallas_call x2, Pallas kernels, power_steps(): pl.pallas_call(power_kernel, out_shape=jax.ShapeDtypeStruct(subspace.shap...  47.5 us
    dot_general x13, matrix products, product(): jnp.einsum(form, left, right, precision=precision, preferred_element_type...  28.8 us
    ppermute x4, starting transfers between devices, shifted(): return lax.ppermute(x, axis, pairs)  14.6 us
    ppermute x4, waiting for transfers between devices, shifted(): return lax.ppermute(x, axis, pairs)  13.6 us
    all_to_all x2, starting transfers between devices, all_sum(): mine = lax.all_to_all(chunks, axis, 0, 0, tiled=True).sum(axis=0)  13.4 us
    all_to_all x2, starting transfers between devices, all_sum(): return lax.all_to_all(copies, axis, 0, 0, tiled=True).reshape(x.shape)  10.7 us
    all_to_all x2, waiting for transfers between devices, all_sum(): mine = lax.all_to_all(chunks, axis, 0, 0, tiled=True).sum(axis=0)  10.4 us
    all_to_all x1, blocking collectives, on_device(): lax.all_to_all(slices, 'freq', split_axis=3, concat_axis=0, tiled=True)  7.67 us
  transfers between devices with their start and end apart: 9, of which 9 were waited for; matrix products, arithmetic and copies ran while one was open for 7% of the time, Pallas kernels for 0%

profile of v1, /device:TPU:8, one launch (start us, length us, event | category | flops | bytes accessed | tf_op | source)
XLA Modules:
  0.0 188.9 jit_solution(9552153440338503674)
XLA Ops:
  0.0 1.1 cosine_multiply_fusion
  1.2 3.8 %convolution_bitcast_fusion.2 = f32[8,2,8,16]{3,0,2,1:T(8,128)S(1)} fusion(f32[8,16,2048]{2,1,0:T(8,128)S(1)} %copy-done, f32[2048,1,8]{0,2,1:T(8,128)S(1)} %get-tuple-element.28, f32[2048,1,8]{0,2,1:T(8,128)S(1)} %get-tuple-element.27), kind=kOutput, calls=%fused_computation.28 | convolution fusion | flops 50364416 | bytes 1187840 | tf_op jit(solution)/shard_map/xyt,tcf->fcxy/dot_general | solution.py:36
  5.0 0.7 reshape.996
  5.7 4.3 %all-to-all-start = ((f32[8,1,256]{2,1,0:T(1,128)}), f32[8,1,256]{2,1,0:T(1,128)S(1)}, u32[]{:S(2)}, u32[]{:S(2)}) async-start(f32[8,1,256]{2,1,0:T(1,128)} %reshape.996), calls=%async_computation | async-start | bytes 16384 | tf_op jit(solution)/shard_map/all_to_all | solution.py:184
  10.0 0.8 slice_bitcast_fusion.16
  10.8 0.8 fusion.156
  11.7 0.7 maximum_maximum_fusion.start_ref
  12.4 3.0 %all-to-all-done = f32[8,1,256]{2,1,0:T(1,128)S(1)} async-done(((f32[8,1,256]{2,1,0:T(1,128)}), f32[8,1,256]{2,1,0:T(1,128)S(1)}, u32[]{:S(2)}, u32[]{:S(2)}) %all-to-all-start) | async-done | bytes 8224 | tf_op jit(solution)/shard_map/all_to_all | solution.py:184
  15.3 0.5 broadcast.1219
  15.9 0.7 reduce.4
  16.7 5.8 %collective-permute-start = (f32[1,2,7,128]{3,2,1,0:T(8,128)S(1)}, f32[1,2,7,128]{3,2,1,0:T(8,128)S(1)}, u32[]{:S(2)}, u32[]{:S(2)}) collective-permute-start(f32[1,2,7,128]{3,2,1,0:T(8,128)S(1)} %bitcast.286), channel_id=1, source_target_pairs={{1,0},{2,1},{3,2},{4,3},{5,4},{6,5},{7,6},{8,7},{9,8},{10,9},{11,1... | collective-permute-start | bytes 21512 | tf_op jit(solution)/shard_map/ppermute | solution.py:24
  22.6 1.3 collective-permute-done
  23.9 0.9 fusion.28
  25.1 0.2 broadcast_multiply_fusion.1
  25.4 0.2 copy.28
  25.6 3.9 %fusion.22 = f32[1,512,512]{2,1,0:T(8,128)S(1)} fusion(f32[64,8,8,128]{3,2,1,0:T(8,128)S(1)} %bitcast.276), kind=kOutput, calls=%fused_computation.22 | convolution fusion | flops 3221225472 | bytes 3145728 | tf_op jit(solution)/shard_map/fik,fjk->fij/dot_general | solution.py:36
  29.6 1.0 all_to_all.60
  30.5 8.9 %all-to-all-start.1 = ((f32[16,1,4096]{2,1,0:T(1,128)}), f32[16,1,4096]{2,1,0:T(1,128)S(1)}, u32[]{:S(2)}, u32[]{:S(2)}) async-start(f32[16,1,4096]{2,1,0:T(1,128)} %all_to_all.60), calls=%async_computation.1 | async-start | bytes 524288 | tf_op jit(solution)/shard_map/all_to_all | solution.py:30
  39.5 1.6 copy.31
  41.1 5.1 %all-to-all-done.1 = f32[16,1,4096]{2,1,0:T(1,128)S(1)} async-done(((f32[16,1,4096]{2,1,0:T(1,128)}), f32[16,1,4096]{2,1,0:T(1,128)S(1)}, u32[]{:S(2)}, u32[]{:S(2)}) %all-to-all-start.1) | async-done | bytes 262176 | tf_op jit(solution)/shard_map/all_to_all | solution.py:30
  46.4 0.9 broadcast_in_dim.14
  47.3 5.3 %all-to-all-start.2 = ((f32[16,1,4096]{2,1,0:T(1,128)}), f32[16,1,4096]{2,1,0:T(1,128)S(1)}, u32[]{:S(2)}, u32[]{:S(2)}) async-start(f32[16,1,4096]{2,1,0:T(1,128)} %broadcast_in_dim.14), calls=%async_computation.2 | async-start | bytes 524288 | tf_op jit(solution)/shard_map/all_to_all | solution.py:32
  52.7 2.1 %fusion.5 = f32[1024,512]{0,1:T(8,128)S(1)} fusion(f32[64,8,8,128]{3,2,1,0:T(8,128)} %bitcast.273, f32[1024]{0:T(1024)S(1)} %broadcast_bitcast_fusion), kind=kLoop, calls=%fused_computation.8 | loop fusion | flops 524288 | bytes 4198400 | tf_op jit(solution)/shard_map/fjk,fkc->fjc/dot_general | solution.py:36
  54.7 1.9 copy.59
  56.6 2.9 %all-to-all-done.2 = f32[16,1,4096]{2,1,0:T(1,128)S(1)} async-done(((f32[16,1,4096]{2,1,0:T(1,128)}), f32[16,1,4096]{2,1,0:T(1,128)S(1)}, u32[]{:S(2)}, u32[]{:S(2)}) %all-to-all-start.2) | async-done | bytes 262176 | tf_op jit(solution)/shard_map/all_to_all | solution.py:32
  59.5 0.6 reduce.2
  60.1 0.7 reshape.973.cov_ref
  60.8 23.7 %shard_map.37.start_ref = f32[1,80,512]{2,1,0:T(8,128)} custom-call(f32[1,256,256]{2,1,0:T(8,128)} %reshape.973.cov_ref, f32[1,80,512]{2,1,0:T(8,128)} %maximum_maximum_fusion.start_ref), custom_call_target="tpu_custom_call" | custom-call | tf_op jit(solution)/shard_map/pallas_call | solution.py:158
  84.6 1.0 multiply_bitcast_fusion.1
  85.6 2.7 %convolution_bitcast_fusion.1 = f32[8,128,80,1,1]{1,2,0,4,3:T(8,128)S(1)} fusion(f32[8,128,512]{2,1,0:T(8,128)} %bitcast.275, f32[1,80,512]{2,1,0:T(8,128)} %shard_map.37.start_ref, f32[80]{0:T(128)S(1)} %compare_select_fusion), kind=kOutput, calls=%fused_computation.27 | convolution fusion | flops 251699200 | bytes 2588992 | tf_op jit(solution)/shard_map/fjk,fkc->fjc/dot_general | solution.py:36
  88.4 1.0 fusion.158
  89.3 2.3 %fusion.34 = f32[1,2,8,8,128]{4,3,2,1,0:T(8,128)S(1)} fusion(f32[2,8,32,8,128]{4,2,3,1,0:T(8,128)S(1)} %fusion.158, pred[128]{0:T(512)(128)(4,1)S(1)} %iota_compare_fusion.1), kind=kOutput, calls=%fused_computation.29 | convolution fusion | flops 806879232 | bytes 2162816 | tf_op jit(solution)/shard_map/fcabxy,vby->fcaxv/dot_general | solution.py:36
  91.7 4.2 %collective-permute-start.2 = (f32[1,2,7,128]{3,2,1,0:T(8,128)S(1)}, f32[1,2,7,128]{3,2,1,0:T(8,128)S(1)}, u32[]{:S(2)}, u32[]{:S(2)}) collective-permute-start(f32[1,2,7,128]{3,2,1,0:T(8,128)S(1)} %slice.229), channel_id=1, source_target_pairs={{1,0},{2,1},{3,2},{4,3},{5,4},{6,5},{7,6},{8,7},{9,8},{10,9},{11,1... | collective-permute-start | bytes 21512 | tf_op jit(solution)/shard_map/ppermute | solution.py:24
  95.9 1.4 collective-permute-done.2
  97.3 2.3 %collective-permute-start.1 = (f32[1,2,7,128]{3,2,1,0:T(8,128)S(1)}, f32[1,2,7,128]{3,2,1,0:T(8,128)S(1)}, u32[]{:S(2)}, u32[]{:S(2)}) collective-permute-start(f32[1,2,7,128]{3,2,1,0:T(8,128)S(1)} %get-tuple-element.23), channel_id=1, source_target_pairs={{0,1},{1,2},{2,3},{3,4},{4,5},{5,6},{6,7},{7,8},{8,9},{9,10},{10,1... | collective-permute-start | bytes 21512 | tf_op jit(solution)/shard_map/ppermute | solution.py:24
  99.6 5.6 %collective-permute-done.1 = f32[1,2,7,128]{3,2,1,0:T(8,128)S(1)} collective-permute-done((f32[1,2,7,128]{3,2,1,0:T(8,128)S(1)}, f32[1,2,7,128]{3,2,1,0:T(8,128)S(1)}, u32[]{:S(2)}, u32[]{:S(2)}) %collective-permute-start.1) | collective-permute-done | bytes 7200 | tf_op jit(solution)/shard_map/ppermute | solution.py:24
  105.2 0.9 fusion.31
  106.4 0.2 broadcast_multiply_fusion
  106.6 0.2 copy.41
  106.9 3.9 %fusion.25 = f32[1,512,512]{2,1,0:T(8,128)S(1)} fusion(f32[64,8,8,128]{3,2,1,0:T(8,128)S(1)} %bitcast.277), kind=kOutput, calls=%fused_computation.23 | convolution fusion | flops 3221225472 | bytes 3145728 | tf_op jit(solution)/shard_map/fik,fjk->fij/dot_general | solution.py:36
  110.8 1.0 all_to_all.61
  111.8 4.5 %all-to-all-start.3 = ((f32[16,1,4096]{2,1,0:T(1,128)}), f32[16,1,4096]{2,1,0:T(1,128)S(1)}, u32[]{:S(2)}, u32[]{:S(2)}) async-start(f32[16,1,4096]{2,1,0:T(1,128)} %all_to_all.61), calls=%async_computation.3 | async-start | bytes 524288 | tf_op jit(solution)/shard_map/all_to_all | solution.py:30
  116.3 1.6 copy.44
  117.9 5.2 %all-to-all-done.3 = f32[16,1,4096]{2,1,0:T(1,128)S(1)} async-done(((f32[16,1,4096]{2,1,0:T(1,128)}), f32[16,1,4096]{2,1,0:T(1,128)S(1)}, u32[]{:S(2)}, u32[]{:S(2)}) %all-to-all-start.3) | async-done | bytes 262176 | tf_op jit(solution)/shard_map/all_to_all | solution.py:30
  123.3 0.9 broadcast_in_dim.17
  124.2 5.3 %all-to-all-start.4 = ((f32[16,1,4096]{2,1,0:T(1,128)}), f32[16,1,4096]{2,1,0:T(1,128)S(1)}, u32[]{:S(2)}, u32[]{:S(2)}) async-start(f32[16,1,4096]{2,1,0:T(1,128)} %broadcast_in_dim.17), calls=%async_computation.4 | async-start | bytes 524288 | tf_op jit(solution)/shard_map/all_to_all | solution.py:32
  129.6 2.1 %fusion.1 = f32[1024,512]{0,1:T(8,128)S(1)} fusion(f32[64,8,8,128]{3,2,1,0:T(8,128)} %bitcast.272, f32[1024]{0:T(1024)S(1)} %broadcast_bitcast_fusion), kind=kLoop, calls=%fused_computation.3 | loop fusion | flops 524288 | bytes 4198400 | tf_op jit(solution)/shard_map/fjk,fkc->fjc/dot_general | solution.py:36
  131.6 1.9 copy.60
  133.5 2.9 %all-to-all-done.4 = f32[16,1,4096]{2,1,0:T(1,128)S(1)} async-done(((f32[16,1,4096]{2,1,0:T(1,128)}), f32[16,1,4096]{2,1,0:T(1,128)S(1)}, u32[]{:S(2)}, u32[]{:S(2)}) %all-to-all-start.4) | async-done | bytes 262176 | tf_op jit(solution)/shard_map/all_to_all | solution.py:32
  136.4 0.6 reduce.3
  137.0 0.7 reshape.976.cov_ref
  137.7 23.7 %shard_map.38 = f32[1,80,512]{2,1,0:T(8,128)} custom-call(f32[1,256,256]{2,1,0:T(8,128)} %reshape.976.cov_ref, f32[1,80,512]{2,1,0:T(8,128)} %shard_map.37.start_ref), custom_call_target="tpu_custom_call" | custom-call | tf_op jit(solution)/shard_map/pallas_call | solution.py:158
  161.5 1.0 multiply_bitcast_fusion
  162.5 2.7 %convolution_bitcast_fusion = f32[8,128,80,1,1]{1,2,0,4,3:T(8,128)S(1)} fusion(f32[8,128,512]{2,1,0:T(8,128)} %bitcast.274, f32[1,80,512]{2,1,0:T(8,128)} %shard_map.38, f32[80]{0:T(128)S(1)} %compare_select_fusion), kind=kOutput, calls=%fused_computation.26 | convolution fusion | flops 251699200 | bytes 2588992 | tf_op jit(solution)/shard_map/fjk,fkc->fjc/dot_general | solution.py:36
  165.3 1.0 fusion.159
  166.3 2.3 %fusion.39 = f32[2,8,8,128]{3,2,1,0:T(8,128)S(1)} fusion(f32[2,8,32,8,128]{4,2,3,1,0:T(8,128)S(1)} %fusion.159, pred[128]{0:T(512)(128)(4,1)S(1)} %iota_compare_fusion.1), kind=kOutput, calls=%fused_computation.30 | convolution fusion | flops 806879232 | bytes 2162816 | tf_op jit(solution)/shard_map/fcabxy,vby->fcaxv/dot_general | solution.py:36
  168.7 2.3 %collective-permute-start.3 = (f32[1,2,7,128]{3,2,1,0:T(8,128)S(1)}, f32[1,2,7,128]{3,2,1,0:T(8,128)S(1)}, u32[]{:S(2)}, u32[]{:S(2)}) collective-permute-start(f32[1,2,7,128]{3,2,1,0:T(8,128)S(1)} %slice.251), channel_id=1, source_target_pairs={{0,1},{1,2},{2,3},{3,4},{4,5},{5,6},{6,7},{7,8},{8,9},{9,10},{10,1... | collective-permute-start | bytes 21512 | tf_op jit(solution)/shard_map/ppermute | solution.py:24
  171.0 5.3 %collective-permute-done.3 = f32[1,2,7,128]{3,2,1,0:T(8,128)S(1)} collective-permute-done((f32[1,2,7,128]{3,2,1,0:T(8,128)S(1)}, f32[1,2,7,128]{3,2,1,0:T(8,128)S(1)}, u32[]{:S(2)}, u32[]{:S(2)}) %collective-permute-start.3) | collective-permute-done | bytes 7200 | tf_op jit(solution)/shard_map/ppermute | solution.py:24
  176.5 0.2 reshape.998
  176.7 7.7 %all_to_all.68 = f32[8,1,256]{2,1,0:T(1,128)S(1)} all-to-all(f32[8,1,256]{2,1,0:T(1,128)S(1)} %reshape.998), channel_id=1, replica_groups=mesh['freq'=8,'space'=16] {'freq'}, dimensions={0} | all-to-all | bytes 16384 | tf_op jit(solution)/shard_map/all_to_all | solution.py:238
  184.4 0.7 reduce.5
  185.0 0.2 reshape.999
  185.4 1.2 fusion.82
  186.6 2.2 %fusion = f32[8,16,2048]{2,1,0:T(8,128)} fusion(f32[8,16,2048]{2,1,0:T(8,128)S(1)} %fusion.82, f32[8,2,8,16]{3,0,2,1:T(8,128)S(1)} %bitcast.283, s32[8]{0:T(128)S(1)} %copy-done.1), kind=kOutput, calls=%fused_computation.1 | convolution fusion | flops 25919488 | bytes 2130432 | tf_op jit(solution)/shard_map/fxy,tf->xyt/dot_general | solution.py:36
  (50 shorter events, 2.1 us)
Async XLA Ops:
  0.0 1.2 copy-start
  5.7 9.6 %all-to-all-start = ((f32[8,1,256]{2,1,0:T(1,128)}), f32[8,1,256]{2,1,0:T(1,128)S(1)}, u32[]{:S(2)}, u32[]{:S(2)}) async-start(f32[8,1,256]{2,1,0:T(1,128)} %reshape.996), calls=%async_computation | async-start | bytes 16384 | tf_op jit(solution)/shard_map/all_to_all | solution.py:184
  16.7 7.2 %collective-permute-start = (f32[1,2,7,128]{3,2,1,0:T(8,128)S(1)}, f32[1,2,7,128]{3,2,1,0:T(8,128)S(1)}, u32[]{:S(2)}, u32[]{:S(2)}) collective-permute-start(f32[1,2,7,128]{3,2,1,0:T(8,128)S(1)} %bitcast.286), channel_id=1, source_target_pairs={{1,0},{2,1},{3,2},{4,3},{5,4},{6,5},{7,6},{8,7},{9,8},{10,9},{11,1... | collective-permute-start | bytes 21512 | tf_op jit(solution)/shard_map/ppermute | solution.py:24
  30.5 15.7 %all-to-all-start.1 = ((f32[16,1,4096]{2,1,0:T(1,128)}), f32[16,1,4096]{2,1,0:T(1,128)S(1)}, u32[]{:S(2)}, u32[]{:S(2)}) async-start(f32[16,1,4096]{2,1,0:T(1,128)} %all_to_all.60), calls=%async_computation.1 | async-start | bytes 524288 | tf_op jit(solution)/shard_map/all_to_all | solution.py:30
  47.3 12.1 %all-to-all-start.2 = ((f32[16,1,4096]{2,1,0:T(1,128)}), f32[16,1,4096]{2,1,0:T(1,128)S(1)}, u32[]{:S(2)}, u32[]{:S(2)}) async-start(f32[16,1,4096]{2,1,0:T(1,128)} %broadcast_in_dim.14), calls=%async_computation.2 | async-start | bytes 524288 | tf_op jit(solution)/shard_map/all_to_all | solution.py:32
  91.7 5.5 %collective-permute-start.2 = (f32[1,2,7,128]{3,2,1,0:T(8,128)S(1)}, f32[1,2,7,128]{3,2,1,0:T(8,128)S(1)}, u32[]{:S(2)}, u32[]{:S(2)}) collective-permute-start(f32[1,2,7,128]{3,2,1,0:T(8,128)S(1)} %slice.229), channel_id=1, source_target_pairs={{1,0},{2,1},{3,2},{4,3},{5,4},{6,5},{7,6},{8,7},{9,8},{10,9},{11,1... | collective-permute-start | bytes 21512 | tf_op jit(solution)/shard_map/ppermute | solution.py:24
  97.3 7.9 %collective-permute-start.1 = (f32[1,2,7,128]{3,2,1,0:T(8,128)S(1)}, f32[1,2,7,128]{3,2,1,0:T(8,128)S(1)}, u32[]{:S(2)}, u32[]{:S(2)}) collective-permute-start(f32[1,2,7,128]{3,2,1,0:T(8,128)S(1)} %get-tuple-element.23), channel_id=1, source_target_pairs={{0,1},{1,2},{2,3},{3,4},{4,5},{5,6},{6,7},{7,8},{8,9},{9,10},{10,1... | collective-permute-start | bytes 21512 | tf_op jit(solution)/shard_map/ppermute | solution.py:24
  111.8 11.3 %all-to-all-start.3 = ((f32[16,1,4096]{2,1,0:T(1,128)}), f32[16,1,4096]{2,1,0:T(1,128)S(1)}, u32[]{:S(2)}, u32[]{:S(2)}) async-start(f32[16,1,4096]{2,1,0:T(1,128)} %all_to_all.61), calls=%async_computation.3 | async-start | bytes 524288 | tf_op jit(solution)/shard_map/all_to_all | solution.py:30
  124.2 12.1 %all-to-all-start.4 = ((f32[16,1,4096]{2,1,0:T(1,128)}), f32[16,1,4096]{2,1,0:T(1,128)S(1)}, u32[]{:S(2)}, u32[]{:S(2)}) async-start(f32[16,1,4096]{2,1,0:T(1,128)} %broadcast_in_dim.17), calls=%async_computation.4 | async-start | bytes 524288 | tf_op jit(solution)/shard_map/all_to_all | solution.py:32
  166.2 19.1 %copy-start.1 = (s32[8]{0:T(128)S(1)}, s32[8]{0:T(128)}, u32[]{:S(2)}) copy-start(s32[8]{0:T(128)} %param.4) | copy-start | bytes 100
  168.7 7.7 %collective-permute-start.3 = (f32[1,2,7,128]{3,2,1,0:T(8,128)S(1)}, f32[1,2,7,128]{3,2,1,0:T(8,128)S(1)}, u32[]{:S(2)}, u32[]{:S(2)}) collective-permute-start(f32[1,2,7,128]{3,2,1,0:T(8,128)S(1)} %slice.251), channel_id=1, source_target_pairs={{0,1},{1,2},{2,3},{3,4},{4,5},{5,6},{6,7},{7,8},{8,9},{9,10},{10,1... | collective-permute-start | bytes 21512 | tf_op jit(solution)/shard_map/ppermute | solution.py:24

commit v2 on v0

--- a/solution.py
+++ b/solution.py
@@ -108,7 +108,7 @@
 
     eye = (row_id == lane_id).astype(jnp.float32)
     start = (left, eye, jnp.zeros((count, 1), jnp.float32))
-    _, inverse, pivots = lax.fori_loop(0, count, body, start)
+    _, inverse, pivots = lax.fori_loop(0, count, body, start, unroll=4)
     return inverse * lax.rsqrt(pivots)
 
 

time: 186 us -> 185 us (level)
  no operation moved by 1% of the time
where the time goes in v2:
time: 185 us; the launch traced here: 184 us
  Pallas kernels  46.5 us (25%)
  starting transfers between devices  43 us (23%)
  waiting for transfers between devices  32.6 us (18%)
  matrix products  25.2 us (14%)
  local copies, waits for them, and re-layouts  16.5 us (9%)
  other arithmetic  12.4 us (7%)
  blocking collectives  7.67 us (4%)
    pallas_call x2, Pallas kernels, power_steps(): pl.pallas_call(power_kernel, out_shape=jax.ShapeDtypeStruct(subspace.shap...  46.5 us
    dot_general x13, matrix products, product(): jnp.einsum(form, left, right, precision=precision, preferred_element_type...  25.2 us
    ppermute x4, starting transfers between devices, shifted(): return lax.ppermute(x, axis, pairs)  14.6 us
    ppermute x4, waiting for transfers between devices, shifted(): return lax.ppermute(x, axis, pairs)  13.6 us
    all_to_all x2, starting transfers between devices, all_sum(): mine = lax.all_to_all(chunks, axis, 0, 0, tiled=True).sum(axis=0)  13.4 us
    all_to_all x2, starting transfers between devices, all_sum(): return lax.all_to_all(copies, axis, 0, 0, tiled=True).reshape(x.shape)  10.7 us
    all_to_all x2, waiting for transfers between devices, all_sum(): mine = lax.all_to_all(chunks, axis, 0, 0, tiled=True).sum(axis=0)  10.4 us
    all_to_all x1, blocking collectives, on_device(): lax.all_to_all(slices, 'freq', split_axis=3, concat_axis=0, tiled=True)  7.67 us
  transfers between devices with their start and end apart: 9, of which 9 were waited for; matrix products, arithmetic and copies ran while one was open for 7% of the time, Pallas kernels for 0%

profile of v2, /device:TPU:8, one launch (start us, length us, event | category | flops | bytes accessed | tf_op | source)
XLA Modules:
  0.0 184.3 jit_solution(14756455952100988156)
XLA Ops:
  0.0 1.1 cosine_multiply_fusion
  1.2 3.8 %convolution_bitcast_fusion.2 = f32[8,2,8,16]{3,0,2,1:T(8,128)S(1)} fusion(f32[8,16,2048]{2,1,0:T(8,128)S(1)} %copy-done, f32[2048,1,8]{0,2,1:T(8,128)S(1)} %get-tuple-element.28, f32[2048,1,8]{0,2,1:T(8,128)S(1)} %get-tuple-element.27), kind=kOutput, calls=%fused_computation.28 | convolution fusion | flops 50364416 | bytes 1187840 | tf_op jit(solution)/shard_map/xyt,tcf->fcxy/dot_general | solution.py:36
  5.0 0.7 reshape.996
  5.7 4.3 %all-to-all-start = ((f32[8,1,256]{2,1,0:T(1,128)}), f32[8,1,256]{2,1,0:T(1,128)S(1)}, u32[]{:S(2)}, u32[]{:S(2)}) async-start(f32[8,1,256]{2,1,0:T(1,128)} %reshape.996), calls=%async_computation | async-start | bytes 16384 | tf_op jit(solution)/shard_map/all_to_all | solution.py:184
  10.0 0.8 slice_bitcast_fusion.16
  10.8 0.8 fusion.156
  11.7 0.7 maximum_maximum_fusion.start_ref
  12.4 3.0 %all-to-all-done = f32[8,1,256]{2,1,0:T(1,128)S(1)} async-done(((f32[8,1,256]{2,1,0:T(1,128)}), f32[8,1,256]{2,1,0:T(1,128)S(1)}, u32[]{:S(2)}, u32[]{:S(2)}) %all-to-all-start) | async-done | bytes 8224 | tf_op jit(solution)/shard_map/all_to_all | solution.py:184
  15.3 0.5 broadcast.1219
  15.9 0.7 reduce.4
  16.7 5.8 %collective-permute-start = (f32[1,2,7,128]{3,2,1,0:T(8,128)S(1)}, f32[1,2,7,128]{3,2,1,0:T(8,128)S(1)}, u32[]{:S(2)}, u32[]{:S(2)}) collective-permute-start(f32[1,2,7,128]{3,2,1,0:T(8,128)S(1)} %bitcast.286), channel_id=1, source_target_pairs={{1,0},{2,1},{3,2},{4,3},{5,4},{6,5},{7,6},{8,7},{9,8},{10,9},{11,1... | collective-permute-start | bytes 21512 | tf_op jit(solution)/shard_map/ppermute | solution.py:24
  22.6 1.3 collective-permute-done
  23.9 0.9 fusion.28
  25.1 0.2 broadcast_multiply_fusion.1
  25.4 0.2 copy.28
  25.6 2.1 %fusion.22 = f32[1,512,512]{2,1,0:T(8,128)S(1)} fusion(f32[64,8,8,128]{3,2,1,0:T(8,128)S(1)} %bitcast.276), kind=kOutput, calls=%fused_computation.22 | convolution fusion | flops 1610612736 | bytes 3145728 | tf_op jit(solution)/shard_map/fik,fjk->fij/dot_general | solution.py:36
  27.8 1.0 all_to_all.60
  28.7 8.9 %all-to-all-start.1 = ((f32[16,1,4096]{2,1,0:T(1,128)}), f32[16,1,4096]{2,1,0:T(1,128)S(1)}, u32[]{:S(2)}, u32[]{:S(2)}) async-start(f32[16,1,4096]{2,1,0:T(1,128)} %all_to_all.60), calls=%async_computation.1 | async-start | bytes 524288 | tf_op jit(solution)/shard_map/all_to_all | solution.py:30
  37.7 1.6 copy.31
  39.3 5.1 %all-to-all-done.1 = f32[16,1,4096]{2,1,0:T(1,128)S(1)} async-done(((f32[16,1,4096]{2,1,0:T(1,128)}), f32[16,1,4096]{2,1,0:T(1,128)S(1)}, u32[]{:S(2)}, u32[]{:S(2)}) %all-to-all-start.1) | async-done | bytes 262176 | tf_op jit(solution)/shard_map/all_to_all | solution.py:30
  44.6 0.9 broadcast_in_dim.14
  45.5 5.3 %all-to-all-start.2 = ((f32[16,1,4096]{2,1,0:T(1,128)}), f32[16,1,4096]{2,1,0:T(1,128)S(1)}, u32[]{:S(2)}, u32[]{:S(2)}) async-start(f32[16,1,4096]{2,1,0:T(1,128)} %broadcast_in_dim.14), calls=%async_computation.2 | async-start | bytes 524288 | tf_op jit(solution)/shard_map/all_to_all | solution.py:32
  50.9 2.1 %fusion.5 = f32[1024,512]{0,1:T(8,128)S(1)} fusion(f32[64,8,8,128]{3,2,1,0:T(8,128)} %bitcast.273, f32[1024]{0:T(1024)S(1)} %broadcast_bitcast_fusion), kind=kLoop, calls=%fused_computation.8 | loop fusion | flops 524288 | bytes 4198400 | tf_op jit(solution)/shard_map/fjk,fkc->fjc/dot_general | solution.py:36
  52.9 1.9 %copy.59 = f32[1024,512]{1,0:T(8,128)} copy(f32[1024,512]{0,1:T(8,128)S(1)} %fusion.5) | data formatting | bytes 4194304 | tf_op jit(solution)/shard_map/fjk,fkc->fjc/dot_general | solution.py:36
  54.8 2.9 %all-to-all-done.2 = f32[16,1,4096]{2,1,0:T(1,128)S(1)} async-done(((f32[16,1,4096]{2,1,0:T(1,128)}), f32[16,1,4096]{2,1,0:T(1,128)S(1)}, u32[]{:S(2)}, u32[]{:S(2)}) %all-to-all-start.2) | async-done | bytes 262176 | tf_op jit(solution)/shard_map/all_to_all | solution.py:32
  57.7 0.6 reduce.2
  58.3 0.7 reshape.973.cov_ref
  59.0 23.2 %shard_map.37.start_ref = f32[1,80,512]{2,1,0:T(8,128)} custom-call(f32[1,256,256]{2,1,0:T(8,128)} %reshape.973.cov_ref, f32[1,80,512]{2,1,0:T(8,128)} %maximum_maximum_fusion.start_ref), custom_call_target="tpu_custom_call" | custom-call | tf_op jit(solution)/shard_map/pallas_call | solution.py:158
  82.3 1.0 multiply_bitcast_fusion.1
  83.3 2.7 %convolution_bitcast_fusion.1 = f32[8,128,80,1,1]{1,2,0,4,3:T(8,128)S(1)} fusion(f32[8,128,512]{2,1,0:T(8,128)} %bitcast.275, f32[1,80,512]{2,1,0:T(8,128)} %shard_map.37.start_ref, f32[80]{0:T(128)S(1)} %compare_select_fusion), kind=kOutput, calls=%fused_computation.27 | convolution fusion | flops 251699200 | bytes 2588992 | tf_op jit(solution)/shard_map/fjk,fkc->fjc/dot_general | solution.py:36
  86.1 1.0 fusion.158
  87.1 2.3 %fusion.34 = f32[1,2,8,8,128]{4,3,2,1,0:T(8,128)S(1)} fusion(f32[2,8,32,8,128]{4,2,3,1,0:T(8,128)S(1)} %fusion.158, pred[128]{0:T(512)(128)(4,1)S(1)} %iota_compare_fusion.1), kind=kOutput, calls=%fused_computation.29 | convolution fusion | flops 806879232 | bytes 2162816 | tf_op jit(solution)/shard_map/fcabxy,vby->fcaxv/dot_general | solution.py:36
  89.5 4.2 %collective-permute-start.2 = (f32[1,2,7,128]{3,2,1,0:T(8,128)S(1)}, f32[1,2,7,128]{3,2,1,0:T(8,128)S(1)}, u32[]{:S(2)}, u32[]{:S(2)}) collective-permute-start(f32[1,2,7,128]{3,2,1,0:T(8,128)S(1)} %slice.229), channel_id=1, source_target_pairs={{1,0},{2,1},{3,2},{4,3},{5,4},{6,5},{7,6},{8,7},{9,8},{10,9},{11,1... | collective-permute-start | bytes 21512 | tf_op jit(solution)/shard_map/ppermute | solution.py:24
  93.6 1.4 collective-permute-done.2
  95.0 2.3 %collective-permute-start.1 = (f32[1,2,7,128]{3,2,1,0:T(8,128)S(1)}, f32[1,2,7,128]{3,2,1,0:T(8,128)S(1)}, u32[]{:S(2)}, u32[]{:S(2)}) collective-permute-start(f32[1,2,7,128]{3,2,1,0:T(8,128)S(1)} %get-tuple-element.23), channel_id=1, source_target_pairs={{0,1},{1,2},{2,3},{3,4},{4,5},{5,6},{6,7},{7,8},{8,9},{9,10},{10,1... | collective-permute-start | bytes 21512 | tf_op jit(solution)/shard_map/ppermute | solution.py:24
  97.3 5.6 %collective-permute-done.1 = f32[1,2,7,128]{3,2,1,0:T(8,128)S(1)} collective-permute-done((f32[1,2,7,128]{3,2,1,0:T(8,128)S(1)}, f32[1,2,7,128]{3,2,1,0:T(8,128)S(1)}, u32[]{:S(2)}, u32[]{:S(2)}) %collective-permute-start.1) | collective-permute-done | bytes 7200 | tf_op jit(solution)/shard_map/ppermute | solution.py:24
  102.9 0.9 fusion.31
  104.1 0.2 broadcast_multiply_fusion
  104.4 0.2 copy.41
  104.6 2.1 %fusion.25 = f32[1,512,512]{2,1,0:T(8,128)S(1)} fusion(f32[64,8,8,128]{3,2,1,0:T(8,128)S(1)} %bitcast.277), kind=kOutput, calls=%fused_computation.23 | convolution fusion | flops 1610612736 | bytes 3145728 | tf_op jit(solution)/shard_map/fik,fjk->fij/dot_general | solution.py:36
  106.8 1.0 all_to_all.61
  107.7 4.5 %all-to-all-start.3 = ((f32[16,1,4096]{2,1,0:T(1,128)}), f32[16,1,4096]{2,1,0:T(1,128)S(1)}, u32[]{:S(2)}, u32[]{:S(2)}) async-start(f32[16,1,4096]{2,1,0:T(1,128)} %all_to_all.61), calls=%async_computation.3 | async-start | bytes 524288 | tf_op jit(solution)/shard_map/all_to_all | solution.py:30
  112.2 1.6 copy.44
  113.8 5.2 %all-to-all-done.3 = f32[16,1,4096]{2,1,0:T(1,128)S(1)} async-done(((f32[16,1,4096]{2,1,0:T(1,128)}), f32[16,1,4096]{2,1,0:T(1,128)S(1)}, u32[]{:S(2)}, u32[]{:S(2)}) %all-to-all-start.3) | async-done | bytes 262176 | tf_op jit(solution)/shard_map/all_to_all | solution.py:30
  119.2 0.9 broadcast_in_dim.17
  120.1 5.3 %all-to-all-start.4 = ((f32[16,1,4096]{2,1,0:T(1,128)}), f32[16,1,4096]{2,1,0:T(1,128)S(1)}, u32[]{:S(2)}, u32[]{:S(2)}) async-start(f32[16,1,4096]{2,1,0:T(1,128)} %broadcast_in_dim.17), calls=%async_computation.4 | async-start | bytes 524288 | tf_op jit(solution)/shard_map/all_to_all | solution.py:32
  125.5 2.1 %fusion.1 = f32[1024,512]{0,1:T(8,128)S(1)} fusion(f32[64,8,8,128]{3,2,1,0:T(8,128)} %bitcast.272, f32[1024]{0:T(1024)S(1)} %broadcast_bitcast_fusion), kind=kLoop, calls=%fused_computation.3 | loop fusion | flops 524288 | bytes 4198400 | tf_op jit(solution)/shard_map/fjk,fkc->fjc/dot_general | solution.py:36
  127.6 1.9 %copy.60 = f32[1024,512]{1,0:T(8,128)} copy(f32[1024,512]{0,1:T(8,128)S(1)} %fusion.1) | data formatting | bytes 4194304 | tf_op jit(solution)/shard_map/fjk,fkc->fjc/dot_general | solution.py:36
  129.4 2.9 %all-to-all-done.4 = f32[16,1,4096]{2,1,0:T(1,128)S(1)} async-done(((f32[16,1,4096]{2,1,0:T(1,128)}), f32[16,1,4096]{2,1,0:T(1,128)S(1)}, u32[]{:S(2)}, u32[]{:S(2)}) %all-to-all-start.4) | async-done | bytes 262176 | tf_op jit(solution)/shard_map/all_to_all | solution.py:32
  132.3 0.6 reduce.3
  132.9 0.7 reshape.976.cov_ref
  133.7 23.2 %shard_map.38 = f32[1,80,512]{2,1,0:T(8,128)} custom-call(f32[1,256,256]{2,1,0:T(8,128)} %reshape.976.cov_ref, f32[1,80,512]{2,1,0:T(8,128)} %shard_map.37.start_ref), custom_call_target="tpu_custom_call" | custom-call | tf_op jit(solution)/shard_map/pallas_call | solution.py:158
  156.9 1.0 multiply_bitcast_fusion
  157.9 2.7 %convolution_bitcast_fusion = f32[8,128,80,1,1]{1,2,0,4,3:T(8,128)S(1)} fusion(f32[8,128,512]{2,1,0:T(8,128)} %bitcast.274, f32[1,80,512]{2,1,0:T(8,128)} %shard_map.38, f32[80]{0:T(128)S(1)} %compare_select_fusion), kind=kOutput, calls=%fused_computation.26 | convolution fusion | flops 251699200 | bytes 2588992 | tf_op jit(solution)/shard_map/fjk,fkc->fjc/dot_general | solution.py:36
  160.7 1.0 fusion.159
  161.7 2.3 %fusion.39 = f32[2,8,8,128]{3,2,1,0:T(8,128)S(1)} fusion(f32[2,8,32,8,128]{4,2,3,1,0:T(8,128)S(1)} %fusion.159, pred[128]{0:T(512)(128)(4,1)S(1)} %iota_compare_fusion.1), kind=kOutput, calls=%fused_computation.30 | convolution fusion | flops 806879232 | bytes 2162816 | tf_op jit(solution)/shard_map/fcabxy,vby->fcaxv/dot_general | solution.py:36
  164.1 2.3 %collective-permute-start.3 = (f32[1,2,7,128]{3,2,1,0:T(8,128)S(1)}, f32[1,2,7,128]{3,2,1,0:T(8,128)S(1)}, u32[]{:S(2)}, u32[]{:S(2)}) collective-permute-start(f32[1,2,7,128]{3,2,1,0:T(8,128)S(1)} %slice.251), channel_id=1, source_target_pairs={{0,1},{1,2},{2,3},{3,4},{4,5},{5,6},{6,7},{7,8},{8,9},{9,10},{10,1... | collective-permute-start | bytes 21512 | tf_op jit(solution)/shard_map/ppermute | solution.py:24
  166.4 5.3 %collective-permute-done.3 = f32[1,2,7,128]{3,2,1,0:T(8,128)S(1)} collective-permute-done((f32[1,2,7,128]{3,2,1,0:T(8,128)S(1)}, f32[1,2,7,128]{3,2,1,0:T(8,128)S(1)}, u32[]{:S(2)}, u32[]{:S(2)}) %collective-permute-start.3) | collective-permute-done | bytes 7200 | tf_op jit(solution)/shard_map/ppermute | solution.py:24
  171.9 0.2 reshape.998
  172.1 7.7 %all_to_all.68 = f32[8,1,256]{2,1,0:T(1,128)S(1)} all-to-all(f32[8,1,256]{2,1,0:T(1,128)S(1)} %reshape.998), channel_id=1, replica_groups=mesh['freq'=8,'space'=16] {'freq'}, dimensions={0} | all-to-all | bytes 16384 | tf_op jit(solution)/shard_map/all_to_all | solution.py:238
  179.8 0.7 reduce.5
  180.5 0.2 reshape.999
  180.8 1.2 fusion.82
  182.1 2.2 %fusion = f32[8,16,2048]{2,1,0:T(8,128)} fusion(f32[8,16,2048]{2,1,0:T(8,128)S(1)} %fusion.82, f32[8,2,8,16]{3,0,2,1:T(8,128)S(1)} %bitcast.283, s32[8]{0:T(128)S(1)} %copy-done.1), kind=kOutput, calls=%fused_computation.1 | convolution fusion | flops 25919488 | bytes 2130432 | tf_op jit(solution)/shard_map/fxy,tf->xyt/dot_general | solution.py:36
  (50 shorter events, 2.1 us)
Async XLA Ops:
  0.0 1.2 copy-start
  5.7 9.6 %all-to-all-start = ((f32[8,1,256]{2,1,0:T(1,128)}), f32[8,1,256]{2,1,0:T(1,128)S(1)}, u32[]{:S(2)}, u32[]{:S(2)}) async-start(f32[8,1,256]{2,1,0:T(1,128)} %reshape.996), calls=%async_computation | async-start | bytes 16384 | tf_op jit(solution)/shard_map/all_to_all | solution.py:184
  16.7 7.2 %collective-permute-start = (f32[1,2,7,128]{3,2,1,0:T(8,128)S(1)}, f32[1,2,7,128]{3,2,1,0:T(8,128)S(1)}, u32[]{:S(2)}, u32[]{:S(2)}) collective-permute-start(f32[1,2,7,128]{3,2,1,0:T(8,128)S(1)} %bitcast.286), channel_id=1, source_target_pairs={{1,0},{2,1},{3,2},{4,3},{5,4},{6,5},{7,6},{8,7},{9,8},{10,9},{11,1... | collective-permute-start | bytes 21512 | tf_op jit(solution)/shard_map/ppermute | solution.py:24
  28.7 15.7 %all-to-all-start.1 = ((f32[16,1,4096]{2,1,0:T(1,128)}), f32[16,1,4096]{2,1,0:T(1,128)S(1)}, u32[]{:S(2)}, u32[]{:S(2)}) async-start(f32[16,1,4096]{2,1,0:T(1,128)} %all_to_all.60), calls=%async_computation.1 | async-start | bytes 524288 | tf_op jit(solution)/shard_map/all_to_all | solution.py:30
  45.5 12.1 %all-to-all-start.2 = ((f32[16,1,4096]{2,1,0:T(1,128)}), f32[16,1,4096]{2,1,0:T(1,128)S(1)}, u32[]{:S(2)}, u32[]{:S(2)}) async-start(f32[16,1,4096]{2,1,0:T(1,128)} %broadcast_in_dim.14), calls=%async_computation.2 | async-start | bytes 524288 | tf_op jit(solution)/shard_map/all_to_all | solution.py:32
  89.5 5.5 %collective-permute-start.2 = (f32[1,2,7,128]{3,2,1,0:T(8,128)S(1)}, f32[1,2,7,128]{3,2,1,0:T(8,128)S(1)}, u32[]{:S(2)}, u32[]{:S(2)}) collective-permute-start(f32[1,2,7,128]{3,2,1,0:T(8,128)S(1)} %slice.229), channel_id=1, source_target_pairs={{1,0},{2,1},{3,2},{4,3},{5,4},{6,5},{7,6},{8,7},{9,8},{10,9},{11,1... | collective-permute-start | bytes 21512 | tf_op jit(solution)/shard_map/ppermute | solution.py:24
  95.0 7.9 %collective-permute-start.1 = (f32[1,2,7,128]{3,2,1,0:T(8,128)S(1)}, f32[1,2,7,128]{3,2,1,0:T(8,128)S(1)}, u32[]{:S(2)}, u32[]{:S(2)}) collective-permute-start(f32[1,2,7,128]{3,2,1,0:T(8,128)S(1)} %get-tuple-element.23), channel_id=1, source_target_pairs={{0,1},{1,2},{2,3},{3,4},{4,5},{5,6},{6,7},{7,8},{8,9},{9,10},{10,1... | collective-permute-start | bytes 21512 | tf_op jit(solution)/shard_map/ppermute | solution.py:24
  107.7 11.3 %all-to-all-start.3 = ((f32[16,1,4096]{2,1,0:T(1,128)}), f32[16,1,4096]{2,1,0:T(1,128)S(1)}, u32[]{:S(2)}, u32[]{:S(2)}) async-start(f32[16,1,4096]{2,1,0:T(1,128)} %all_to_all.61), calls=%async_computation.3 | async-start | bytes 524288 | tf_op jit(solution)/shard_map/all_to_all | solution.py:30
  120.1 12.1 %all-to-all-start.4 = ((f32[16,1,4096]{2,1,0:T(1,128)}), f32[16,1,4096]{2,1,0:T(1,128)S(1)}, u32[]{:S(2)}, u32[]{:S(2)}) async-start(f32[16,1,4096]{2,1,0:T(1,128)} %broadcast_in_dim.17), calls=%async_computation.4 | async-start | bytes 524288 | tf_op jit(solution)/shard_map/all_to_all | solution.py:32
  161.7 19.1 %copy-start.1 = (s32[8]{0:T(128)S(1)}, s32[8]{0:T(128)}, u32[]{:S(2)}) copy-start(s32[8]{0:T(128)} %param.4) | copy-start | bytes 100
  164.1 7.7 %collective-permute-start.3 = (f32[1,2,7,128]{3,2,1,0:T(8,128)S(1)}, f32[1,2,7,128]{3,2,1,0:T(8,128)S(1)}, u32[]{:S(2)}, u32[]{:S(2)}) collective-permute-start(f32[1,2,7,128]{3,2,1,0:T(8,128)S(1)} %slice.251), channel_id=1, source_target_pairs={{0,1},{1,2},{2,3},{3,4},{4,5},{5,6},{6,7},{7,8},{8,9},{9,10},{10,1... | collective-permute-start | bytes 21512 | tf_op jit(solution)/shard_map/ppermute | solution.py:24

commit v3 on v2

--- a/solution.py
+++ b/solution.py
@@ -236,9 +236,8 @@
         slices = (full[:, :, :strip_width, :] + spill) / counts
     out_scale = math.sqrt(2.0 / kept_bins.shape[0])
     received = lax.all_to_all(slices, "freq", split_axis=3, concat_axis=0, tiled=True)
-    synth = product("fxy,tf->xyt", received[:, 0], cosines)
-    synth = synth - product("fxy,tf->xyt", received[:, 1], sines)
-    return out_scale * synth
+    basis_waves = jnp.stack([cosines * out_scale, -sines * out_scale], axis=1)
+    return product("fcxy,tcf->xyt", received, basis_waves)
 
 
 def solution(mesh):

time: 185 us -> 189 us (1.022)
  local copies, waits for them, and re-layouts: 16.5 us -> 20.5 us
  other arithmetic: 12.4 us -> 16.2 us
  matrix products: 25.2 us -> 22.4 us
    dot_general x13 -> x12, matrix products: 25.2 us -> 22.4 us  [product(): jnp.einsum(form, left, right, precision=precision, preferred_element_type...]
  transfers between devices with their start and end apart: 9 -> 9, of which waited for: 9 -> 9; matrix products, arithmetic and copies ran while one was open for 7% -> 8% of each run, Pallas kernels for 0% -> 0%
where the time goes in v3:
time: 189 us; the launch traced here: 188 us
  Pallas kernels  46.5 us (25%)
  starting transfers between devices  43 us (23%)
  waiting for transfers between devices  31.4 us (17%)
  matrix products  22.4 us (12%)
  local copies, waits for them, and re-layouts  20.5 us (11%)
  other arithmetic  16.2 us (9%)
  blocking collectives  7.67 us (4%)
    pallas_call x2, Pallas kernels, power_steps(): pl.pallas_call(power_kernel, out_shape=jax.ShapeDtypeStruct(subspace.shap...  46.5 us
    dot_general x12, matrix products, product(): jnp.einsum(form, left, right, precision=precision, preferred_element_type...  22.4 us
    ppermute x4, starting transfers between devices, shifted(): return lax.ppermute(x, axis, pairs)  14.6 us
    ppermute x4, waiting for transfers between devices, shifted(): return lax.ppermute(x, axis, pairs)  13.6 us
    all_to_all x2, starting transfers between devices, all_sum(): mine = lax.all_to_all(chunks, axis, 0, 0, tiled=True).sum(axis=0)  13.4 us
    all_to_all x2, starting transfers between devices, all_sum(): return lax.all_to_all(copies, axis, 0, 0, tiled=True).reshape(x.shape)  10.7 us
    all_to_all x2, waiting for transfers between devices, all_sum(): mine = lax.all_to_all(chunks, axis, 0, 0, tiled=True).sum(axis=0)  9.7 us
    all_to_all x1, blocking collectives, on_device(): lax.all_to_all(slices, 'freq', split_axis=3, concat_axis=0, tiled=True)  7.67 us
  transfers between devices with their start and end apart: 9, of which 9 were waited for; matrix products, arithmetic and copies ran while one was open for 8% of the time, Pallas kernels for 0%

profile of v3, /device:TPU:8, one launch (start us, length us, event | category | flops | bytes accessed | tf_op | source)
XLA Modules:
  0.0 188.1 jit_solution(9320364763894278350)
XLA Ops:
  0.0 1.1 broadcast_multiply_fusion.3
  1.2 3.8 %convolution_bitcast_fusion.3 = f32[8,2,8,16]{3,0,2,1:T(8,128)S(1)} fusion(f32[8,16,2048]{2,1,0:T(8,128)S(1)} %copy-done, f32[2048,1,8]{0,2,1:T(8,128)S(1)} %get-tuple-element.29, f32[2048,1,8]{0,2,1:T(8,128)S(1)} %get-tuple-element.27), kind=kOutput, calls=%fused_computation.27 | convolution fusion | flops 50364416 | bytes 1187840 | tf_op jit(solution)/shard_map/xyt,tcf->fcxy/dot_general | solution.py:36
  5.0 0.7 reshape.1040
  5.7 4.3 %all-to-all-start = ((f32[8,1,256]{2,1,0:T(1,128)}), f32[8,1,256]{2,1,0:T(1,128)S(1)}, u32[]{:S(2)}, u32[]{:S(2)}) async-start(f32[8,1,256]{2,1,0:T(1,128)} %reshape.1040), calls=%async_computation | async-start | bytes 16384 | tf_op jit(solution)/shard_map/all_to_all | solution.py:184
  10.0 0.8 slice_bitcast_fusion.16
  10.8 0.8 fusion.141
  11.6 0.6 fusion.98
  12.3 0.7 maximum_maximum_fusion.start_ref
  13.0 2.4 %all-to-all-done = f32[8,1,256]{2,1,0:T(1,128)S(1)} async-done(((f32[8,1,256]{2,1,0:T(1,128)}), f32[8,1,256]{2,1,0:T(1,128)S(1)}, u32[]{:S(2)}, u32[]{:S(2)}) %all-to-all-start) | async-done | bytes 8224 | tf_op jit(solution)/shard_map/all_to_all | solution.py:184
  15.3 0.5 broadcast.1307
  15.8 0.6 reduce.4
  16.6 5.8 %collective-permute-start = (f32[1,2,7,128]{3,2,1,0:T(8,128)S(1)}, f32[1,2,7,128]{3,2,1,0:T(8,128)S(1)}, u32[]{:S(2)}, u32[]{:S(2)}) collective-permute-start(f32[1,2,7,128]{3,2,1,0:T(8,128)S(1)} %bitcast.281), channel_id=1, source_target_pairs={{1,0},{2,1},{3,2},{4,3},{5,4},{6,5},{7,6},{8,7},{9,8},{10,9},{11,1... | collective-permute-start | bytes 21512 | tf_op jit(solution)/shard_map/ppermute | solution.py:24
  22.5 1.3 collective-permute-done
  23.8 0.9 fusion.27
  25.0 0.2 broadcast_multiply_fusion.1
  25.5 2.1 %fusion.21 = f32[1,512,512]{2,1,0:T(8,128)S(1)} fusion(f32[64,8,8,128]{3,2,1,0:T(8,128)S(1)} %bitcast.273), kind=kOutput, calls=%fused_computation.21 | convolution fusion | flops 1610612736 | bytes 3145728 | tf_op jit(solution)/shard_map/fik,fjk->fij/dot_general | solution.py:36
  27.7 1.0 all_to_all.60
  28.7 8.9 %all-to-all-start.1 = ((f32[16,1,4096]{2,1,0:T(1,128)}), f32[16,1,4096]{2,1,0:T(1,128)S(1)}, u32[]{:S(2)}, u32[]{:S(2)}) async-start(f32[16,1,4096]{2,1,0:T(1,128)} %all_to_all.60), calls=%async_computation.1 | async-start | bytes 524288 | tf_op jit(solution)/shard_map/all_to_all | solution.py:30
  37.6 0.7 broadcast_multiply_fusion.5
  38.3 1.6 copy.33
  39.9 4.5 %all-to-all-done.1 = f32[16,1,4096]{2,1,0:T(1,128)S(1)} async-done(((f32[16,1,4096]{2,1,0:T(1,128)}), f32[16,1,4096]{2,1,0:T(1,128)S(1)}, u32[]{:S(2)}, u32[]{:S(2)}) %all-to-all-start.1) | async-done | bytes 262176 | tf_op jit(solution)/shard_map/all_to_all | solution.py:30
  44.5 0.9 broadcast_in_dim.14
  45.4 5.3 %all-to-all-start.2 = ((f32[16,1,4096]{2,1,0:T(1,128)}), f32[16,1,4096]{2,1,0:T(1,128)S(1)}, u32[]{:S(2)}, u32[]{:S(2)}) async-start(f32[16,1,4096]{2,1,0:T(1,128)} %broadcast_in_dim.14), calls=%async_computation.2 | async-start | bytes 524288 | tf_op jit(solution)/shard_map/all_to_all | solution.py:32
  50.8 2.1 %fusion.4 = f32[1024,512]{0,1:T(8,128)S(1)} fusion(f32[64,8,8,128]{3,2,1,0:T(8,128)} %bitcast.270, f32[1024]{0:T(1024)S(1)} %broadcast_bitcast_fusion), kind=kLoop, calls=%fused_computation.7 | loop fusion | flops 524288 | bytes 4198400 | tf_op jit(solution)/shard_map/fjk,fkc->fjc/dot_general | solution.py:36
  52.8 1.8 copy.62
  54.7 2.9 %all-to-all-done.2 = f32[16,1,4096]{2,1,0:T(1,128)S(1)} async-done(((f32[16,1,4096]{2,1,0:T(1,128)}), f32[16,1,4096]{2,1,0:T(1,128)S(1)}, u32[]{:S(2)}, u32[]{:S(2)}) %all-to-all-start.2) | async-done | bytes 262176 | tf_op jit(solution)/shard_map/all_to_all | solution.py:32
  57.6 1.3 reduce.2
  58.9 1.7 reshape.1017.cov_ref
  60.6 23.2 %shard_map.37.start_ref = f32[1,80,512]{2,1,0:T(8,128)} custom-call(f32[1,256,256]{2,1,0:T(8,128)} %reshape.1017.cov_ref, f32[1,80,512]{2,1,0:T(8,128)} %maximum_maximum_fusion.start_ref), custom_call_target="tpu_custom_call" | custom-call | tf_op jit(solution)/shard_map/pallas_call | solution.py:158
  83.8 1.7 multiply_bitcast_fusion.1
  85.5 1.0 copy.32
  86.6 2.0 %convolution_bitcast_fusion.2 = f32[8,128,80,1,1]{1,2,0,4,3:T(8,128)S(1)} fusion(f32[8,128,512]{2,1,0:T(8,128)S(1)} %bitcast.272, f32[1,80,512]{2,1,0:T(8,128)} %shard_map.37.start_ref, f32[80]{0:T(128)S(1)} %compare_select_fusion), kind=kOutput, calls=%fused_computation.26 | convolution fusion | flops 251699200 | bytes 2588992 | tf_op jit(solution)/shard_map/fjk,fkc->fjc/dot_general | solution.py:36
  88.6 1.0 fusion.143
  89.6 2.3 %fusion.33 = f32[1,2,8,8,128]{4,3,2,1,0:T(8,128)S(1)} fusion(f32[2,8,32,8,128]{4,2,3,1,0:T(8,128)S(1)} %fusion.143, pred[128]{0:T(512)(128)(4,1)S(1)} %copy-done.6), kind=kOutput, calls=%fused_computation.28 | convolution fusion | flops 806879232 | bytes 2162816 | tf_op jit(solution)/shard_map/fcabxy,vby->fcaxv/dot_general | solution.py:36
  91.9 4.2 %collective-permute-start.2 = (f32[1,2,7,128]{3,2,1,0:T(8,128)S(1)}, f32[1,2,7,128]{3,2,1,0:T(8,128)S(1)}, u32[]{:S(2)}, u32[]{:S(2)}) collective-permute-start(f32[1,2,7,128]{3,2,1,0:T(8,128)S(1)} %slice.221), channel_id=1, source_target_pairs={{1,0},{2,1},{3,2},{4,3},{5,4},{6,5},{7,6},{8,7},{9,8},{10,9},{11,1... | collective-permute-start | bytes 21512 | tf_op jit(solution)/shard_map/ppermute | solution.py:24
  96.1 1.4 collective-permute-done.2
  97.5 2.3 %collective-permute-start.1 = (f32[1,2,7,128]{3,2,1,0:T(8,128)S(1)}, f32[1,2,7,128]{3,2,1,0:T(8,128)S(1)}, u32[]{:S(2)}, u32[]{:S(2)}) collective-permute-start(f32[1,2,7,128]{3,2,1,0:T(8,128)S(1)} %get-tuple-element.23), channel_id=1, source_target_pairs={{0,1},{1,2},{2,3},{3,4},{4,5},{5,6},{6,7},{7,8},{8,9},{9,10},{10,1... | collective-permute-start | bytes 21512 | tf_op jit(solution)/shard_map/ppermute | solution.py:24
  99.8 5.6 %collective-permute-done.1 = f32[1,2,7,128]{3,2,1,0:T(8,128)S(1)} collective-permute-done((f32[1,2,7,128]{3,2,1,0:T(8,128)S(1)}, f32[1,2,7,128]{3,2,1,0:T(8,128)S(1)}, u32[]{:S(2)}, u32[]{:S(2)}) %collective-permute-start.1) | collective-permute-done | bytes 7200 | tf_op jit(solution)/shard_map/ppermute | solution.py:24
  105.4 0.9 fusion.30
  106.6 0.3 copy-done.4
  106.9 0.2 broadcast_multiply_fusion
  107.4 2.1 %fusion.24 = f32[1,512,512]{2,1,0:T(8,128)S(1)} fusion(f32[64,8,8,128]{3,2,1,0:T(8,128)S(1)} %bitcast.274), kind=kOutput, calls=%fused_computation.22 | convolution fusion | flops 1610612736 | bytes 3145728 | tf_op jit(solution)/shard_map/fik,fjk->fij/dot_general | solution.py:36
  109.6 1.0 all_to_all.61
  110.6 4.5 %all-to-all-start.3 = ((f32[16,1,4096]{2,1,0:T(1,128)}), f32[16,1,4096]{2,1,0:T(1,128)S(1)}, u32[]{:S(2)}, u32[]{:S(2)}) async-start(f32[16,1,4096]{2,1,0:T(1,128)} %all_to_all.61), calls=%async_computation.3 | async-start | bytes 524288 | tf_op jit(solution)/shard_map/all_to_all | solution.py:30
  115.1 1.6 copy.46
  116.6 5.2 %all-to-all-done.3 = f32[16,1,4096]{2,1,0:T(1,128)S(1)} async-done(((f32[16,1,4096]{2,1,0:T(1,128)}), f32[16,1,4096]{2,1,0:T(1,128)S(1)}, u32[]{:S(2)}, u32[]{:S(2)}) %all-to-all-start.3) | async-done | bytes 262176 | tf_op jit(solution)/shard_map/all_to_all | solution.py:30
  122.1 0.9 broadcast_in_dim.17
  123.0 5.3 %all-to-all-start.4 = ((f32[16,1,4096]{2,1,0:T(1,128)}), f32[16,1,4096]{2,1,0:T(1,128)S(1)}, u32[]{:S(2)}, u32[]{:S(2)}) async-start(f32[16,1,4096]{2,1,0:T(1,128)} %broadcast_in_dim.17), calls=%async_computation.4 | async-start | bytes 524288 | tf_op jit(solution)/shard_map/all_to_all | solution.py:32
  128.3 2.1 %fusion = f32[1024,512]{0,1:T(8,128)S(1)} fusion(f32[64,8,8,128]{3,2,1,0:T(8,128)} %bitcast.269, f32[1024]{0:T(1024)S(1)} %broadcast_bitcast_fusion), kind=kLoop, calls=%fused_computation.2 | loop fusion | flops 524288 | bytes 4198400 | tf_op jit(solution)/shard_map/fjk,fkc->fjc/dot_general | solution.py:36
  130.4 1.8 copy.63
  132.2 2.9 %all-to-all-done.4 = f32[16,1,4096]{2,1,0:T(1,128)S(1)} async-done(((f32[16,1,4096]{2,1,0:T(1,128)}), f32[16,1,4096]{2,1,0:T(1,128)S(1)}, u32[]{:S(2)}, u32[]{:S(2)}) %all-to-all-start.4) | async-done | bytes 262176 | tf_op jit(solution)/shard_map/all_to_all | solution.py:32
  135.1 1.3 reduce.3
  136.4 1.7 reshape.1020.cov_ref
  138.1 23.2 %shard_map.38 = f32[1,80,512]{2,1,0:T(8,128)} custom-call(f32[1,256,256]{2,1,0:T(8,128)} %reshape.1020.cov_ref, f32[1,80,512]{2,1,0:T(8,128)} %shard_map.37.start_ref), custom_call_target="tpu_custom_call" | custom-call | tf_op jit(solution)/shard_map/pallas_call | solution.py:158
  161.4 1.6 multiply_bitcast_fusion
  163.0 1.0 copy.45
  164.1 2.0 %convolution_bitcast_fusion.1 = f32[8,128,80,1,1]{1,2,0,4,3:T(8,128)S(1)} fusion(f32[8,128,512]{2,1,0:T(8,128)S(1)} %bitcast.271, f32[1,80,512]{2,1,0:T(8,128)} %shard_map.38, f32[80]{0:T(128)S(1)} %compare_select_fusion), kind=kOutput, calls=%fused_computation.25 | convolution fusion | flops 251699200 | bytes 2588992 | tf_op jit(solution)/shard_map/fjk,fkc->fjc/dot_general | solution.py:36
  166.1 1.0 fusion.144
  167.1 2.3 %fusion.38 = f32[2,8,8,128]{3,2,1,0:T(8,128)S(1)} fusion(f32[2,8,32,8,128]{4,2,3,1,0:T(8,128)S(1)} %fusion.144, pred[128]{0:T(512)(128)(4,1)S(1)} %copy-done.7), kind=kOutput, calls=%fused_computation.29 | convolution fusion | flops 806879232 | bytes 2162816 | tf_op jit(solution)/shard_map/fcabxy,vby->fcaxv/dot_general | solution.py:36
  169.5 2.3 %collective-permute-start.3 = (f32[1,2,7,128]{3,2,1,0:T(8,128)S(1)}, f32[1,2,7,128]{3,2,1,0:T(8,128)S(1)}, u32[]{:S(2)}, u32[]{:S(2)}) collective-permute-start(f32[1,2,7,128]{3,2,1,0:T(8,128)S(1)} %slice.243), channel_id=1, source_target_pairs={{0,1},{1,2},{2,3},{3,4},{4,5},{5,6},{6,7},{7,8},{8,9},{9,10},{10,1... | collective-permute-start | bytes 21512 | tf_op jit(solution)/shard_map/ppermute | solution.py:24
  171.8 5.3 %collective-permute-done.3 = f32[1,2,7,128]{3,2,1,0:T(8,128)S(1)} collective-permute-done((f32[1,2,7,128]{3,2,1,0:T(8,128)S(1)}, f32[1,2,7,128]{3,2,1,0:T(8,128)S(1)}, u32[]{:S(2)}, u32[]{:S(2)}) %collective-permute-start.3) | collective-permute-done | bytes 7200 | tf_op jit(solution)/shard_map/ppermute | solution.py:24
  177.5 7.7 %all_to_all.68 = f32[8,1,256]{2,1,0:T(1,128)S(1)} all-to-all(f32[8,1,256]{2,1,0:T(1,128)S(1)} %reshape.1042), channel_id=1, replica_groups=mesh['freq'=8,'space'=16] {'freq'}, dimensions={0} | all-to-all | bytes 16384 | tf_op jit(solution)/shard_map/all_to_all | solution.py:238
  185.2 0.6 reduce.5
  186.1 2.0 %convolution_bitcast_fusion = f32[8,16,2048]{2,1,0:T(8,128)} fusion(f32[2048,1,8]{0,2,1:T(8,128)S(1)} %get-tuple-element.30, f32[2048,1,8]{0,2,1:T(8,128)S(1)} %get-tuple-element.28, f32[1,2,8,8,16]{4,3,2,1,0:T(8,128)S(1)} %copy.64), kind=kOutput, calls=%fused_computation | convolution fusion | flops 50364416 | bytes 1187840 | tf_op jit(solution)/shard_map/fcxy,tcf->xyt/dot_general | solution.py:36
  (61 shorter events, 2.7 us)
Async XLA Ops:
  0.0 1.2 copy-start
  5.7 9.6 %all-to-all-start = ((f32[8,1,256]{2,1,0:T(1,128)}), f32[8,1,256]{2,1,0:T(1,128)S(1)}, u32[]{:S(2)}, u32[]{:S(2)}) async-start(f32[8,1,256]{2,1,0:T(1,128)} %reshape.1040), calls=%async_computation | async-start | bytes 16384 | tf_op jit(solution)/shard_map/all_to_all | solution.py:184
  11.6 13.4 %copy-start.3 = (f32[8]{0:T(128)}, f32[8]{0:T(128)S(1)}, u32[]{:S(2)}) copy-start(f32[8]{0:T(128)S(1)} %compare_convert_fusion) | copy-start | bytes 100
  13.0 11.9 %copy-start.5 = (pred[128]{0:T(512)(128)(4,1)}, pred[128]{0:T(512)(128)(4,1)S(1)}, u32[]{:S(2)}) copy-start(pred[128]{0:T(512)(128)(4,1)S(1)} %iota_compare_fusion.1) | copy-start | bytes 388
  16.6 7.2 %collective-permute-start = (f32[1,2,7,128]{3,2,1,0:T(8,128)S(1)}, f32[1,2,7,128]{3,2,1,0:T(8,128)S(1)}, u32[]{:S(2)}, u32[]{:S(2)}) collective-permute-start(f32[1,2,7,128]{3,2,1,0:T(8,128)S(1)} %bitcast.281), channel_id=1, source_target_pairs={{1,0},{2,1},{3,2},{4,3},{5,4},{6,5},{7,6},{8,7},{9,8},{10,9},{11,1... | collective-permute-start | bytes 21512 | tf_op jit(solution)/shard_map/ppermute | solution.py:24
  28.7 15.7 %all-to-all-start.1 = ((f32[16,1,4096]{2,1,0:T(1,128)}), f32[16,1,4096]{2,1,0:T(1,128)S(1)}, u32[]{:S(2)}, u32[]{:S(2)}) async-start(f32[16,1,4096]{2,1,0:T(1,128)} %all_to_all.60), calls=%async_computation.1 | async-start | bytes 524288 | tf_op jit(solution)/shard_map/all_to_all | solution.py:30
  45.4 12.1 %all-to-all-start.2 = ((f32[16,1,4096]{2,1,0:T(1,128)}), f32[16,1,4096]{2,1,0:T(1,128)S(1)}, u32[]{:S(2)}, u32[]{:S(2)}) async-start(f32[16,1,4096]{2,1,0:T(1,128)} %broadcast_in_dim.14), calls=%async_computation.2 | async-start | bytes 524288 | tf_op jit(solution)/shard_map/all_to_all | solution.py:32
  54.7 31.9 %copy-start.2 = (f32[1024,512]{1,0:T(8,128)S(1)}, f32[1024,512]{1,0:T(8,128)}, u32[]{:S(2)}) copy-start(f32[1024,512]{1,0:T(8,128)} %copy.62) | copy-start | bytes 6291460
  86.6 3.0 %copy-start.6 = (pred[128]{0:T(512)(128)(4,1)S(1)}, pred[128]{0:T(512)(128)(4,1)}, u32[]{:S(2)}) copy-start(pred[128]{0:T(512)(128)(4,1)} %copy-done.5) | copy-start | bytes 388
  91.9 5.5 %collective-permute-start.2 = (f32[1,2,7,128]{3,2,1,0:T(8,128)S(1)}, f32[1,2,7,128]{3,2,1,0:T(8,128)S(1)}, u32[]{:S(2)}, u32[]{:S(2)}) collective-permute-start(f32[1,2,7,128]{3,2,1,0:T(8,128)S(1)} %slice.221), channel_id=1, source_target_pairs={{1,0},{2,1},{3,2},{4,3},{5,4},{6,5},{7,6},{8,7},{9,8},{10,9},{11,1... | collective-permute-start | bytes 21512 | tf_op jit(solution)/shard_map/ppermute | solution.py:24
  97.5 7.9 %collective-permute-start.1 = (f32[1,2,7,128]{3,2,1,0:T(8,128)S(1)}, f32[1,2,7,128]{3,2,1,0:T(8,128)S(1)}, u32[]{:S(2)}, u32[]{:S(2)}) collective-permute-start(f32[1,2,7,128]{3,2,1,0:T(8,128)S(1)} %get-tuple-element.23), channel_id=1, source_target_pairs={{0,1},{1,2},{2,3},{3,4},{4,5},{5,6},{6,7},{7,8},{8,9},{9,10},{10,1... | collective-permute-start | bytes 21512 | tf_op jit(solution)/shard_map/ppermute | solution.py:24
  106.3 0.7 copy-start.4
  110.6 11.3 %all-to-all-start.3 = ((f32[16,1,4096]{2,1,0:T(1,128)}), f32[16,1,4096]{2,1,0:T(1,128)S(1)}, u32[]{:S(2)}, u32[]{:S(2)}) async-start(f32[16,1,4096]{2,1,0:T(1,128)} %all_to_all.61), calls=%async_computation.3 | async-start | bytes 524288 | tf_op jit(solution)/shard_map/all_to_all | solution.py:30
  123.0 12.1 %all-to-all-start.4 = ((f32[16,1,4096]{2,1,0:T(1,128)}), f32[16,1,4096]{2,1,0:T(1,128)S(1)}, u32[]{:S(2)}, u32[]{:S(2)}) async-start(f32[16,1,4096]{2,1,0:T(1,128)} %broadcast_in_dim.17), calls=%async_computation.4 | async-start | bytes 524288 | tf_op jit(solution)/shard_map/all_to_all | solution.py:32
  132.2 31.8 %copy-start.1 = (f32[1024,512]{1,0:T(8,128)S(1)}, f32[1024,512]{1,0:T(8,128)}, u32[]{:S(2)}) copy-start(f32[1024,512]{1,0:T(8,128)} %copy.63) | copy-start | bytes 6291460
  164.1 3.0 %copy-start.7 = (pred[128]{0:T(512)(128)(4,1)S(1)}, pred[128]{0:T(512)(128)(4,1)}, u32[]{:S(2)}) copy-start(pred[128]{0:T(512)(128)(4,1)} %copy-done.5) | copy-start | bytes 388
  169.5 7.7 %collective-permute-start.3 = (f32[1,2,7,128]{3,2,1,0:T(8,128)S(1)}, f32[1,2,7,128]{3,2,1,0:T(8,128)S(1)}, u32[]{:S(2)}, u32[]{:S(2)}) collective-permute-start(f32[1,2,7,128]{3,2,1,0:T(8,128)S(1)} %slice.243), channel_id=1, source_target_pairs={{0,1},{1,2},{2,3},{3,4},{4,5},{5,6},{6,7},{7,8},{8,9},{9,10},{10,1... | collective-permute-start | bytes 21512 | tf_op jit(solution)/shard_map/ppermute | solution.py:24

commit v4 on v2

--- a/solution.py
+++ b/solution.py
@@ -222,7 +222,7 @@
         coeffs = product("fjk,fkc->fjc", weights, matrix, lax.Precision.HIGH)
         projected = product("fjk,fjc->fkc", weights, coeffs, lax.Precision.HIGH)
         projected = projected.reshape(freq_count, 2, LX, LY, strip_width, trace_cols)
-        along_y = product("fcabxy,vby->fcaxv", projected, lag_shift)
+        along_y = product("fcabxy,vby->fcaxv", projected, lag_shift, lax.Precision.HIGH)
         full = sum(
             jnp.pad(along_y[:, :, lag_x], ((0, 0), (0, 0), (lag_x, LX - 1 - lag_x), (0, 0)))
             for lag_x in range(LX)

time: 185 us -> 183 us (0.989)
  no operation moved by 1% of the time
where the time goes in v4:
time: 183 us; the launch traced here: 182 us
  Pallas kernels  46.5 us (25%)
  starting transfers between devices  43 us (23%)
  waiting for transfers between devices  32.6 us (18%)
  matrix products  23.4 us (13%)
  local copies, waits for them, and re-layouts  16.5 us (9%)
  other arithmetic  12.4 us (7%)
  blocking collectives  7.67 us (4%)
    pallas_call x2, Pallas kernels, power_steps(): pl.pallas_call(power_kernel, out_shape=jax.ShapeDtypeStruct(subspace.shap...  46.5 us
    dot_general x13, matrix products, product(): jnp.einsum(form, left, right, precision=precision, preferred_element_type...  23.4 us
    ppermute x4, starting transfers between devices, shifted(): return lax.ppermute(x, axis, pairs)  14.6 us
    ppermute x4, waiting for transfers between devices, shifted(): return lax.ppermute(x, axis, pairs)  13.6 us
    all_to_all x2, starting transfers between devices, all_sum(): mine = lax.all_to_all(chunks, axis, 0, 0, tiled=True).sum(axis=0)  13.4 us
    all_to_all x2, starting transfers between devices, all_sum(): return lax.all_to_all(copies, axis, 0, 0, tiled=True).reshape(x.shape)  10.7 us
    all_to_all x2, waiting for transfers between devices, all_sum(): mine = lax.all_to_all(chunks, axis, 0, 0, tiled=True).sum(axis=0)  10.4 us
    all_to_all x1, blocking collectives, on_device(): lax.all_to_all(slices, 'freq', split_axis=3, concat_axis=0, tiled=True)  7.67 us
  transfers between devices with their start and end apart: 9, of which 9 were waited for; matrix products, arithmetic and copies ran while one was open for 7% of the time, Pallas kernels for 0%

profile of v4, /device:TPU:8, one launch (start us, length us, event | category | flops | bytes accessed | tf_op | source)
XLA Modules:
  0.0 182.5 jit_solution(9259721046605851738)
XLA Ops:
  0.0 1.1 cosine_multiply_fusion
  1.2 3.8 %convolution_bitcast_fusion.2 = f32[8,2,8,16]{3,0,2,1:T(8,128)S(1)} fusion(f32[8,16,2048]{2,1,0:T(8,128)S(1)} %copy-done, f32[2048,1,8]{0,2,1:T(8,128)S(1)} %get-tuple-element.28, f32[2048,1,8]{0,2,1:T(8,128)S(1)} %get-tuple-element.27), kind=kOutput, calls=%fused_computation.28 | convolution fusion | flops 50364416 | bytes 1187840 | tf_op jit(solution)/shard_map/xyt,tcf->fcxy/dot_general | solution.py:36
  5.0 0.7 reshape.996
  5.7 4.3 %all-to-all-start = ((f32[8,1,256]{2,1,0:T(1,128)}), f32[8,1,256]{2,1,0:T(1,128)S(1)}, u32[]{:S(2)}, u32[]{:S(2)}) async-start(f32[8,1,256]{2,1,0:T(1,128)} %reshape.996), calls=%async_computation | async-start | bytes 16384 | tf_op jit(solution)/shard_map/all_to_all | solution.py:184
  10.0 0.8 slice_bitcast_fusion.16
  10.8 0.8 fusion.156
  11.7 0.7 maximum_maximum_fusion.start_ref
  12.4 3.0 %all-to-all-done = f32[8,1,256]{2,1,0:T(1,128)S(1)} async-done(((f32[8,1,256]{2,1,0:T(1,128)}), f32[8,1,256]{2,1,0:T(1,128)S(1)}, u32[]{:S(2)}, u32[]{:S(2)}) %all-to-all-start) | async-done | bytes 8224 | tf_op jit(solution)/shard_map/all_to_all | solution.py:184
  15.3 0.5 broadcast.1219
  15.9 0.7 reduce.4
  16.7 5.8 %collective-permute-start = (f32[1,2,7,128]{3,2,1,0:T(8,128)S(1)}, f32[1,2,7,128]{3,2,1,0:T(8,128)S(1)}, u32[]{:S(2)}, u32[]{:S(2)}) collective-permute-start(f32[1,2,7,128]{3,2,1,0:T(8,128)S(1)} %bitcast.286), channel_id=1, source_target_pairs={{1,0},{2,1},{3,2},{4,3},{5,4},{6,5},{7,6},{8,7},{9,8},{10,9},{11,1... | collective-permute-start | bytes 21512 | tf_op jit(solution)/shard_map/ppermute | solution.py:24
  22.6 1.3 collective-permute-done
  23.9 0.9 fusion.28
  25.1 0.2 broadcast_multiply_fusion.1
  25.4 0.2 copy.28
  25.6 2.1 %fusion.22 = f32[1,512,512]{2,1,0:T(8,128)S(1)} fusion(f32[64,8,8,128]{3,2,1,0:T(8,128)S(1)} %bitcast.276), kind=kOutput, calls=%fused_computation.22 | convolution fusion | flops 1610612736 | bytes 3145728 | tf_op jit(solution)/shard_map/fik,fjk->fij/dot_general | solution.py:36
  27.8 1.0 all_to_all.60
  28.7 8.9 %all-to-all-start.1 = ((f32[16,1,4096]{2,1,0:T(1,128)}), f32[16,1,4096]{2,1,0:T(1,128)S(1)}, u32[]{:S(2)}, u32[]{:S(2)}) async-start(f32[16,1,4096]{2,1,0:T(1,128)} %all_to_all.60), calls=%async_computation.1 | async-start | bytes 524288 | tf_op jit(solution)/shard_map/all_to_all | solution.py:30
  37.7 1.6 copy.31
  39.3 5.1 %all-to-all-done.1 = f32[16,1,4096]{2,1,0:T(1,128)S(1)} async-done(((f32[16,1,4096]{2,1,0:T(1,128)}), f32[16,1,4096]{2,1,0:T(1,128)S(1)}, u32[]{:S(2)}, u32[]{:S(2)}) %all-to-all-start.1) | async-done | bytes 262176 | tf_op jit(solution)/shard_map/all_to_all | solution.py:30
  44.6 0.9 broadcast_in_dim.14
  45.5 5.3 %all-to-all-start.2 = ((f32[16,1,4096]{2,1,0:T(1,128)}), f32[16,1,4096]{2,1,0:T(1,128)S(1)}, u32[]{:S(2)}, u32[]{:S(2)}) async-start(f32[16,1,4096]{2,1,0:T(1,128)} %broadcast_in_dim.14), calls=%async_computation.2 | async-start | bytes 524288 | tf_op jit(solution)/shard_map/all_to_all | solution.py:32
  50.9 2.1 %fusion.5 = f32[1024,512]{0,1:T(8,128)S(1)} fusion(f32[64,8,8,128]{3,2,1,0:T(8,128)} %bitcast.273, f32[1024]{0:T(1024)S(1)} %broadcast_bitcast_fusion), kind=kLoop, calls=%fused_computation.8 | loop fusion | flops 524288 | bytes 4198400 | tf_op jit(solution)/shard_map/fjk,fkc->fjc/dot_general | solution.py:36
  52.9 1.9 %copy.59 = f32[1024,512]{1,0:T(8,128)} copy(f32[1024,512]{0,1:T(8,128)S(1)} %fusion.5) | data formatting | bytes 4194304 | tf_op jit(solution)/shard_map/fjk,fkc->fjc/dot_general | solution.py:36
  54.8 2.9 %all-to-all-done.2 = f32[16,1,4096]{2,1,0:T(1,128)S(1)} async-done(((f32[16,1,4096]{2,1,0:T(1,128)}), f32[16,1,4096]{2,1,0:T(1,128)S(1)}, u32[]{:S(2)}, u32[]{:S(2)}) %all-to-all-start.2) | async-done | bytes 262176 | tf_op jit(solution)/shard_map/all_to_all | solution.py:32
  57.7 0.6 reduce.2
  58.3 0.7 reshape.973.cov_ref
  59.0 23.2 %shard_map.37.start_ref = f32[1,80,512]{2,1,0:T(8,128)} custom-call(f32[1,256,256]{2,1,0:T(8,128)} %reshape.973.cov_ref, f32[1,80,512]{2,1,0:T(8,128)} %maximum_maximum_fusion.start_ref), custom_call_target="tpu_custom_call" | custom-call | tf_op jit(solution)/shard_map/pallas_call | solution.py:158
  82.3 1.0 multiply_bitcast_fusion.1
  83.3 2.7 %convolution_bitcast_fusion.1 = f32[8,128,80,1,1]{1,2,0,4,3:T(8,128)S(1)} fusion(f32[8,128,512]{2,1,0:T(8,128)} %bitcast.275, f32[1,80,512]{2,1,0:T(8,128)} %shard_map.37.start_ref, f32[80]{0:T(128)S(1)} %compare_select_fusion), kind=kOutput, calls=%fused_computation.27 | convolution fusion | flops 251699200 | bytes 2588992 | tf_op jit(solution)/shard_map/fjk,fkc->fjc/dot_general | solution.py:36
  86.1 1.0 fusion.158
  87.1 1.4 fusion.34
  88.5 4.2 %collective-permute-start.2 = (f32[1,2,7,128]{3,2,1,0:T(8,128)S(1)}, f32[1,2,7,128]{3,2,1,0:T(8,128)S(1)}, u32[]{:S(2)}, u32[]{:S(2)}) collective-permute-start(f32[1,2,7,128]{3,2,1,0:T(8,128)S(1)} %slice.229), channel_id=1, source_target_pairs={{1,0},{2,1},{3,2},{4,3},{5,4},{6,5},{7,6},{8,7},{9,8},{10,9},{11,1... | collective-permute-start | bytes 21512 | tf_op jit(solution)/shard_map/ppermute | solution.py:24
  92.7 1.4 collective-permute-done.2
  94.1 2.3 %collective-permute-start.1 = (f32[1,2,7,128]{3,2,1,0:T(8,128)S(1)}, f32[1,2,7,128]{3,2,1,0:T(8,128)S(1)}, u32[]{:S(2)}, u32[]{:S(2)}) collective-permute-start(f32[1,2,7,128]{3,2,1,0:T(8,128)S(1)} %get-tuple-element.23), channel_id=1, source_target_pairs={{0,1},{1,2},{2,3},{3,4},{4,5},{5,6},{6,7},{7,8},{8,9},{9,10},{10,1... | collective-permute-start | bytes 21512 | tf_op jit(solution)/shard_map/ppermute | solution.py:24
  96.4 5.6 %collective-permute-done.1 = f32[1,2,7,128]{3,2,1,0:T(8,128)S(1)} collective-permute-done((f32[1,2,7,128]{3,2,1,0:T(8,128)S(1)}, f32[1,2,7,128]{3,2,1,0:T(8,128)S(1)}, u32[]{:S(2)}, u32[]{:S(2)}) %collective-permute-start.1) | collective-permute-done | bytes 7200 | tf_op jit(solution)/shard_map/ppermute | solution.py:24
  102.0 0.9 fusion.31
  103.2 0.2 broadcast_multiply_fusion
  103.4 0.2 copy.41
  103.7 2.1 %fusion.25 = f32[1,512,512]{2,1,0:T(8,128)S(1)} fusion(f32[64,8,8,128]{3,2,1,0:T(8,128)S(1)} %bitcast.277), kind=kOutput, calls=%fused_computation.23 | convolution fusion | flops 1610612736 | bytes 3145728 | tf_op jit(solution)/shard_map/fik,fjk->fij/dot_general | solution.py:36
  105.9 1.0 all_to_all.61
  106.8 4.5 %all-to-all-start.3 = ((f32[16,1,4096]{2,1,0:T(1,128)}), f32[16,1,4096]{2,1,0:T(1,128)S(1)}, u32[]{:S(2)}, u32[]{:S(2)}) async-start(f32[16,1,4096]{2,1,0:T(1,128)} %all_to_all.61), calls=%async_computation.3 | async-start | bytes 524288 | tf_op jit(solution)/shard_map/all_to_all | solution.py:30
  111.3 1.6 copy.44
  112.9 5.2 %all-to-all-done.3 = f32[16,1,4096]{2,1,0:T(1,128)S(1)} async-done(((f32[16,1,4096]{2,1,0:T(1,128)}), f32[16,1,4096]{2,1,0:T(1,128)S(1)}, u32[]{:S(2)}, u32[]{:S(2)}) %all-to-all-start.3) | async-done | bytes 262176 | tf_op jit(solution)/shard_map/all_to_all | solution.py:30
  118.3 0.9 broadcast_in_dim.17
  119.2 5.3 %all-to-all-start.4 = ((f32[16,1,4096]{2,1,0:T(1,128)}), f32[16,1,4096]{2,1,0:T(1,128)S(1)}, u32[]{:S(2)}, u32[]{:S(2)}) async-start(f32[16,1,4096]{2,1,0:T(1,128)} %broadcast_in_dim.17), calls=%async_computation.4 | async-start | bytes 524288 | tf_op jit(solution)/shard_map/all_to_all | solution.py:32
  124.6 2.1 %fusion.1 = f32[1024,512]{0,1:T(8,128)S(1)} fusion(f32[64,8,8,128]{3,2,1,0:T(8,128)} %bitcast.272, f32[1024]{0:T(1024)S(1)} %broadcast_bitcast_fusion), kind=kLoop, calls=%fused_computation.3 | loop fusion | flops 524288 | bytes 4198400 | tf_op jit(solution)/shard_map/fjk,fkc->fjc/dot_general | solution.py:36
  126.6 1.9 %copy.60 = f32[1024,512]{1,0:T(8,128)} copy(f32[1024,512]{0,1:T(8,128)S(1)} %fusion.1) | data formatting | bytes 4194304 | tf_op jit(solution)/shard_map/fjk,fkc->fjc/dot_general | solution.py:36
  128.5 2.9 %all-to-all-done.4 = f32[16,1,4096]{2,1,0:T(1,128)S(1)} async-done(((f32[16,1,4096]{2,1,0:T(1,128)}), f32[16,1,4096]{2,1,0:T(1,128)S(1)}, u32[]{:S(2)}, u32[]{:S(2)}) %all-to-all-start.4) | async-done | bytes 262176 | tf_op jit(solution)/shard_map/all_to_all | solution.py:32
  131.4 0.6 reduce.3
  132.0 0.7 reshape.976.cov_ref
  132.7 23.2 %shard_map.38 = f32[1,80,512]{2,1,0:T(8,128)} custom-call(f32[1,256,256]{2,1,0:T(8,128)} %reshape.976.cov_ref, f32[1,80,512]{2,1,0:T(8,128)} %shard_map.37.start_ref), custom_call_target="tpu_custom_call" | custom-call | tf_op jit(solution)/shard_map/pallas_call | solution.py:158
  156.0 1.0 multiply_bitcast_fusion
  157.0 2.7 %convolution_bitcast_fusion = f32[8,128,80,1,1]{1,2,0,4,3:T(8,128)S(1)} fusion(f32[8,128,512]{2,1,0:T(8,128)} %bitcast.274, f32[1,80,512]{2,1,0:T(8,128)} %shard_map.38, f32[80]{0:T(128)S(1)} %compare_select_fusion), kind=kOutput, calls=%fused_computation.26 | convolution fusion | flops 251699200 | bytes 2588992 | tf_op jit(solution)/shard_map/fjk,fkc->fjc/dot_general | solution.py:36
  159.8 1.0 fusion.159
  160.8 1.4 fusion.39
  162.3 2.3 %collective-permute-start.3 = (f32[1,2,7,128]{3,2,1,0:T(8,128)S(1)}, f32[1,2,7,128]{3,2,1,0:T(8,128)S(1)}, u32[]{:S(2)}, u32[]{:S(2)}) collective-permute-start(f32[1,2,7,128]{3,2,1,0:T(8,128)S(1)} %slice.251), channel_id=1, source_target_pairs={{0,1},{1,2},{2,3},{3,4},{4,5},{5,6},{6,7},{7,8},{8,9},{9,10},{10,1... | collective-permute-start | bytes 21512 | tf_op jit(solution)/shard_map/ppermute | solution.py:24
  164.6 5.3 %collective-permute-done.3 = f32[1,2,7,128]{3,2,1,0:T(8,128)S(1)} collective-permute-done((f32[1,2,7,128]{3,2,1,0:T(8,128)S(1)}, f32[1,2,7,128]{3,2,1,0:T(8,128)S(1)}, u32[]{:S(2)}, u32[]{:S(2)}) %collective-permute-start.3) | collective-permute-done | bytes 7200 | tf_op jit(solution)/shard_map/ppermute | solution.py:24
  170.1 0.2 reshape.998
  170.3 7.7 %all_to_all.68 = f32[8,1,256]{2,1,0:T(1,128)S(1)} all-to-all(f32[8,1,256]{2,1,0:T(1,128)S(1)} %reshape.998), channel_id=1, replica_groups=mesh['freq'=8,'space'=16] {'freq'}, dimensions={0} | all-to-all | bytes 16384 | tf_op jit(solution)/shard_map/all_to_all | solution.py:238
  178.0 0.7 reduce.5
  178.6 0.2 reshape.999
  179.0 1.2 fusion.82
  180.2 2.2 %fusion = f32[8,16,2048]{2,1,0:T(8,128)} fusion(f32[8,16,2048]{2,1,0:T(8,128)S(1)} %fusion.82, f32[8,2,8,16]{3,0,2,1:T(8,128)S(1)} %bitcast.283, s32[8]{0:T(128)S(1)} %copy-done.1), kind=kOutput, calls=%fused_computation.1 | convolution fusion | flops 25919488 | bytes 2130432 | tf_op jit(solution)/shard_map/fxy,tf->xyt/dot_general | solution.py:36
  (50 shorter events, 2.1 us)
Async XLA Ops:
  0.0 1.2 copy-start
  5.7 9.6 %all-to-all-start = ((f32[8,1,256]{2,1,0:T(1,128)}), f32[8,1,256]{2,1,0:T(1,128)S(1)}, u32[]{:S(2)}, u32[]{:S(2)}) async-start(f32[8,1,256]{2,1,0:T(1,128)} %reshape.996), calls=%async_computation | async-start | bytes 16384 | tf_op jit(solution)/shard_map/all_to_all | solution.py:184
  16.7 7.2 %collective-permute-start = (f32[1,2,7,128]{3,2,1,0:T(8,128)S(1)}, f32[1,2,7,128]{3,2,1,0:T(8,128)S(1)}, u32[]{:S(2)}, u32[]{:S(2)}) collective-permute-start(f32[1,2,7,128]{3,2,1,0:T(8,128)S(1)} %bitcast.286), channel_id=1, source_target_pairs={{1,0},{2,1},{3,2},{4,3},{5,4},{6,5},{7,6},{8,7},{9,8},{10,9},{11,1... | collective-permute-start | bytes 21512 | tf_op jit(solution)/shard_map/ppermute | solution.py:24
  28.7 15.7 %all-to-all-start.1 = ((f32[16,1,4096]{2,1,0:T(1,128)}), f32[16,1,4096]{2,1,0:T(1,128)S(1)}, u32[]{:S(2)}, u32[]{:S(2)}) async-start(f32[16,1,4096]{2,1,0:T(1,128)} %all_to_all.60), calls=%async_computation.1 | async-start | bytes 524288 | tf_op jit(solution)/shard_map/all_to_all | solution.py:30
  45.5 12.1 %all-to-all-start.2 = ((f32[16,1,4096]{2,1,0:T(1,128)}), f32[16,1,4096]{2,1,0:T(1,128)S(1)}, u32[]{:S(2)}, u32[]{:S(2)}) async-start(f32[16,1,4096]{2,1,0:T(1,128)} %broadcast_in_dim.14), calls=%async_computation.2 | async-start | bytes 524288 | tf_op jit(solution)/shard_map/all_to_all | solution.py:32
  88.5 5.5 %collective-permute-start.2 = (f32[1,2,7,128]{3,2,1,0:T(8,128)S(1)}, f32[1,2,7,128]{3,2,1,0:T(8,128)S(1)}, u32[]{:S(2)}, u32[]{:S(2)}) collective-permute-start(f32[1,2,7,128]{3,2,1,0:T(8,128)S(1)} %slice.229), channel_id=1, source_target_pairs={{1,0},{2,1},{3,2},{4,3},{5,4},{6,5},{7,6},{8,7},{9,8},{10,9},{11,1... | collective-permute-start | bytes 21512 | tf_op jit(solution)/shard_map/ppermute | solution.py:24
  94.1 7.9 %collective-permute-start.1 = (f32[1,2,7,128]{3,2,1,0:T(8,128)S(1)}, f32[1,2,7,128]{3,2,1,0:T(8,128)S(1)}, u32[]{:S(2)}, u32[]{:S(2)}) collective-permute-start(f32[1,2,7,128]{3,2,1,0:T(8,128)S(1)} %get-tuple-element.23), channel_id=1, source_target_pairs={{0,1},{1,2},{2,3},{3,4},{4,5},{5,6},{6,7},{7,8},{8,9},{9,10},{10,1... | collective-permute-start | bytes 21512 | tf_op jit(solution)/shard_map/ppermute | solution.py:24
  106.8 11.3 %all-to-all-start.3 = ((f32[16,1,4096]{2,1,0:T(1,128)}), f32[16,1,4096]{2,1,0:T(1,128)S(1)}, u32[]{:S(2)}, u32[]{:S(2)}) async-start(f32[16,1,4096]{2,1,0:T(1,128)} %all_to_all.61), calls=%async_computation.3 | async-start | bytes 524288 | tf_op jit(solution)/shard_map/all_to_all | solution.py:30
  119.2 12.1 %all-to-all-start.4 = ((f32[16,1,4096]{2,1,0:T(1,128)}), f32[16,1,4096]{2,1,0:T(1,128)S(1)}, u32[]{:S(2)}, u32[]{:S(2)}) async-start(f32[16,1,4096]{2,1,0:T(1,128)} %broadcast_in_dim.17), calls=%async_computation.4 | async-start | bytes 524288 | tf_op jit(solution)/shard_map/all_to_all | solution.py:32
  160.8 18.2 %copy-start.1 = (s32[8]{0:T(128)S(1)}, s32[8]{0:T(128)}, u32[]{:S(2)}) copy-start(s32[8]{0:T(128)} %param.4) | copy-start | bytes 100
  162.3 7.7 %collective-permute-start.3 = (f32[1,2,7,128]{3,2,1,0:T(8,128)S(1)}, f32[1,2,7,128]{3,2,1,0:T(8,128)S(1)}, u32[]{:S(2)}, u32[]{:S(2)}) collective-permute-start(f32[1,2,7,128]{3,2,1,0:T(8,128)S(1)} %slice.251), channel_id=1, source_target_pairs={{0,1},{1,2},{2,3},{3,4},{4,5},{5,6},{6,7},{7,8},{8,9},{9,10},{10,1... | collective-permute-start | bytes 21512 | tf_op jit(solution)/shard_map/ppermute | solution.py:24

commit v5 on v4

--- a/solution.py
+++ b/solution.py
@@ -117,8 +117,8 @@
     return jnp.concatenate([-rows[:, width:], rows[:, :width]], axis=1)
 
 
-def dot(left, right):
-    return jnp.dot(left, right, precision=exact_mode, preferred_element_type=jnp.float32)
+def dot(left, right, precision=exact_mode):
+    return jnp.dot(left, right, precision=precision, preferred_element_type=jnp.float32)
 
 
 def power_kernel(cov_ref, start_ref, out_ref):
@@ -138,8 +138,10 @@
         sub_imag = subspace[:, width:]
         summed = jnp.concatenate(
             [
-                dot(sub_real, cov_real) + dot(sub_imag, cov_imag),
-                dot(sub_imag, cov_real) - dot(sub_real, cov_imag),
+                dot(sub_real, cov_real, lax.Precision.HIGH)
+                + dot(sub_imag, cov_imag, lax.Precision.HIGH),
+                dot(sub_imag, cov_real, lax.Precision.HIGH)
+                - dot(sub_real, cov_imag, lax.Precision.HIGH),
             ],
             axis=1,
         )

time: 183 us -> 182 us (level)
  Pallas kernels: 46.5 us -> 44.6 us
    pallas_call x2, Pallas kernels: 46.5 us -> 44.6 us  [power_steps(): pl.pallas_call(power_kernel, out_shape=jax.ShapeDtypeStruct(subspace.shap...]
where the time goes in v5:
time: 182 us; the launch traced here: 181 us
  Pallas kernels  44.6 us (25%)
  starting transfers between devices  43 us (24%)
  waiting for transfers between devices  32.6 us (18%)
  matrix products  23.4 us (13%)
  local copies, waits for them, and re-layouts  16.5 us (9%)
  other arithmetic  12.4 us (7%)
  blocking collectives  7.67 us (4%)
    pallas_call x2, Pallas kernels, power_steps(): pl.pallas_call(power_kernel, out_shape=jax.ShapeDtypeStruct(subspace.shap...  44.6 us
    dot_general x13, matrix products, product(): jnp.einsum(form, left, right, precision=precision, preferred_element_type...  23.4 us
    ppermute x4, starting transfers between devices, shifted(): return lax.ppermute(x, axis, pairs)  14.6 us
    ppermute x4, waiting for transfers between devices, shifted(): return lax.ppermute(x, axis, pairs)  13.6 us
    all_to_all x2, starting transfers between devices, all_sum(): mine = lax.all_to_all(chunks, axis, 0, 0, tiled=True).sum(axis=0)  13.4 us
    all_to_all x2, starting transfers between devices, all_sum(): return lax.all_to_all(copies, axis, 0, 0, tiled=True).reshape(x.shape)  10.7 us
    all_to_all x2, waiting for transfers between devices, all_sum(): mine = lax.all_to_all(chunks, axis, 0, 0, tiled=True).sum(axis=0)  10.4 us
    all_to_all x1, blocking collectives, on_device(): lax.all_to_all(slices, 'freq', split_axis=3, concat_axis=0, tiled=True)  7.67 us
  transfers between devices with their start and end apart: 9, of which 9 were waited for; matrix products, arithmetic and copies ran while one was open for 7% of the time, Pallas kernels for 0%

profile of v5, /device:TPU:8, one launch (start us, length us, event | category | flops | bytes accessed | tf_op | source)
XLA Modules:
  0.0 180.6 jit_solution(15641564042350279748)
XLA Ops:
  0.0 1.1 cosine_multiply_fusion
  1.2 3.8 %convolution_bitcast_fusion.2 = f32[8,2,8,16]{3,0,2,1:T(8,128)S(1)} fusion(f32[8,16,2048]{2,1,0:T(8,128)S(1)} %copy-done, f32[2048,1,8]{0,2,1:T(8,128)S(1)} %get-tuple-element.28, f32[2048,1,8]{0,2,1:T(8,128)S(1)} %get-tuple-element.27), kind=kOutput, calls=%fused_computation.28 | convolution fusion | flops 50364416 | bytes 1187840 | tf_op jit(solution)/shard_map/xyt,tcf->fcxy/dot_general | solution.py:36
  5.0 0.7 reshape.996
  5.7 4.3 %all-to-all-start = ((f32[8,1,256]{2,1,0:T(1,128)}), f32[8,1,256]{2,1,0:T(1,128)S(1)}, u32[]{:S(2)}, u32[]{:S(2)}) async-start(f32[8,1,256]{2,1,0:T(1,128)} %reshape.996), calls=%async_computation | async-start | bytes 16384 | tf_op jit(solution)/shard_map/all_to_all | solution.py:186
  10.0 0.8 slice_bitcast_fusion.16
  10.8 0.8 fusion.156
  11.7 0.7 maximum_maximum_fusion.start_ref
  12.4 3.0 %all-to-all-done = f32[8,1,256]{2,1,0:T(1,128)S(1)} async-done(((f32[8,1,256]{2,1,0:T(1,128)}), f32[8,1,256]{2,1,0:T(1,128)S(1)}, u32[]{:S(2)}, u32[]{:S(2)}) %all-to-all-start) | async-done | bytes 8224 | tf_op jit(solution)/shard_map/all_to_all | solution.py:186
  15.3 0.5 broadcast.1219
  15.9 0.7 reduce.4
  16.7 5.8 %collective-permute-start = (f32[1,2,7,128]{3,2,1,0:T(8,128)S(1)}, f32[1,2,7,128]{3,2,1,0:T(8,128)S(1)}, u32[]{:S(2)}, u32[]{:S(2)}) collective-permute-start(f32[1,2,7,128]{3,2,1,0:T(8,128)S(1)} %bitcast.286), channel_id=1, source_target_pairs={{1,0},{2,1},{3,2},{4,3},{5,4},{6,5},{7,6},{8,7},{9,8},{10,9},{11,1... | collective-permute-start | bytes 21512 | tf_op jit(solution)/shard_map/ppermute | solution.py:24
  22.6 1.3 collective-permute-done
  23.9 0.9 fusion.28
  25.1 0.2 broadcast_multiply_fusion.1
  25.4 0.2 copy.28
  25.6 2.1 %fusion.22 = f32[1,512,512]{2,1,0:T(8,128)S(1)} fusion(f32[64,8,8,128]{3,2,1,0:T(8,128)S(1)} %bitcast.276), kind=kOutput, calls=%fused_computation.22 | convolution fusion | flops 1610612736 | bytes 3145728 | tf_op jit(solution)/shard_map/fik,fjk->fij/dot_general | solution.py:36
  27.8 1.0 all_to_all.60
  28.7 8.9 %all-to-all-start.1 = ((f32[16,1,4096]{2,1,0:T(1,128)}), f32[16,1,4096]{2,1,0:T(1,128)S(1)}, u32[]{:S(2)}, u32[]{:S(2)}) async-start(f32[16,1,4096]{2,1,0:T(1,128)} %all_to_all.60), calls=%async_computation.1 | async-start | bytes 524288 | tf_op jit(solution)/shard_map/all_to_all | solution.py:30
  37.7 1.6 copy.31
  39.3 5.1 %all-to-all-done.1 = f32[16,1,4096]{2,1,0:T(1,128)S(1)} async-done(((f32[16,1,4096]{2,1,0:T(1,128)}), f32[16,1,4096]{2,1,0:T(1,128)S(1)}, u32[]{:S(2)}, u32[]{:S(2)}) %all-to-all-start.1) | async-done | bytes 262176 | tf_op jit(solution)/shard_map/all_to_all | solution.py:30
  44.6 0.9 broadcast_in_dim.14
  45.5 5.3 %all-to-all-start.2 = ((f32[16,1,4096]{2,1,0:T(1,128)}), f32[16,1,4096]{2,1,0:T(1,128)S(1)}, u32[]{:S(2)}, u32[]{:S(2)}) async-start(f32[16,1,4096]{2,1,0:T(1,128)} %broadcast_in_dim.14), calls=%async_computation.2 | async-start | bytes 524288 | tf_op jit(solution)/shard_map/all_to_all | solution.py:32
  50.9 2.1 %fusion.5 = f32[1024,512]{0,1:T(8,128)S(1)} fusion(f32[64,8,8,128]{3,2,1,0:T(8,128)} %bitcast.273, f32[1024]{0:T(1024)S(1)} %broadcast_bitcast_fusion), kind=kLoop, calls=%fused_computation.8 | loop fusion | flops 524288 | bytes 4198400 | tf_op jit(solution)/shard_map/fjk,fkc->fjc/dot_general | solution.py:36
  52.9 1.9 %copy.59 = f32[1024,512]{1,0:T(8,128)} copy(f32[1024,512]{0,1:T(8,128)S(1)} %fusion.5) | data formatting | bytes 4194304 | tf_op jit(solution)/shard_map/fjk,fkc->fjc/dot_general | solution.py:36
  54.8 2.9 %all-to-all-done.2 = f32[16,1,4096]{2,1,0:T(1,128)S(1)} async-done(((f32[16,1,4096]{2,1,0:T(1,128)}), f32[16,1,4096]{2,1,0:T(1,128)S(1)}, u32[]{:S(2)}, u32[]{:S(2)}) %all-to-all-start.2) | async-done | bytes 262176 | tf_op jit(solution)/shard_map/all_to_all | solution.py:32
  57.7 0.6 reduce.2
  58.3 0.7 reshape.973.cov_ref
  59.0 22.3 %shard_map.37.start_ref = f32[1,80,512]{2,1,0:T(8,128)} custom-call(f32[1,256,256]{2,1,0:T(8,128)} %reshape.973.cov_ref, f32[1,80,512]{2,1,0:T(8,128)} %maximum_maximum_fusion.start_ref), custom_call_target="tpu_custom_call" | custom-call | tf_op jit(solution)/shard_map/pallas_call | solution.py:160
  81.3 1.0 multiply_bitcast_fusion.1
  82.3 2.7 %convolution_bitcast_fusion.1 = f32[8,128,80,1,1]{1,2,0,4,3:T(8,128)S(1)} fusion(f32[8,128,512]{2,1,0:T(8,128)} %bitcast.275, f32[1,80,512]{2,1,0:T(8,128)} %shard_map.37.start_ref, f32[80]{0:T(128)S(1)} %compare_select_fusion), kind=kOutput, calls=%fused_computation.27 | convolution fusion | flops 251699200 | bytes 2588992 | tf_op jit(solution)/shard_map/fjk,fkc->fjc/dot_general | solution.py:36
  85.2 1.0 fusion.158
  86.1 1.4 fusion.34
  87.6 4.2 %collective-permute-start.2 = (f32[1,2,7,128]{3,2,1,0:T(8,128)S(1)}, f32[1,2,7,128]{3,2,1,0:T(8,128)S(1)}, u32[]{:S(2)}, u32[]{:S(2)}) collective-permute-start(f32[1,2,7,128]{3,2,1,0:T(8,128)S(1)} %slice.229), channel_id=1, source_target_pairs={{1,0},{2,1},{3,2},{4,3},{5,4},{6,5},{7,6},{8,7},{9,8},{10,9},{11,1... | collective-permute-start | bytes 21512 | tf_op jit(solution)/shard_map/ppermute | solution.py:24
  91.8 1.4 collective-permute-done.2
  93.2 2.3 %collective-permute-start.1 = (f32[1,2,7,128]{3,2,1,0:T(8,128)S(1)}, f32[1,2,7,128]{3,2,1,0:T(8,128)S(1)}, u32[]{:S(2)}, u32[]{:S(2)}) collective-permute-start(f32[1,2,7,128]{3,2,1,0:T(8,128)S(1)} %get-tuple-element.23), channel_id=1, source_target_pairs={{0,1},{1,2},{2,3},{3,4},{4,5},{5,6},{6,7},{7,8},{8,9},{9,10},{10,1... | collective-permute-start | bytes 21512 | tf_op jit(solution)/shard_map/ppermute | solution.py:24
  95.5 5.6 %collective-permute-done.1 = f32[1,2,7,128]{3,2,1,0:T(8,128)S(1)} collective-permute-done((f32[1,2,7,128]{3,2,1,0:T(8,128)S(1)}, f32[1,2,7,128]{3,2,1,0:T(8,128)S(1)}, u32[]{:S(2)}, u32[]{:S(2)}) %collective-permute-start.1) | collective-permute-done | bytes 7200 | tf_op jit(solution)/shard_map/ppermute | solution.py:24
  101.0 0.9 fusion.31
  102.3 0.2 broadcast_multiply_fusion
  102.5 0.2 copy.41
  102.7 2.1 %fusion.25 = f32[1,512,512]{2,1,0:T(8,128)S(1)} fusion(f32[64,8,8,128]{3,2,1,0:T(8,128)S(1)} %bitcast.277), kind=kOutput, calls=%fused_computation.23 | convolution fusion | flops 1610612736 | bytes 3145728 | tf_op jit(solution)/shard_map/fik,fjk->fij/dot_general | solution.py:36
  104.9 1.0 all_to_all.61
  105.9 4.5 %all-to-all-start.3 = ((f32[16,1,4096]{2,1,0:T(1,128)}), f32[16,1,4096]{2,1,0:T(1,128)S(1)}, u32[]{:S(2)}, u32[]{:S(2)}) async-start(f32[16,1,4096]{2,1,0:T(1,128)} %all_to_all.61), calls=%async_computation.3 | async-start | bytes 524288 | tf_op jit(solution)/shard_map/all_to_all | solution.py:30
  110.4 1.6 copy.44
  112.0 5.2 %all-to-all-done.3 = f32[16,1,4096]{2,1,0:T(1,128)S(1)} async-done(((f32[16,1,4096]{2,1,0:T(1,128)}), f32[16,1,4096]{2,1,0:T(1,128)S(1)}, u32[]{:S(2)}, u32[]{:S(2)}) %all-to-all-start.3) | async-done | bytes 262176 | tf_op jit(solution)/shard_map/all_to_all | solution.py:30
  117.4 0.9 broadcast_in_dim.17
  118.3 5.3 %all-to-all-start.4 = ((f32[16,1,4096]{2,1,0:T(1,128)}), f32[16,1,4096]{2,1,0:T(1,128)S(1)}, u32[]{:S(2)}, u32[]{:S(2)}) async-start(f32[16,1,4096]{2,1,0:T(1,128)} %broadcast_in_dim.17), calls=%async_computation.4 | async-start | bytes 524288 | tf_op jit(solution)/shard_map/all_to_all | solution.py:32
  123.6 2.1 %fusion.1 = f32[1024,512]{0,1:T(8,128)S(1)} fusion(f32[64,8,8,128]{3,2,1,0:T(8,128)} %bitcast.272, f32[1024]{0:T(1024)S(1)} %broadcast_bitcast_fusion), kind=kLoop, calls=%fused_computation.3 | loop fusion | flops 524288 | bytes 4198400 | tf_op jit(solution)/shard_map/fjk,fkc->fjc/dot_general | solution.py:36
  125.7 1.9 %copy.60 = f32[1024,512]{1,0:T(8,128)} copy(f32[1024,512]{0,1:T(8,128)S(1)} %fusion.1) | data formatting | bytes 4194304 | tf_op jit(solution)/shard_map/fjk,fkc->fjc/dot_general | solution.py:36
  127.6 2.9 %all-to-all-done.4 = f32[16,1,4096]{2,1,0:T(1,128)S(1)} async-done(((f32[16,1,4096]{2,1,0:T(1,128)}), f32[16,1,4096]{2,1,0:T(1,128)S(1)}, u32[]{:S(2)}, u32[]{:S(2)}) %all-to-all-start.4) | async-done | bytes 262176 | tf_op jit(solution)/shard_map/all_to_all | solution.py:32
  130.4 0.6 reduce.3
  131.1 0.7 reshape.976.cov_ref
  131.8 22.3 %shard_map.38 = f32[1,80,512]{2,1,0:T(8,128)} custom-call(f32[1,256,256]{2,1,0:T(8,128)} %reshape.976.cov_ref, f32[1,80,512]{2,1,0:T(8,128)} %shard_map.37.start_ref), custom_call_target="tpu_custom_call" | custom-call | tf_op jit(solution)/shard_map/pallas_call | solution.py:160
  154.1 1.0 multiply_bitcast_fusion
  155.1 2.7 %convolution_bitcast_fusion = f32[8,128,80,1,1]{1,2,0,4,3:T(8,128)S(1)} fusion(f32[8,128,512]{2,1,0:T(8,128)} %bitcast.274, f32[1,80,512]{2,1,0:T(8,128)} %shard_map.38, f32[80]{0:T(128)S(1)} %compare_select_fusion), kind=kOutput, calls=%fused_computation.26 | convolution fusion | flops 251699200 | bytes 2588992 | tf_op jit(solution)/shard_map/fjk,fkc->fjc/dot_general | solution.py:36
  157.9 1.0 fusion.159
  158.9 1.4 fusion.39
  160.4 2.3 %collective-permute-start.3 = (f32[1,2,7,128]{3,2,1,0:T(8,128)S(1)}, f32[1,2,7,128]{3,2,1,0:T(8,128)S(1)}, u32[]{:S(2)}, u32[]{:S(2)}) collective-permute-start(f32[1,2,7,128]{3,2,1,0:T(8,128)S(1)} %slice.251), channel_id=1, source_target_pairs={{0,1},{1,2},{2,3},{3,4},{4,5},{5,6},{6,7},{7,8},{8,9},{9,10},{10,1... | collective-permute-start | bytes 21512 | tf_op jit(solution)/shard_map/ppermute | solution.py:24
  162.7 5.3 %collective-permute-done.3 = f32[1,2,7,128]{3,2,1,0:T(8,128)S(1)} collective-permute-done((f32[1,2,7,128]{3,2,1,0:T(8,128)S(1)}, f32[1,2,7,128]{3,2,1,0:T(8,128)S(1)}, u32[]{:S(2)}, u32[]{:S(2)}) %collective-permute-start.3) | collective-permute-done | bytes 7200 | tf_op jit(solution)/shard_map/ppermute | solution.py:24
  168.2 0.2 reshape.998
  168.4 7.7 %all_to_all.68 = f32[8,1,256]{2,1,0:T(1,128)S(1)} all-to-all(f32[8,1,256]{2,1,0:T(1,128)S(1)} %reshape.998), channel_id=1, replica_groups=mesh['freq'=8,'space'=16] {'freq'}, dimensions={0} | all-to-all | bytes 16384 | tf_op jit(solution)/shard_map/all_to_all | solution.py:240
  176.1 0.7 reduce.5
  176.8 0.2 reshape.999
  177.1 1.2 fusion.82
  178.4 2.2 %fusion = f32[8,16,2048]{2,1,0:T(8,128)} fusion(f32[8,16,2048]{2,1,0:T(8,128)S(1)} %fusion.82, f32[8,2,8,16]{3,0,2,1:T(8,128)S(1)} %bitcast.283, s32[8]{0:T(128)S(1)} %copy-done.1), kind=kOutput, calls=%fused_computation.1 | convolution fusion | flops 25919488 | bytes 2130432 | tf_op jit(solution)/shard_map/fxy,tf->xyt/dot_general | solution.py:36
  (50 shorter events, 2.1 us)
Async XLA Ops:
  0.0 1.2 copy-start
  5.7 9.6 %all-to-all-start = ((f32[8,1,256]{2,1,0:T(1,128)}), f32[8,1,256]{2,1,0:T(1,128)S(1)}, u32[]{:S(2)}, u32[]{:S(2)}) async-start(f32[8,1,256]{2,1,0:T(1,128)} %reshape.996), calls=%async_computation | async-start | bytes 16384 | tf_op jit(solution)/shard_map/all_to_all | solution.py:186
  16.7 7.2 %collective-permute-start = (f32[1,2,7,128]{3,2,1,0:T(8,128)S(1)}, f32[1,2,7,128]{3,2,1,0:T(8,128)S(1)}, u32[]{:S(2)}, u32[]{:S(2)}) collective-permute-start(f32[1,2,7,128]{3,2,1,0:T(8,128)S(1)} %bitcast.286), channel_id=1, source_target_pairs={{1,0},{2,1},{3,2},{4,3},{5,4},{6,5},{7,6},{8,7},{9,8},{10,9},{11,1... | collective-permute-start | bytes 21512 | tf_op jit(solution)/shard_map/ppermute | solution.py:24
  28.7 15.7 %all-to-all-start.1 = ((f32[16,1,4096]{2,1,0:T(1,128)}), f32[16,1,4096]{2,1,0:T(1,128)S(1)}, u32[]{:S(2)}, u32[]{:S(2)}) async-start(f32[16,1,4096]{2,1,0:T(1,128)} %all_to_all.60), calls=%async_computation.1 | async-start | bytes 524288 | tf_op jit(solution)/shard_map/all_to_all | solution.py:30
  45.5 12.1 %all-to-all-start.2 = ((f32[16,1,4096]{2,1,0:T(1,128)}), f32[16,1,4096]{2,1,0:T(1,128)S(1)}, u32[]{:S(2)}, u32[]{:S(2)}) async-start(f32[16,1,4096]{2,1,0:T(1,128)} %broadcast_in_dim.14), calls=%async_computation.2 | async-start | bytes 524288 | tf_op jit(solution)/shard_map/all_to_all | solution.py:32
  87.6 5.5 %collective-permute-start.2 = (f32[1,2,7,128]{3,2,1,0:T(8,128)S(1)}, f32[1,2,7,128]{3,2,1,0:T(8,128)S(1)}, u32[]{:S(2)}, u32[]{:S(2)}) collective-permute-start(f32[1,2,7,128]{3,2,1,0:T(8,128)S(1)} %slice.229), channel_id=1, source_target_pairs={{1,0},{2,1},{3,2},{4,3},{5,4},{6,5},{7,6},{8,7},{9,8},{10,9},{11,1... | collective-permute-start | bytes 21512 | tf_op jit(solution)/shard_map/ppermute | solution.py:24
  93.2 7.9 %collective-permute-start.1 = (f32[1,2,7,128]{3,2,1,0:T(8,128)S(1)}, f32[1,2,7,128]{3,2,1,0:T(8,128)S(1)}, u32[]{:S(2)}, u32[]{:S(2)}) collective-permute-start(f32[1,2,7,128]{3,2,1,0:T(8,128)S(1)} %get-tuple-element.23), channel_id=1, source_target_pairs={{0,1},{1,2},{2,3},{3,4},{4,5},{5,6},{6,7},{7,8},{8,9},{9,10},{10,1... | collective-permute-start | bytes 21512 | tf_op jit(solution)/shard_map/ppermute | solution.py:24
  105.9 11.3 %all-to-all-start.3 = ((f32[16,1,4096]{2,1,0:T(1,128)}), f32[16,1,4096]{2,1,0:T(1,128)S(1)}, u32[]{:S(2)}, u32[]{:S(2)}) async-start(f32[16,1,4096]{2,1,0:T(1,128)} %all_to_all.61), calls=%async_computation.3 | async-start | bytes 524288 | tf_op jit(solution)/shard_map/all_to_all | solution.py:30
  118.3 12.1 %all-to-all-start.4 = ((f32[16,1,4096]{2,1,0:T(1,128)}), f32[16,1,4096]{2,1,0:T(1,128)S(1)}, u32[]{:S(2)}, u32[]{:S(2)}) async-start(f32[16,1,4096]{2,1,0:T(1,128)} %broadcast_in_dim.17), calls=%async_computation.4 | async-start | bytes 524288 | tf_op jit(solution)/shard_map/all_to_all | solution.py:32
  158.9 18.2 %copy-start.1 = (s32[8]{0:T(128)S(1)}, s32[8]{0:T(128)}, u32[]{:S(2)}) copy-start(s32[8]{0:T(128)} %param.4) | copy-start | bytes 100
  160.4 7.7 %collective-permute-start.3 = (f32[1,2,7,128]{3,2,1,0:T(8,128)S(1)}, f32[1,2,7,128]{3,2,1,0:T(8,128)S(1)}, u32[]{:S(2)}, u32[]{:S(2)}) collective-permute-start(f32[1,2,7,128]{3,2,1,0:T(8,128)S(1)} %slice.251), channel_id=1, source_target_pairs={{0,1},{1,2},{2,3},{3,4},{4,5},{5,6},{6,7},{7,8},{8,9},{9,10},{10,1... | collective-permute-start | bytes 21512 | tf_op jit(solution)/shard_map/ppermute | solution.py:24

commit v6 on v5

--- a/solution.py
+++ b/solution.py
@@ -182,7 +182,7 @@
     cosines, sines = tables(kept_bins)
     dft_scale = 1.0 / math.sqrt(NT)
     waves = jnp.stack([cosines * dft_scale, -sines * dft_scale], axis=1)
-    spectra_tile = product("xyt,tcf->fcxy", traces, waves)
+    spectra_tile = product("xyt,tcf->fcxy", traces, waves, lax.Precision.HIGH)
     slices = lax.all_to_all(spectra_tile, "freq", split_axis=0, concat_axis=3, tiled=True)
     freq_count = slices.shape[0]
     strip_width = slices.shape[2]

time: 182 us -> 180 us (0.989)
  matrix products: 23.4 us -> 21.5 us
  transfers between devices with their start and end apart: 9 -> 9, of which waited for: 9 -> 9; matrix products, arithmetic and copies ran while one was open for 7% -> 8% of each run, Pallas kernels for 0% -> 0%
where the time goes in v6:
time: 180 us; the launch traced here: 179 us
  Pallas kernels  44.6 us (25%)
  starting transfers between devices  43 us (24%)
  waiting for transfers between devices  32.6 us (18%)
  matrix products  21.5 us (12%)
  local copies, waits for them, and re-layouts  16.5 us (9%)
  other arithmetic  12.4 us (7%)
  blocking collectives  7.67 us (4%)
    pallas_call x2, Pallas kernels, power_steps(): pl.pallas_call(power_kernel, out_shape=jax.ShapeDtypeStruct(subspace.shap...  44.6 us
    dot_general x13, matrix products, product(): jnp.einsum(form, left, right, precision=precision, preferred_element_type...  21.5 us
    ppermute x4, starting transfers between devices, shifted(): return lax.ppermute(x, axis, pairs)  14.6 us
    ppermute x4, waiting for transfers between devices, shifted(): return lax.ppermute(x, axis, pairs)  13.6 us
    all_to_all x2, starting transfers between devices, all_sum(): mine = lax.all_to_all(chunks, axis, 0, 0, tiled=True).sum(axis=0)  13.4 us
    all_to_all x2, starting transfers between devices, all_sum(): return lax.all_to_all(copies, axis, 0, 0, tiled=True).reshape(x.shape)  10.7 us
    all_to_all x2, waiting for transfers between devices, all_sum(): mine = lax.all_to_all(chunks, axis, 0, 0, tiled=True).sum(axis=0)  10.4 us
    all_to_all x1, blocking collectives, on_device(): lax.all_to_all(slices, 'freq', split_axis=3, concat_axis=0, tiled=True)  7.67 us
  transfers between devices with their start and end apart: 9, of which 9 were waited for; matrix products, arithmetic and copies ran while one was open for 8% of the time, Pallas kernels for 0%

profile of v6, /device:TPU:8, one launch (start us, length us, event | category | flops | bytes accessed | tf_op | source)
XLA Modules:
  0.0 178.8 jit_solution(399639609080257099)
XLA Ops:
  0.0 1.1 cosine_multiply_fusion
  1.2 1.9 %convolution_bitcast_fusion.2 = f32[8,2,8,16]{3,0,2,1:T(8,128)S(1)} fusion(f32[8,16,2048]{2,1,0:T(8,128)S(1)} %copy-done, f32[2048,1,8]{0,2,1:T(8,128)S(1)} %get-tuple-element.28, f32[2048,1,8]{0,2,1:T(8,128)S(1)} %get-tuple-element.27), kind=kOutput, calls=%fused_computation.28 | convolution fusion | flops 25198592 | bytes 1187840 | tf_op jit(solution)/shard_map/xyt,tcf->fcxy/dot_general | solution.py:36
  3.2 0.7 reshape.996
  3.9 4.3 %all-to-all-start = ((f32[8,1,256]{2,1,0:T(1,128)}), f32[8,1,256]{2,1,0:T(1,128)S(1)}, u32[]{:S(2)}, u32[]{:S(2)}) async-start(f32[8,1,256]{2,1,0:T(1,128)} %reshape.996), calls=%async_computation | async-start | bytes 16384 | tf_op jit(solution)/shard_map/all_to_all | solution.py:186
  8.2 0.8 slice_bitcast_fusion.16
  9.0 0.8 fusion.156
  9.9 0.7 maximum_maximum_fusion.start_ref
  10.6 3.0 %all-to-all-done = f32[8,1,256]{2,1,0:T(1,128)S(1)} async-done(((f32[8,1,256]{2,1,0:T(1,128)}), f32[8,1,256]{2,1,0:T(1,128)S(1)}, u32[]{:S(2)}, u32[]{:S(2)}) %all-to-all-start) | async-done | bytes 8224 | tf_op jit(solution)/shard_map/all_to_all | solution.py:186
  13.5 0.5 broadcast.1219
  14.1 0.7 reduce.4
  14.9 5.8 %collective-permute-start = (f32[1,2,7,128]{3,2,1,0:T(8,128)S(1)}, f32[1,2,7,128]{3,2,1,0:T(8,128)S(1)}, u32[]{:S(2)}, u32[]{:S(2)}) collective-permute-start(f32[1,2,7,128]{3,2,1,0:T(8,128)S(1)} %bitcast.286), channel_id=1, source_target_pairs={{1,0},{2,1},{3,2},{4,3},{5,4},{6,5},{7,6},{8,7},{9,8},{10,9},{11,1... | collective-permute-start | bytes 21512 | tf_op jit(solution)/shard_map/ppermute | solution.py:24
  20.8 1.3 collective-permute-done
  22.1 0.9 fusion.28
  23.3 0.2 broadcast_multiply_fusion.1
  23.5 0.2 copy.28
  23.8 2.1 %fusion.22 = f32[1,512,512]{2,1,0:T(8,128)S(1)} fusion(f32[64,8,8,128]{3,2,1,0:T(8,128)S(1)} %bitcast.276), kind=kOutput, calls=%fused_computation.22 | convolution fusion | flops 1610612736 | bytes 3145728 | tf_op jit(solution)/shard_map/fik,fjk->fij/dot_general | solution.py:36
  26.0 1.0 all_to_all.60
  26.9 8.9 %all-to-all-start.1 = ((f32[16,1,4096]{2,1,0:T(1,128)}), f32[16,1,4096]{2,1,0:T(1,128)S(1)}, u32[]{:S(2)}, u32[]{:S(2)}) async-start(f32[16,1,4096]{2,1,0:T(1,128)} %all_to_all.60), calls=%async_computation.1 | async-start | bytes 524288 | tf_op jit(solution)/shard_map/all_to_all | solution.py:30
  35.9 1.6 copy.31
  37.5 5.1 %all-to-all-done.1 = f32[16,1,4096]{2,1,0:T(1,128)S(1)} async-done(((f32[16,1,4096]{2,1,0:T(1,128)}), f32[16,1,4096]{2,1,0:T(1,128)S(1)}, u32[]{:S(2)}, u32[]{:S(2)}) %all-to-all-start.1) | async-done | bytes 262176 | tf_op jit(solution)/shard_map/all_to_all | solution.py:30
  42.8 0.9 broadcast_in_dim.14
  43.7 5.3 %all-to-all-start.2 = ((f32[16,1,4096]{2,1,0:T(1,128)}), f32[16,1,4096]{2,1,0:T(1,128)S(1)}, u32[]{:S(2)}, u32[]{:S(2)}) async-start(f32[16,1,4096]{2,1,0:T(1,128)} %broadcast_in_dim.14), calls=%async_computation.2 | async-start | bytes 524288 | tf_op jit(solution)/shard_map/all_to_all | solution.py:32
  49.0 2.1 %fusion.5 = f32[1024,512]{0,1:T(8,128)S(1)} fusion(f32[64,8,8,128]{3,2,1,0:T(8,128)} %bitcast.273, f32[1024]{0:T(1024)S(1)} %broadcast_bitcast_fusion), kind=kLoop, calls=%fused_computation.8 | loop fusion | flops 524288 | bytes 4198400 | tf_op jit(solution)/shard_map/fjk,fkc->fjc/dot_general | solution.py:36
  51.1 1.9 %copy.59 = f32[1024,512]{1,0:T(8,128)} copy(f32[1024,512]{0,1:T(8,128)S(1)} %fusion.5) | data formatting | bytes 4194304 | tf_op jit(solution)/shard_map/fjk,fkc->fjc/dot_general | solution.py:36
  53.0 2.9 %all-to-all-done.2 = f32[16,1,4096]{2,1,0:T(1,128)S(1)} async-done(((f32[16,1,4096]{2,1,0:T(1,128)}), f32[16,1,4096]{2,1,0:T(1,128)S(1)}, u32[]{:S(2)}, u32[]{:S(2)}) %all-to-all-start.2) | async-done | bytes 262176 | tf_op jit(solution)/shard_map/all_to_all | solution.py:32
  55.8 0.6 reduce.2
  56.5 0.7 reshape.973.cov_ref
  57.2 22.3 %shard_map.37.start_ref = f32[1,80,512]{2,1,0:T(8,128)} custom-call(f32[1,256,256]{2,1,0:T(8,128)} %reshape.973.cov_ref, f32[1,80,512]{2,1,0:T(8,128)} %maximum_maximum_fusion.start_ref), custom_call_target="tpu_custom_call" | custom-call | tf_op jit(solution)/shard_map/pallas_call | solution.py:160
  79.5 1.0 multiply_bitcast_fusion.1
  80.5 2.7 %convolution_bitcast_fusion.1 = f32[8,128,80,1,1]{1,2,0,4,3:T(8,128)S(1)} fusion(f32[8,128,512]{2,1,0:T(8,128)} %bitcast.275, f32[1,80,512]{2,1,0:T(8,128)} %shard_map.37.start_ref, f32[80]{0:T(128)S(1)} %compare_select_fusion), kind=kOutput, calls=%fused_computation.27 | convolution fusion | flops 251699200 | bytes 2588992 | tf_op jit(solution)/shard_map/fjk,fkc->fjc/dot_general | solution.py:36
  83.3 1.0 fusion.158
  84.3 1.4 fusion.34
  85.8 4.2 %collective-permute-start.2 = (f32[1,2,7,128]{3,2,1,0:T(8,128)S(1)}, f32[1,2,7,128]{3,2,1,0:T(8,128)S(1)}, u32[]{:S(2)}, u32[]{:S(2)}) collective-permute-start(f32[1,2,7,128]{3,2,1,0:T(8,128)S(1)} %slice.229), channel_id=1, source_target_pairs={{1,0},{2,1},{3,2},{4,3},{5,4},{6,5},{7,6},{8,7},{9,8},{10,9},{11,1... | collective-permute-start | bytes 21512 | tf_op jit(solution)/shard_map/ppermute | solution.py:24
  90.0 1.4 collective-permute-done.2
  91.3 2.3 %collective-permute-start.1 = (f32[1,2,7,128]{3,2,1,0:T(8,128)S(1)}, f32[1,2,7,128]{3,2,1,0:T(8,128)S(1)}, u32[]{:S(2)}, u32[]{:S(2)}) collective-permute-start(f32[1,2,7,128]{3,2,1,0:T(8,128)S(1)} %get-tuple-element.23), channel_id=1, source_target_pairs={{0,1},{1,2},{2,3},{3,4},{4,5},{5,6},{6,7},{7,8},{8,9},{9,10},{10,1... | collective-permute-start | bytes 21512 | tf_op jit(solution)/shard_map/ppermute | solution.py:24
  93.7 5.6 %collective-permute-done.1 = f32[1,2,7,128]{3,2,1,0:T(8,128)S(1)} collective-permute-done((f32[1,2,7,128]{3,2,1,0:T(8,128)S(1)}, f32[1,2,7,128]{3,2,1,0:T(8,128)S(1)}, u32[]{:S(2)}, u32[]{:S(2)}) %collective-permute-start.1) | collective-permute-done | bytes 7200 | tf_op jit(solution)/shard_map/ppermute | solution.py:24
  99.2 0.9 fusion.31
  100.4 0.2 broadcast_multiply_fusion
  100.7 0.2 copy.41
  100.9 2.1 %fusion.25 = f32[1,512,512]{2,1,0:T(8,128)S(1)} fusion(f32[64,8,8,128]{3,2,1,0:T(8,128)S(1)} %bitcast.277), kind=kOutput, calls=%fused_computation.23 | convolution fusion | flops 1610612736 | bytes 3145728 | tf_op jit(solution)/shard_map/fik,fjk->fij/dot_general | solution.py:36
  103.1 1.0 all_to_all.61
  104.1 4.5 %all-to-all-start.3 = ((f32[16,1,4096]{2,1,0:T(1,128)}), f32[16,1,4096]{2,1,0:T(1,128)S(1)}, u32[]{:S(2)}, u32[]{:S(2)}) async-start(f32[16,1,4096]{2,1,0:T(1,128)} %all_to_all.61), calls=%async_computation.3 | async-start | bytes 524288 | tf_op jit(solution)/shard_map/all_to_all | solution.py:30
  108.6 1.6 copy.44
  110.1 5.2 %all-to-all-done.3 = f32[16,1,4096]{2,1,0:T(1,128)S(1)} async-done(((f32[16,1,4096]{2,1,0:T(1,128)}), f32[16,1,4096]{2,1,0:T(1,128)S(1)}, u32[]{:S(2)}, u32[]{:S(2)}) %all-to-all-start.3) | async-done | bytes 262176 | tf_op jit(solution)/shard_map/all_to_all | solution.py:30
  115.6 0.9 broadcast_in_dim.17
  116.5 5.3 %all-to-all-start.4 = ((f32[16,1,4096]{2,1,0:T(1,128)}), f32[16,1,4096]{2,1,0:T(1,128)S(1)}, u32[]{:S(2)}, u32[]{:S(2)}) async-start(f32[16,1,4096]{2,1,0:T(1,128)} %broadcast_in_dim.17), calls=%async_computation.4 | async-start | bytes 524288 | tf_op jit(solution)/shard_map/all_to_all | solution.py:32
  121.8 2.1 %fusion.1 = f32[1024,512]{0,1:T(8,128)S(1)} fusion(f32[64,8,8,128]{3,2,1,0:T(8,128)} %bitcast.272, f32[1024]{0:T(1024)S(1)} %broadcast_bitcast_fusion), kind=kLoop, calls=%fused_computation.3 | loop fusion | flops 524288 | bytes 4198400 | tf_op jit(solution)/shard_map/fjk,fkc->fjc/dot_general | solution.py:36
  123.9 1.9 %copy.60 = f32[1024,512]{1,0:T(8,128)} copy(f32[1024,512]{0,1:T(8,128)S(1)} %fusion.1) | data formatting | bytes 4194304 | tf_op jit(solution)/shard_map/fjk,fkc->fjc/dot_general | solution.py:36
  125.8 2.9 %all-to-all-done.4 = f32[16,1,4096]{2,1,0:T(1,128)S(1)} async-done(((f32[16,1,4096]{2,1,0:T(1,128)}), f32[16,1,4096]{2,1,0:T(1,128)S(1)}, u32[]{:S(2)}, u32[]{:S(2)}) %all-to-all-start.4) | async-done | bytes 262176 | tf_op jit(solution)/shard_map/all_to_all | solution.py:32
  128.6 0.6 reduce.3
  129.2 0.7 reshape.976.cov_ref
  130.0 22.3 %shard_map.38 = f32[1,80,512]{2,1,0:T(8,128)} custom-call(f32[1,256,256]{2,1,0:T(8,128)} %reshape.976.cov_ref, f32[1,80,512]{2,1,0:T(8,128)} %shard_map.37.start_ref), custom_call_target="tpu_custom_call" | custom-call | tf_op jit(solution)/shard_map/pallas_call | solution.py:160
  152.3 1.0 multiply_bitcast_fusion
  153.3 2.7 %convolution_bitcast_fusion = f32[8,128,80,1,1]{1,2,0,4,3:T(8,128)S(1)} fusion(f32[8,128,512]{2,1,0:T(8,128)} %bitcast.274, f32[1,80,512]{2,1,0:T(8,128)} %shard_map.38, f32[80]{0:T(128)S(1)} %compare_select_fusion), kind=kOutput, calls=%fused_computation.26 | convolution fusion | flops 251699200 | bytes 2588992 | tf_op jit(solution)/shard_map/fjk,fkc->fjc/dot_general | solution.py:36
  156.1 1.0 fusion.159
  157.1 1.4 fusion.39
  158.6 2.3 %collective-permute-start.3 = (f32[1,2,7,128]{3,2,1,0:T(8,128)S(1)}, f32[1,2,7,128]{3,2,1,0:T(8,128)S(1)}, u32[]{:S(2)}, u32[]{:S(2)}) collective-permute-start(f32[1,2,7,128]{3,2,1,0:T(8,128)S(1)} %slice.251), channel_id=1, source_target_pairs={{0,1},{1,2},{2,3},{3,4},{4,5},{5,6},{6,7},{7,8},{8,9},{9,10},{10,1... | collective-permute-start | bytes 21512 | tf_op jit(solution)/shard_map/ppermute | solution.py:24
  160.9 5.3 %collective-permute-done.3 = f32[1,2,7,128]{3,2,1,0:T(8,128)S(1)} collective-permute-done((f32[1,2,7,128]{3,2,1,0:T(8,128)S(1)}, f32[1,2,7,128]{3,2,1,0:T(8,128)S(1)}, u32[]{:S(2)}, u32[]{:S(2)}) %collective-permute-start.3) | collective-permute-done | bytes 7200 | tf_op jit(solution)/shard_map/ppermute | solution.py:24
  166.4 0.2 reshape.998
  166.6 7.7 %all_to_all.68 = f32[8,1,256]{2,1,0:T(1,128)S(1)} all-to-all(f32[8,1,256]{2,1,0:T(1,128)S(1)} %reshape.998), channel_id=1, replica_groups=mesh['freq'=8,'space'=16] {'freq'}, dimensions={0} | all-to-all | bytes 16384 | tf_op jit(solution)/shard_map/all_to_all | solution.py:240
  174.3 0.7 reduce.5
  174.9 0.2 reshape.999
  175.3 1.2 fusion.82
  176.5 2.2 %fusion = f32[8,16,2048]{2,1,0:T(8,128)} fusion(f32[8,16,2048]{2,1,0:T(8,128)S(1)} %fusion.82, f32[8,2,8,16]{3,0,2,1:T(8,128)S(1)} %bitcast.283, s32[8]{0:T(128)S(1)} %copy-done.1), kind=kOutput, calls=%fused_computation.1 | convolution fusion | flops 25919488 | bytes 2130432 | tf_op jit(solution)/shard_map/fxy,tf->xyt/dot_general | solution.py:36
  (50 shorter events, 2.1 us)
Async XLA Ops:
  0.0 1.2 copy-start
  3.9 9.6 %all-to-all-start = ((f32[8,1,256]{2,1,0:T(1,128)}), f32[8,1,256]{2,1,0:T(1,128)S(1)}, u32[]{:S(2)}, u32[]{:S(2)}) async-start(f32[8,1,256]{2,1,0:T(1,128)} %reshape.996), calls=%async_computation | async-start | bytes 16384 | tf_op jit(solution)/shard_map/all_to_all | solution.py:186
  14.9 7.2 %collective-permute-start = (f32[1,2,7,128]{3,2,1,0:T(8,128)S(1)}, f32[1,2,7,128]{3,2,1,0:T(8,128)S(1)}, u32[]{:S(2)}, u32[]{:S(2)}) collective-permute-start(f32[1,2,7,128]{3,2,1,0:T(8,128)S(1)} %bitcast.286), channel_id=1, source_target_pairs={{1,0},{2,1},{3,2},{4,3},{5,4},{6,5},{7,6},{8,7},{9,8},{10,9},{11,1... | collective-permute-start | bytes 21512 | tf_op jit(solution)/shard_map/ppermute | solution.py:24
  26.9 15.7 %all-to-all-start.1 = ((f32[16,1,4096]{2,1,0:T(1,128)}), f32[16,1,4096]{2,1,0:T(1,128)S(1)}, u32[]{:S(2)}, u32[]{:S(2)}) async-start(f32[16,1,4096]{2,1,0:T(1,128)} %all_to_all.60), calls=%async_computation.1 | async-start | bytes 524288 | tf_op jit(solution)/shard_map/all_to_all | solution.py:30
  43.7 12.1 %all-to-all-start.2 = ((f32[16,1,4096]{2,1,0:T(1,128)}), f32[16,1,4096]{2,1,0:T(1,128)S(1)}, u32[]{:S(2)}, u32[]{:S(2)}) async-start(f32[16,1,4096]{2,1,0:T(1,128)} %broadcast_in_dim.14), calls=%async_computation.2 | async-start | bytes 524288 | tf_op jit(solution)/shard_map/all_to_all | solution.py:32
  85.8 5.5 %collective-permute-start.2 = (f32[1,2,7,128]{3,2,1,0:T(8,128)S(1)}, f32[1,2,7,128]{3,2,1,0:T(8,128)S(1)}, u32[]{:S(2)}, u32[]{:S(2)}) collective-permute-start(f32[1,2,7,128]{3,2,1,0:T(8,128)S(1)} %slice.229), channel_id=1, source_target_pairs={{1,0},{2,1},{3,2},{4,3},{5,4},{6,5},{7,6},{8,7},{9,8},{10,9},{11,1... | collective-permute-start | bytes 21512 | tf_op jit(solution)/shard_map/ppermute | solution.py:24
  91.3 7.9 %collective-permute-start.1 = (f32[1,2,7,128]{3,2,1,0:T(8,128)S(1)}, f32[1,2,7,128]{3,2,1,0:T(8,128)S(1)}, u32[]{:S(2)}, u32[]{:S(2)}) collective-permute-start(f32[1,2,7,128]{3,2,1,0:T(8,128)S(1)} %get-tuple-element.23), channel_id=1, source_target_pairs={{0,1},{1,2},{2,3},{3,4},{4,5},{5,6},{6,7},{7,8},{8,9},{9,10},{10,1... | collective-permute-start | bytes 21512 | tf_op jit(solution)/shard_map/ppermute | solution.py:24
  104.1 11.3 %all-to-all-start.3 = ((f32[16,1,4096]{2,1,0:T(1,128)}), f32[16,1,4096]{2,1,0:T(1,128)S(1)}, u32[]{:S(2)}, u32[]{:S(2)}) async-start(f32[16,1,4096]{2,1,0:T(1,128)} %all_to_all.61), calls=%async_computation.3 | async-start | bytes 524288 | tf_op jit(solution)/shard_map/all_to_all | solution.py:30
  116.5 12.1 %all-to-all-start.4 = ((f32[16,1,4096]{2,1,0:T(1,128)}), f32[16,1,4096]{2,1,0:T(1,128)S(1)}, u32[]{:S(2)}, u32[]{:S(2)}) async-start(f32[16,1,4096]{2,1,0:T(1,128)} %broadcast_in_dim.17), calls=%async_computation.4 | async-start | bytes 524288 | tf_op jit(solution)/shard_map/all_to_all | solution.py:32
  157.1 18.2 %copy-start.1 = (s32[8]{0:T(128)S(1)}, s32[8]{0:T(128)}, u32[]{:S(2)}) copy-start(s32[8]{0:T(128)} %param.4) | copy-start | bytes 100
  158.6 7.7 %collective-permute-start.3 = (f32[1,2,7,128]{3,2,1,0:T(8,128)S(1)}, f32[1,2,7,128]{3,2,1,0:T(8,128)S(1)}, u32[]{:S(2)}, u32[]{:S(2)}) collective-permute-start(f32[1,2,7,128]{3,2,1,0:T(8,128)S(1)} %slice.251), channel_id=1, source_target_pairs={{0,1},{1,2},{2,3},{3,4},{4,5},{5,6},{6,7},{7,8},{8,9},{9,10},{10,1... | collective-permute-start | bytes 21512 | tf_op jit(solution)/shard_map/ppermute | solution.py:24

commit v7 on v5

--- a/solution.py
+++ b/solution.py
@@ -207,7 +207,7 @@
     rim_rows = shifted(slices[:, :, : LX - 1, :], "space", -1)
     for cadzow_step in range(CADZOW):
         extended = jnp.concatenate([slices, rim_rows], axis=2)
-        lagged = product("fcpz,zby->fcbpy", extended, lag_shift)
+        lagged = product("fcpz,zby->fcbpy", extended, lag_shift, lax.Precision.HIGH)
         matrix = jnp.stack(
             [lagged[:, :, :, lag_x : lag_x + strip_width, :] for lag_x in range(LX)], axis=2
         )

time: 182 us -> 181 us (level)
  no operation moved by 1% of the time
where the time goes in v7:
time: 181 us; the launch traced here: 180 us
  Pallas kernels  44.6 us (25%)
  starting transfers between devices  43 us (24%)
  waiting for transfers between devices  32.6 us (18%)
  matrix products  23.1 us (13%)
  local copies, waits for them, and re-layouts  16.5 us (9%)
  other arithmetic  12.4 us (7%)
  blocking collectives  7.67 us (4%)
    pallas_call x2, Pallas kernels, power_steps(): pl.pallas_call(power_kernel, out_shape=jax.ShapeDtypeStruct(subspace.shap...  44.6 us
    dot_general x13, matrix products, product(): jnp.einsum(form, left, right, precision=precision, preferred_element_type...  23.1 us
    ppermute x4, starting transfers between devices, shifted(): return lax.ppermute(x, axis, pairs)  14.6 us
    ppermute x4, waiting for transfers between devices, shifted(): return lax.ppermute(x, axis, pairs)  13.6 us
    all_to_all x2, starting transfers between devices, all_sum(): mine = lax.all_to_all(chunks, axis, 0, 0, tiled=True).sum(axis=0)  13.4 us
    all_to_all x2, starting transfers between devices, all_sum(): return lax.all_to_all(copies, axis, 0, 0, tiled=True).reshape(x.shape)  10.7 us
    all_to_all x2, waiting for transfers between devices, all_sum(): mine = lax.all_to_all(chunks, axis, 0, 0, tiled=True).sum(axis=0)  10.4 us
    all_to_all x1, blocking collectives, on_device(): lax.all_to_all(slices, 'freq', split_axis=3, concat_axis=0, tiled=True)  7.67 us
  transfers between devices with their start and end apart: 9, of which 9 were waited for; matrix products, arithmetic and copies ran while one was open for 7% of the time, Pallas kernels for 0%

profile of v7, /device:TPU:8, one launch (start us, length us, event | category | flops | bytes accessed | tf_op | source)
XLA Modules:
  0.0 180.3 jit_solution(13211130211786869137)
XLA Ops:
  0.0 1.1 cosine_multiply_fusion
  1.2 3.8 %convolution_bitcast_fusion.2 = f32[8,2,8,16]{3,0,2,1:T(8,128)S(1)} fusion(f32[8,16,2048]{2,1,0:T(8,128)S(1)} %copy-done, f32[2048,1,8]{0,2,1:T(8,128)S(1)} %get-tuple-element.28, f32[2048,1,8]{0,2,1:T(8,128)S(1)} %get-tuple-element.27), kind=kOutput, calls=%fused_computation.28 | convolution fusion | flops 50364416 | bytes 1187840 | tf_op jit(solution)/shard_map/xyt,tcf->fcxy/dot_general | solution.py:36
  5.0 0.7 reshape.996
  5.7 4.3 %all-to-all-start = ((f32[8,1,256]{2,1,0:T(1,128)}), f32[8,1,256]{2,1,0:T(1,128)S(1)}, u32[]{:S(2)}, u32[]{:S(2)}) async-start(f32[8,1,256]{2,1,0:T(1,128)} %reshape.996), calls=%async_computation | async-start | bytes 16384 | tf_op jit(solution)/shard_map/all_to_all | solution.py:186
  10.0 0.8 slice_bitcast_fusion.16
  10.8 0.8 fusion.156
  11.7 0.7 maximum_maximum_fusion.start_ref
  12.4 3.0 %all-to-all-done = f32[8,1,256]{2,1,0:T(1,128)S(1)} async-done(((f32[8,1,256]{2,1,0:T(1,128)}), f32[8,1,256]{2,1,0:T(1,128)S(1)}, u32[]{:S(2)}, u32[]{:S(2)}) %all-to-all-start) | async-done | bytes 8224 | tf_op jit(solution)/shard_map/all_to_all | solution.py:186
  15.3 0.5 broadcast.1219
  15.9 0.7 reduce.4
  16.7 5.8 %collective-permute-start = (f32[1,2,7,128]{3,2,1,0:T(8,128)S(1)}, f32[1,2,7,128]{3,2,1,0:T(8,128)S(1)}, u32[]{:S(2)}, u32[]{:S(2)}) collective-permute-start(f32[1,2,7,128]{3,2,1,0:T(8,128)S(1)} %bitcast.286), channel_id=1, source_target_pairs={{1,0},{2,1},{3,2},{4,3},{5,4},{6,5},{7,6},{8,7},{9,8},{10,9},{11,1... | collective-permute-start | bytes 21512 | tf_op jit(solution)/shard_map/ppermute | solution.py:24
  22.6 1.3 collective-permute-done
  23.9 0.7 fusion.28
  25.0 0.2 broadcast_multiply_fusion.1
  25.2 0.2 copy.28
  25.5 2.1 %fusion.22 = f32[1,512,512]{2,1,0:T(8,128)S(1)} fusion(f32[64,8,8,128]{3,2,1,0:T(8,128)S(1)} %bitcast.276), kind=kOutput, calls=%fused_computation.22 | convolution fusion | flops 1610612736 | bytes 3145728 | tf_op jit(solution)/shard_map/fik,fjk->fij/dot_general | solution.py:36
  27.6 1.0 all_to_all.60
  28.6 8.9 %all-to-all-start.1 = ((f32[16,1,4096]{2,1,0:T(1,128)}), f32[16,1,4096]{2,1,0:T(1,128)S(1)}, u32[]{:S(2)}, u32[]{:S(2)}) async-start(f32[16,1,4096]{2,1,0:T(1,128)} %all_to_all.60), calls=%async_computation.1 | async-start | bytes 524288 | tf_op jit(solution)/shard_map/all_to_all | solution.py:30
  37.6 1.6 copy.31
  39.2 5.1 %all-to-all-done.1 = f32[16,1,4096]{2,1,0:T(1,128)S(1)} async-done(((f32[16,1,4096]{2,1,0:T(1,128)}), f32[16,1,4096]{2,1,0:T(1,128)S(1)}, u32[]{:S(2)}, u32[]{:S(2)}) %all-to-all-start.1) | async-done | bytes 262176 | tf_op jit(solution)/shard_map/all_to_all | solution.py:30
  44.5 0.9 broadcast_in_dim.14
  45.4 5.3 %all-to-all-start.2 = ((f32[16,1,4096]{2,1,0:T(1,128)}), f32[16,1,4096]{2,1,0:T(1,128)S(1)}, u32[]{:S(2)}, u32[]{:S(2)}) async-start(f32[16,1,4096]{2,1,0:T(1,128)} %broadcast_in_dim.14), calls=%async_computation.2 | async-start | bytes 524288 | tf_op jit(solution)/shard_map/all_to_all | solution.py:32
  50.7 2.1 %fusion.5 = f32[1024,512]{0,1:T(8,128)S(1)} fusion(f32[64,8,8,128]{3,2,1,0:T(8,128)} %bitcast.273, f32[1024]{0:T(1024)S(1)} %broadcast_bitcast_fusion), kind=kLoop, calls=%fused_computation.8 | loop fusion | flops 524288 | bytes 4198400 | tf_op jit(solution)/shard_map/fjk,fkc->fjc/dot_general | solution.py:36
  52.8 1.9 %copy.59 = f32[1024,512]{1,0:T(8,128)} copy(f32[1024,512]{0,1:T(8,128)S(1)} %fusion.5) | data formatting | bytes 4194304 | tf_op jit(solution)/shard_map/fjk,fkc->fjc/dot_general | solution.py:36
  54.7 2.9 %all-to-all-done.2 = f32[16,1,4096]{2,1,0:T(1,128)S(1)} async-done(((f32[16,1,4096]{2,1,0:T(1,128)}), f32[16,1,4096]{2,1,0:T(1,128)S(1)}, u32[]{:S(2)}, u32[]{:S(2)}) %all-to-all-start.2) | async-done | bytes 262176 | tf_op jit(solution)/shard_map/all_to_all | solution.py:32
  57.5 0.6 reduce.2
  58.1 0.7 reshape.973.cov_ref
  58.9 22.3 %shard_map.37.start_ref = f32[1,80,512]{2,1,0:T(8,128)} custom-call(f32[1,256,256]{2,1,0:T(8,128)} %reshape.973.cov_ref, f32[1,80,512]{2,1,0:T(8,128)} %maximum_maximum_fusion.start_ref), custom_call_target="tpu_custom_call" | custom-call | tf_op jit(solution)/shard_map/pallas_call | solution.py:160
  81.2 1.0 multiply_bitcast_fusion.1
  82.2 2.7 %convolution_bitcast_fusion.1 = f32[8,128,80,1,1]{1,2,0,4,3:T(8,128)S(1)} fusion(f32[8,128,512]{2,1,0:T(8,128)} %bitcast.275, f32[1,80,512]{2,1,0:T(8,128)} %shard_map.37.start_ref, f32[80]{0:T(128)S(1)} %compare_select_fusion), kind=kOutput, calls=%fused_computation.27 | convolution fusion | flops 251699200 | bytes 2588992 | tf_op jit(solution)/shard_map/fjk,fkc->fjc/dot_general | solution.py:36
  85.0 1.0 fusion.158
  86.0 1.4 fusion.34
  87.5 4.2 %collective-permute-start.2 = (f32[1,2,7,128]{3,2,1,0:T(8,128)S(1)}, f32[1,2,7,128]{3,2,1,0:T(8,128)S(1)}, u32[]{:S(2)}, u32[]{:S(2)}) collective-permute-start(f32[1,2,7,128]{3,2,1,0:T(8,128)S(1)} %slice.229), channel_id=1, source_target_pairs={{1,0},{2,1},{3,2},{4,3},{5,4},{6,5},{7,6},{8,7},{9,8},{10,9},{11,1... | collective-permute-start | bytes 21512 | tf_op jit(solution)/shard_map/ppermute | solution.py:24
  91.6 1.4 collective-permute-done.2
  93.0 2.3 %collective-permute-start.1 = (f32[1,2,7,128]{3,2,1,0:T(8,128)S(1)}, f32[1,2,7,128]{3,2,1,0:T(8,128)S(1)}, u32[]{:S(2)}, u32[]{:S(2)}) collective-permute-start(f32[1,2,7,128]{3,2,1,0:T(8,128)S(1)} %get-tuple-element.23), channel_id=1, source_target_pairs={{0,1},{1,2},{2,3},{3,4},{4,5},{5,6},{6,7},{7,8},{8,9},{9,10},{10,1... | collective-permute-start | bytes 21512 | tf_op jit(solution)/shard_map/ppermute | solution.py:24
  95.3 5.6 %collective-permute-done.1 = f32[1,2,7,128]{3,2,1,0:T(8,128)S(1)} collective-permute-done((f32[1,2,7,128]{3,2,1,0:T(8,128)S(1)}, f32[1,2,7,128]{3,2,1,0:T(8,128)S(1)}, u32[]{:S(2)}, u32[]{:S(2)}) %collective-permute-start.1) | collective-permute-done | bytes 7200 | tf_op jit(solution)/shard_map/ppermute | solution.py:24
  100.9 0.8 fusion.31
  102.0 0.2 broadcast_multiply_fusion
  102.2 0.2 copy.41
  102.5 2.1 %fusion.25 = f32[1,512,512]{2,1,0:T(8,128)S(1)} fusion(f32[64,8,8,128]{3,2,1,0:T(8,128)S(1)} %bitcast.277), kind=kOutput, calls=%fused_computation.23 | convolution fusion | flops 1610612736 | bytes 3145728 | tf_op jit(solution)/shard_map/fik,fjk->fij/dot_general | solution.py:36
  104.6 1.0 all_to_all.61
  105.6 4.5 %all-to-all-start.3 = ((f32[16,1,4096]{2,1,0:T(1,128)}), f32[16,1,4096]{2,1,0:T(1,128)S(1)}, u32[]{:S(2)}, u32[]{:S(2)}) async-start(f32[16,1,4096]{2,1,0:T(1,128)} %all_to_all.61), calls=%async_computation.3 | async-start | bytes 524288 | tf_op jit(solution)/shard_map/all_to_all | solution.py:30
  110.1 1.6 copy.44
  111.7 5.2 %all-to-all-done.3 = f32[16,1,4096]{2,1,0:T(1,128)S(1)} async-done(((f32[16,1,4096]{2,1,0:T(1,128)}), f32[16,1,4096]{2,1,0:T(1,128)S(1)}, u32[]{:S(2)}, u32[]{:S(2)}) %all-to-all-start.3) | async-done | bytes 262176 | tf_op jit(solution)/shard_map/all_to_all | solution.py:30
  117.1 0.9 broadcast_in_dim.17
  118.0 5.3 %all-to-all-start.4 = ((f32[16,1,4096]{2,1,0:T(1,128)}), f32[16,1,4096]{2,1,0:T(1,128)S(1)}, u32[]{:S(2)}, u32[]{:S(2)}) async-start(f32[16,1,4096]{2,1,0:T(1,128)} %broadcast_in_dim.17), calls=%async_computation.4 | async-start | bytes 524288 | tf_op jit(solution)/shard_map/all_to_all | solution.py:32
  123.4 2.1 %fusion.1 = f32[1024,512]{0,1:T(8,128)S(1)} fusion(f32[64,8,8,128]{3,2,1,0:T(8,128)} %bitcast.272, f32[1024]{0:T(1024)S(1)} %broadcast_bitcast_fusion), kind=kLoop, calls=%fused_computation.3 | loop fusion | flops 524288 | bytes 4198400 | tf_op jit(solution)/shard_map/fjk,fkc->fjc/dot_general | solution.py:36
  125.4 1.9 %copy.60 = f32[1024,512]{1,0:T(8,128)} copy(f32[1024,512]{0,1:T(8,128)S(1)} %fusion.1) | data formatting | bytes 4194304 | tf_op jit(solution)/shard_map/fjk,fkc->fjc/dot_general | solution.py:36
  127.3 2.9 %all-to-all-done.4 = f32[16,1,4096]{2,1,0:T(1,128)S(1)} async-done(((f32[16,1,4096]{2,1,0:T(1,128)}), f32[16,1,4096]{2,1,0:T(1,128)S(1)}, u32[]{:S(2)}, u32[]{:S(2)}) %all-to-all-start.4) | async-done | bytes 262176 | tf_op jit(solution)/shard_map/all_to_all | solution.py:32
  130.2 0.6 reduce.3
  130.8 0.7 reshape.976.cov_ref
  131.5 22.3 %shard_map.38 = f32[1,80,512]{2,1,0:T(8,128)} custom-call(f32[1,256,256]{2,1,0:T(8,128)} %reshape.976.cov_ref, f32[1,80,512]{2,1,0:T(8,128)} %shard_map.37.start_ref), custom_call_target="tpu_custom_call" | custom-call | tf_op jit(solution)/shard_map/pallas_call | solution.py:160
  153.8 1.0 multiply_bitcast_fusion
  154.8 2.7 %convolution_bitcast_fusion = f32[8,128,80,1,1]{1,2,0,4,3:T(8,128)S(1)} fusion(f32[8,128,512]{2,1,0:T(8,128)} %bitcast.274, f32[1,80,512]{2,1,0:T(8,128)} %shard_map.38, f32[80]{0:T(128)S(1)} %compare_select_fusion), kind=kOutput, calls=%fused_computation.26 | convolution fusion | flops 251699200 | bytes 2588992 | tf_op jit(solution)/shard_map/fjk,fkc->fjc/dot_general | solution.py:36
  157.7 1.0 fusion.159
  158.6 1.4 fusion.39
  160.1 2.3 %collective-permute-start.3 = (f32[1,2,7,128]{3,2,1,0:T(8,128)S(1)}, f32[1,2,7,128]{3,2,1,0:T(8,128)S(1)}, u32[]{:S(2)}, u32[]{:S(2)}) collective-permute-start(f32[1,2,7,128]{3,2,1,0:T(8,128)S(1)} %slice.251), channel_id=1, source_target_pairs={{0,1},{1,2},{2,3},{3,4},{4,5},{5,6},{6,7},{7,8},{8,9},{9,10},{10,1... | collective-permute-start | bytes 21512 | tf_op jit(solution)/shard_map/ppermute | solution.py:24
  162.5 5.3 %collective-permute-done.3 = f32[1,2,7,128]{3,2,1,0:T(8,128)S(1)} collective-permute-done((f32[1,2,7,128]{3,2,1,0:T(8,128)S(1)}, f32[1,2,7,128]{3,2,1,0:T(8,128)S(1)}, u32[]{:S(2)}, u32[]{:S(2)}) %collective-permute-start.3) | collective-permute-done | bytes 7200 | tf_op jit(solution)/shard_map/ppermute | solution.py:24
  167.9 0.2 reshape.998
  168.2 7.7 %all_to_all.68 = f32[8,1,256]{2,1,0:T(1,128)S(1)} all-to-all(f32[8,1,256]{2,1,0:T(1,128)S(1)} %reshape.998), channel_id=1, replica_groups=mesh['freq'=8,'space'=16] {'freq'}, dimensions={0} | all-to-all | bytes 16384 | tf_op jit(solution)/shard_map/all_to_all | solution.py:240
  175.8 0.7 reduce.5
  176.5 0.2 reshape.999
  176.9 1.2 fusion.82
  178.1 2.2 %fusion = f32[8,16,2048]{2,1,0:T(8,128)} fusion(f32[8,16,2048]{2,1,0:T(8,128)S(1)} %fusion.82, f32[8,2,8,16]{3,0,2,1:T(8,128)S(1)} %bitcast.283, s32[8]{0:T(128)S(1)} %copy-done.1), kind=kOutput, calls=%fused_computation.1 | convolution fusion | flops 25919488 | bytes 2130432 | tf_op jit(solution)/shard_map/fxy,tf->xyt/dot_general | solution.py:36
  (50 shorter events, 2.1 us)
Async XLA Ops:
  0.0 1.2 copy-start
  5.7 9.6 %all-to-all-start = ((f32[8,1,256]{2,1,0:T(1,128)}), f32[8,1,256]{2,1,0:T(1,128)S(1)}, u32[]{:S(2)}, u32[]{:S(2)}) async-start(f32[8,1,256]{2,1,0:T(1,128)} %reshape.996), calls=%async_computation | async-start | bytes 16384 | tf_op jit(solution)/shard_map/all_to_all | solution.py:186
  16.7 7.2 %collective-permute-start = (f32[1,2,7,128]{3,2,1,0:T(8,128)S(1)}, f32[1,2,7,128]{3,2,1,0:T(8,128)S(1)}, u32[]{:S(2)}, u32[]{:S(2)}) collective-permute-start(f32[1,2,7,128]{3,2,1,0:T(8,128)S(1)} %bitcast.286), channel_id=1, source_target_pairs={{1,0},{2,1},{3,2},{4,3},{5,4},{6,5},{7,6},{8,7},{9,8},{10,9},{11,1... | collective-permute-start | bytes 21512 | tf_op jit(solution)/shard_map/ppermute | solution.py:24
  28.6 15.7 %all-to-all-start.1 = ((f32[16,1,4096]{2,1,0:T(1,128)}), f32[16,1,4096]{2,1,0:T(1,128)S(1)}, u32[]{:S(2)}, u32[]{:S(2)}) async-start(f32[16,1,4096]{2,1,0:T(1,128)} %all_to_all.60), calls=%async_computation.1 | async-start | bytes 524288 | tf_op jit(solution)/shard_map/all_to_all | solution.py:30
  45.4 12.1 %all-to-all-start.2 = ((f32[16,1,4096]{2,1,0:T(1,128)}), f32[16,1,4096]{2,1,0:T(1,128)S(1)}, u32[]{:S(2)}, u32[]{:S(2)}) async-start(f32[16,1,4096]{2,1,0:T(1,128)} %broadcast_in_dim.14), calls=%async_computation.2 | async-start | bytes 524288 | tf_op jit(solution)/shard_map/all_to_all | solution.py:32
  87.5 5.5 %collective-permute-start.2 = (f32[1,2,7,128]{3,2,1,0:T(8,128)S(1)}, f32[1,2,7,128]{3,2,1,0:T(8,128)S(1)}, u32[]{:S(2)}, u32[]{:S(2)}) collective-permute-start(f32[1,2,7,128]{3,2,1,0:T(8,128)S(1)} %slice.229), channel_id=1, source_target_pairs={{1,0},{2,1},{3,2},{4,3},{5,4},{6,5},{7,6},{8,7},{9,8},{10,9},{11,1... | collective-permute-start | bytes 21512 | tf_op jit(solution)/shard_map/ppermute | solution.py:24
  93.0 7.9 %collective-permute-start.1 = (f32[1,2,7,128]{3,2,1,0:T(8,128)S(1)}, f32[1,2,7,128]{3,2,1,0:T(8,128)S(1)}, u32[]{:S(2)}, u32[]{:S(2)}) collective-permute-start(f32[1,2,7,128]{3,2,1,0:T(8,128)S(1)} %get-tuple-element.23), channel_id=1, source_target_pairs={{0,1},{1,2},{2,3},{3,4},{4,5},{5,6},{6,7},{7,8},{8,9},{9,10},{10,1... | collective-permute-start | bytes 21512 | tf_op jit(solution)/shard_map/ppermute | solution.py:24
  105.6 11.3 %all-to-all-start.3 = ((f32[16,1,4096]{2,1,0:T(1,128)}), f32[16,1,4096]{2,1,0:T(1,128)S(1)}, u32[]{:S(2)}, u32[]{:S(2)}) async-start(f32[16,1,4096]{2,1,0:T(1,128)} %all_to_all.61), calls=%async_computation.3 | async-start | bytes 524288 | tf_op jit(solution)/shard_map/all_to_all | solution.py:30
  118.0 12.1 %all-to-all-start.4 = ((f32[16,1,4096]{2,1,0:T(1,128)}), f32[16,1,4096]{2,1,0:T(1,128)S(1)}, u32[]{:S(2)}, u32[]{:S(2)}) async-start(f32[16,1,4096]{2,1,0:T(1,128)} %broadcast_in_dim.17), calls=%async_computation.4 | async-start | bytes 524288 | tf_op jit(solution)/shard_map/all_to_all | solution.py:32
  158.6 18.2 %copy-start.1 = (s32[8]{0:T(128)S(1)}, s32[8]{0:T(128)}, u32[]{:S(2)}) copy-start(s32[8]{0:T(128)} %param.4) | copy-start | bytes 100
  160.1 7.7 %collective-permute-start.3 = (f32[1,2,7,128]{3,2,1,0:T(8,128)S(1)}, f32[1,2,7,128]{3,2,1,0:T(8,128)S(1)}, u32[]{:S(2)}, u32[]{:S(2)}) collective-permute-start(f32[1,2,7,128]{3,2,1,0:T(8,128)S(1)} %slice.251), channel_id=1, source_target_pairs={{0,1},{1,2},{2,3},{3,4},{4,5},{5,6},{6,7},{7,8},{8,9},{9,10},{10,1... | collective-permute-start | bytes 21512 | tf_op jit(solution)/shard_map/ppermute | solution.py:24

commit v8 on v5

--- a/solution.py
+++ b/solution.py
@@ -238,8 +238,8 @@
         slices = (full[:, :, :strip_width, :] + spill) / counts
     out_scale = math.sqrt(2.0 / kept_bins.shape[0])
     received = lax.all_to_all(slices, "freq", split_axis=3, concat_axis=0, tiled=True)
-    synth = product("fxy,tf->xyt", received[:, 0], cosines)
-    synth = synth - product("fxy,tf->xyt", received[:, 1], sines)
+    synth = product("fxy,tf->xyt", received[:, 0], cosines, lax.Precision.HIGH)
+    synth = synth - product("fxy,tf->xyt", received[:, 1], sines, lax.Precision.HIGH)
     return out_scale * synth
 
 

time: 182 us -> 181 us (level)
  transfers between devices with their start and end apart: 9 -> 9, of which waited for: 9 -> 9; matrix products, arithmetic and copies ran while one was open for 7% -> 8% of each run, Pallas kernels for 0% -> 0%
where the time goes in v8:
time: 181 us; the launch traced here: 180 us
  Pallas kernels  44.6 us (25%)
  starting transfers between devices  43 us (24%)
  waiting for transfers between devices  32.6 us (18%)
  matrix products  22.5 us (12%)
  local copies, waits for them, and re-layouts  16.5 us (9%)
  other arithmetic  12.4 us (7%)
  blocking collectives  7.67 us (4%)
    pallas_call x2, Pallas kernels, power_steps(): pl.pallas_call(power_kernel, out_shape=jax.ShapeDtypeStruct(subspace.shap...  44.6 us
    dot_general x13, matrix products, product(): jnp.einsum(form, left, right, precision=precision, preferred_element_type...  22.5 us
    ppermute x4, starting transfers between devices, shifted(): return lax.ppermute(x, axis, pairs)  14.6 us
    ppermute x4, waiting for transfers between devices, shifted(): return lax.ppermute(x, axis, pairs)  13.6 us
    all_to_all x2, starting transfers between devices, all_sum(): mine = lax.all_to_all(chunks, axis, 0, 0, tiled=True).sum(axis=0)  13.4 us
    all_to_all x2, starting transfers between devices, all_sum(): return lax.all_to_all(copies, axis, 0, 0, tiled=True).reshape(x.shape)  10.7 us
    all_to_all x2, waiting for transfers between devices, all_sum(): mine = lax.all_to_all(chunks, axis, 0, 0, tiled=True).sum(axis=0)  10.4 us
    all_to_all x1, blocking collectives, on_device(): lax.all_to_all(slices, 'freq', split_axis=3, concat_axis=0, tiled=True)  7.67 us
  transfers between devices with their start and end apart: 9, of which 9 were waited for; matrix products, arithmetic and copies ran while one was open for 8% of the time, Pallas kernels for 0%

profile of v8, /device:TPU:8, one launch (start us, length us, event | category | flops | bytes accessed | tf_op | source)
XLA Modules:
  0.0 179.7 jit_solution(15543351196884100650)
XLA Ops:
  0.0 1.1 cosine_multiply_fusion
  1.2 3.8 %convolution_bitcast_fusion.2 = f32[8,2,8,16]{3,0,2,1:T(8,128)S(1)} fusion(f32[8,16,2048]{2,1,0:T(8,128)S(1)} %copy-done, f32[2048,1,8]{0,2,1:T(8,128)S(1)} %get-tuple-element.28, f32[2048,1,8]{0,2,1:T(8,128)S(1)} %get-tuple-element.27), kind=kOutput, calls=%fused_computation.28 | convolution fusion | flops 50364416 | bytes 1187840 | tf_op jit(solution)/shard_map/xyt,tcf->fcxy/dot_general | solution.py:36
  5.0 0.7 reshape.996
  5.7 4.3 %all-to-all-start = ((f32[8,1,256]{2,1,0:T(1,128)}), f32[8,1,256]{2,1,0:T(1,128)S(1)}, u32[]{:S(2)}, u32[]{:S(2)}) async-start(f32[8,1,256]{2,1,0:T(1,128)} %reshape.996), calls=%async_computation | async-start | bytes 16384 | tf_op jit(solution)/shard_map/all_to_all | solution.py:186
  10.0 0.8 slice_bitcast_fusion.16
  10.8 0.8 fusion.156
  11.7 0.7 maximum_maximum_fusion.start_ref
  12.4 3.0 %all-to-all-done = f32[8,1,256]{2,1,0:T(1,128)S(1)} async-done(((f32[8,1,256]{2,1,0:T(1,128)}), f32[8,1,256]{2,1,0:T(1,128)S(1)}, u32[]{:S(2)}, u32[]{:S(2)}) %all-to-all-start) | async-done | bytes 8224 | tf_op jit(solution)/shard_map/all_to_all | solution.py:186
  15.3 0.5 broadcast.1219
  15.9 0.7 reduce.4
  16.7 5.8 %collective-permute-start = (f32[1,2,7,128]{3,2,1,0:T(8,128)S(1)}, f32[1,2,7,128]{3,2,1,0:T(8,128)S(1)}, u32[]{:S(2)}, u32[]{:S(2)}) collective-permute-start(f32[1,2,7,128]{3,2,1,0:T(8,128)S(1)} %bitcast.286), channel_id=1, source_target_pairs={{1,0},{2,1},{3,2},{4,3},{5,4},{6,5},{7,6},{8,7},{9,8},{10,9},{11,1... | collective-permute-start | bytes 21512 | tf_op jit(solution)/shard_map/ppermute | solution.py:24
  22.6 1.3 collective-permute-done
  23.9 0.9 fusion.28
  25.1 0.2 broadcast_multiply_fusion.1
  25.4 0.2 copy.28
  25.6 2.1 %fusion.22 = f32[1,512,512]{2,1,0:T(8,128)S(1)} fusion(f32[64,8,8,128]{3,2,1,0:T(8,128)S(1)} %bitcast.276), kind=kOutput, calls=%fused_computation.22 | convolution fusion | flops 1610612736 | bytes 3145728 | tf_op jit(solution)/shard_map/fik,fjk->fij/dot_general | solution.py:36
  27.8 1.0 all_to_all.60
  28.7 8.9 %all-to-all-start.1 = ((f32[16,1,4096]{2,1,0:T(1,128)}), f32[16,1,4096]{2,1,0:T(1,128)S(1)}, u32[]{:S(2)}, u32[]{:S(2)}) async-start(f32[16,1,4096]{2,1,0:T(1,128)} %all_to_all.60), calls=%async_computation.1 | async-start | bytes 524288 | tf_op jit(solution)/shard_map/all_to_all | solution.py:30
  37.7 1.6 copy.31
  39.3 5.1 %all-to-all-done.1 = f32[16,1,4096]{2,1,0:T(1,128)S(1)} async-done(((f32[16,1,4096]{2,1,0:T(1,128)}), f32[16,1,4096]{2,1,0:T(1,128)S(1)}, u32[]{:S(2)}, u32[]{:S(2)}) %all-to-all-start.1) | async-done | bytes 262176 | tf_op jit(solution)/shard_map/all_to_all | solution.py:30
  44.6 0.9 broadcast_in_dim.14
  45.5 5.3 %all-to-all-start.2 = ((f32[16,1,4096]{2,1,0:T(1,128)}), f32[16,1,4096]{2,1,0:T(1,128)S(1)}, u32[]{:S(2)}, u32[]{:S(2)}) async-start(f32[16,1,4096]{2,1,0:T(1,128)} %broadcast_in_dim.14), calls=%async_computation.2 | async-start | bytes 524288 | tf_op jit(solution)/shard_map/all_to_all | solution.py:32
  50.9 2.1 %fusion.5 = f32[1024,512]{0,1:T(8,128)S(1)} fusion(f32[64,8,8,128]{3,2,1,0:T(8,128)} %bitcast.273, f32[1024]{0:T(1024)S(1)} %broadcast_bitcast_fusion), kind=kLoop, calls=%fused_computation.8 | loop fusion | flops 524288 | bytes 4198400 | tf_op jit(solution)/shard_map/fjk,fkc->fjc/dot_general | solution.py:36
  52.9 1.9 %copy.59 = f32[1024,512]{1,0:T(8,128)} copy(f32[1024,512]{0,1:T(8,128)S(1)} %fusion.5) | data formatting | bytes 4194304 | tf_op jit(solution)/shard_map/fjk,fkc->fjc/dot_general | solution.py:36
  54.8 2.9 %all-to-all-done.2 = f32[16,1,4096]{2,1,0:T(1,128)S(1)} async-done(((f32[16,1,4096]{2,1,0:T(1,128)}), f32[16,1,4096]{2,1,0:T(1,128)S(1)}, u32[]{:S(2)}, u32[]{:S(2)}) %all-to-all-start.2) | async-done | bytes 262176 | tf_op jit(solution)/shard_map/all_to_all | solution.py:32
  57.7 0.6 reduce.2
  58.3 0.7 reshape.973.cov_ref
  59.0 22.3 %shard_map.37.start_ref = f32[1,80,512]{2,1,0:T(8,128)} custom-call(f32[1,256,256]{2,1,0:T(8,128)} %reshape.973.cov_ref, f32[1,80,512]{2,1,0:T(8,128)} %maximum_maximum_fusion.start_ref), custom_call_target="tpu_custom_call" | custom-call | tf_op jit(solution)/shard_map/pallas_call | solution.py:160
  81.3 1.0 multiply_bitcast_fusion.1
  82.3 2.7 %convolution_bitcast_fusion.1 = f32[8,128,80,1,1]{1,2,0,4,3:T(8,128)S(1)} fusion(f32[8,128,512]{2,1,0:T(8,128)} %bitcast.275, f32[1,80,512]{2,1,0:T(8,128)} %shard_map.37.start_ref, f32[80]{0:T(128)S(1)} %compare_select_fusion), kind=kOutput, calls=%fused_computation.27 | convolution fusion | flops 251699200 | bytes 2588992 | tf_op jit(solution)/shard_map/fjk,fkc->fjc/dot_general | solution.py:36
  85.2 1.0 fusion.158
  86.1 1.4 fusion.34
  87.6 4.2 %collective-permute-start.2 = (f32[1,2,7,128]{3,2,1,0:T(8,128)S(1)}, f32[1,2,7,128]{3,2,1,0:T(8,128)S(1)}, u32[]{:S(2)}, u32[]{:S(2)}) collective-permute-start(f32[1,2,7,128]{3,2,1,0:T(8,128)S(1)} %slice.229), channel_id=1, source_target_pairs={{1,0},{2,1},{3,2},{4,3},{5,4},{6,5},{7,6},{8,7},{9,8},{10,9},{11,1... | collective-permute-start | bytes 21512 | tf_op jit(solution)/shard_map/ppermute | solution.py:24
  91.8 1.4 collective-permute-done.2
  93.2 2.3 %collective-permute-start.1 = (f32[1,2,7,128]{3,2,1,0:T(8,128)S(1)}, f32[1,2,7,128]{3,2,1,0:T(8,128)S(1)}, u32[]{:S(2)}, u32[]{:S(2)}) collective-permute-start(f32[1,2,7,128]{3,2,1,0:T(8,128)S(1)} %get-tuple-element.23), channel_id=1, source_target_pairs={{0,1},{1,2},{2,3},{3,4},{4,5},{5,6},{6,7},{7,8},{8,9},{9,10},{10,1... | collective-permute-start | bytes 21512 | tf_op jit(solution)/shard_map/ppermute | solution.py:24
  95.5 5.6 %collective-permute-done.1 = f32[1,2,7,128]{3,2,1,0:T(8,128)S(1)} collective-permute-done((f32[1,2,7,128]{3,2,1,0:T(8,128)S(1)}, f32[1,2,7,128]{3,2,1,0:T(8,128)S(1)}, u32[]{:S(2)}, u32[]{:S(2)}) %collective-permute-start.1) | collective-permute-done | bytes 7200 | tf_op jit(solution)/shard_map/ppermute | solution.py:24
  101.0 0.9 fusion.31
  102.3 0.2 broadcast_multiply_fusion
  102.5 0.2 copy.41
  102.7 2.1 %fusion.25 = f32[1,512,512]{2,1,0:T(8,128)S(1)} fusion(f32[64,8,8,128]{3,2,1,0:T(8,128)S(1)} %bitcast.277), kind=kOutput, calls=%fused_computation.23 | convolution fusion | flops 1610612736 | bytes 3145728 | tf_op jit(solution)/shard_map/fik,fjk->fij/dot_general | solution.py:36
  104.9 1.0 all_to_all.61
  105.9 4.5 %all-to-all-start.3 = ((f32[16,1,4096]{2,1,0:T(1,128)}), f32[16,1,4096]{2,1,0:T(1,128)S(1)}, u32[]{:S(2)}, u32[]{:S(2)}) async-start(f32[16,1,4096]{2,1,0:T(1,128)} %all_to_all.61), calls=%async_computation.3 | async-start | bytes 524288 | tf_op jit(solution)/shard_map/all_to_all | solution.py:30
  110.4 1.6 copy.44
  112.0 5.2 %all-to-all-done.3 = f32[16,1,4096]{2,1,0:T(1,128)S(1)} async-done(((f32[16,1,4096]{2,1,0:T(1,128)}), f32[16,1,4096]{2,1,0:T(1,128)S(1)}, u32[]{:S(2)}, u32[]{:S(2)}) %all-to-all-start.3) | async-done | bytes 262176 | tf_op jit(solution)/shard_map/all_to_all | solution.py:30
  117.4 0.9 broadcast_in_dim.17
  118.3 5.3 %all-to-all-start.4 = ((f32[16,1,4096]{2,1,0:T(1,128)}), f32[16,1,4096]{2,1,0:T(1,128)S(1)}, u32[]{:S(2)}, u32[]{:S(2)}) async-start(f32[16,1,4096]{2,1,0:T(1,128)} %broadcast_in_dim.17), calls=%async_computation.4 | async-start | bytes 524288 | tf_op jit(solution)/shard_map/all_to_all | solution.py:32
  123.6 2.1 %fusion.1 = f32[1024,512]{0,1:T(8,128)S(1)} fusion(f32[64,8,8,128]{3,2,1,0:T(8,128)} %bitcast.272, f32[1024]{0:T(1024)S(1)} %broadcast_bitcast_fusion), kind=kLoop, calls=%fused_computation.3 | loop fusion | flops 524288 | bytes 4198400 | tf_op jit(solution)/shard_map/fjk,fkc->fjc/dot_general | solution.py:36
  125.7 1.9 %copy.60 = f32[1024,512]{1,0:T(8,128)} copy(f32[1024,512]{0,1:T(8,128)S(1)} %fusion.1) | data formatting | bytes 4194304 | tf_op jit(solution)/shard_map/fjk,fkc->fjc/dot_general | solution.py:36
  127.6 2.9 %all-to-all-done.4 = f32[16,1,4096]{2,1,0:T(1,128)S(1)} async-done(((f32[16,1,4096]{2,1,0:T(1,128)}), f32[16,1,4096]{2,1,0:T(1,128)S(1)}, u32[]{:S(2)}, u32[]{:S(2)}) %all-to-all-start.4) | async-done | bytes 262176 | tf_op jit(solution)/shard_map/all_to_all | solution.py:32
  130.4 0.6 reduce.3
  131.1 0.7 reshape.976.cov_ref
  131.8 22.3 %shard_map.38 = f32[1,80,512]{2,1,0:T(8,128)} custom-call(f32[1,256,256]{2,1,0:T(8,128)} %reshape.976.cov_ref, f32[1,80,512]{2,1,0:T(8,128)} %shard_map.37.start_ref), custom_call_target="tpu_custom_call" | custom-call | tf_op jit(solution)/shard_map/pallas_call | solution.py:160
  154.1 1.0 multiply_bitcast_fusion
  155.1 2.7 %convolution_bitcast_fusion = f32[8,128,80,1,1]{1,2,0,4,3:T(8,128)S(1)} fusion(f32[8,128,512]{2,1,0:T(8,128)} %bitcast.274, f32[1,80,512]{2,1,0:T(8,128)} %shard_map.38, f32[80]{0:T(128)S(1)} %compare_select_fusion), kind=kOutput, calls=%fused_computation.26 | convolution fusion | flops 251699200 | bytes 2588992 | tf_op jit(solution)/shard_map/fjk,fkc->fjc/dot_general | solution.py:36
  157.9 1.0 fusion.159
  158.9 1.4 fusion.39
  160.4 2.3 %collective-permute-start.3 = (f32[1,2,7,128]{3,2,1,0:T(8,128)S(1)}, f32[1,2,7,128]{3,2,1,0:T(8,128)S(1)}, u32[]{:S(2)}, u32[]{:S(2)}) collective-permute-start(f32[1,2,7,128]{3,2,1,0:T(8,128)S(1)} %slice.251), channel_id=1, source_target_pairs={{0,1},{1,2},{2,3},{3,4},{4,5},{5,6},{6,7},{7,8},{8,9},{9,10},{10,1... | collective-permute-start | bytes 21512 | tf_op jit(solution)/shard_map/ppermute | solution.py:24
  162.7 5.3 %collective-permute-done.3 = f32[1,2,7,128]{3,2,1,0:T(8,128)S(1)} collective-permute-done((f32[1,2,7,128]{3,2,1,0:T(8,128)S(1)}, f32[1,2,7,128]{3,2,1,0:T(8,128)S(1)}, u32[]{:S(2)}, u32[]{:S(2)}) %collective-permute-start.3) | collective-permute-done | bytes 7200 | tf_op jit(solution)/shard_map/ppermute | solution.py:24
  168.2 0.2 reshape.998
  168.4 7.7 %all_to_all.68 = f32[8,1,256]{2,1,0:T(1,128)S(1)} all-to-all(f32[8,1,256]{2,1,0:T(1,128)S(1)} %reshape.998), channel_id=1, replica_groups=mesh['freq'=8,'space'=16] {'freq'}, dimensions={0} | all-to-all | bytes 16384 | tf_op jit(solution)/shard_map/all_to_all | solution.py:240
  176.1 0.7 reduce.5
  176.8 0.2 reshape.999
  177.1 0.8 fusion.82
  177.9 1.8 fusion
  (50 shorter events, 2.1 us)
Async XLA Ops:
  0.0 1.2 copy-start
  5.7 9.6 %all-to-all-start = ((f32[8,1,256]{2,1,0:T(1,128)}), f32[8,1,256]{2,1,0:T(1,128)S(1)}, u32[]{:S(2)}, u32[]{:S(2)}) async-start(f32[8,1,256]{2,1,0:T(1,128)} %reshape.996), calls=%async_computation | async-start | bytes 16384 | tf_op jit(solution)/shard_map/all_to_all | solution.py:186
  16.7 7.2 %collective-permute-start = (f32[1,2,7,128]{3,2,1,0:T(8,128)S(1)}, f32[1,2,7,128]{3,2,1,0:T(8,128)S(1)}, u32[]{:S(2)}, u32[]{:S(2)}) collective-permute-start(f32[1,2,7,128]{3,2,1,0:T(8,128)S(1)} %bitcast.286), channel_id=1, source_target_pairs={{1,0},{2,1},{3,2},{4,3},{5,4},{6,5},{7,6},{8,7},{9,8},{10,9},{11,1... | collective-permute-start | bytes 21512 | tf_op jit(solution)/shard_map/ppermute | solution.py:24
  28.7 15.7 %all-to-all-start.1 = ((f32[16,1,4096]{2,1,0:T(1,128)}), f32[16,1,4096]{2,1,0:T(1,128)S(1)}, u32[]{:S(2)}, u32[]{:S(2)}) async-start(f32[16,1,4096]{2,1,0:T(1,128)} %all_to_all.60), calls=%async_computation.1 | async-start | bytes 524288 | tf_op jit(solution)/shard_map/all_to_all | solution.py:30
  45.5 12.1 %all-to-all-start.2 = ((f32[16,1,4096]{2,1,0:T(1,128)}), f32[16,1,4096]{2,1,0:T(1,128)S(1)}, u32[]{:S(2)}, u32[]{:S(2)}) async-start(f32[16,1,4096]{2,1,0:T(1,128)} %broadcast_in_dim.14), calls=%async_computation.2 | async-start | bytes 524288 | tf_op jit(solution)/shard_map/all_to_all | solution.py:32
  87.6 5.5 %collective-permute-start.2 = (f32[1,2,7,128]{3,2,1,0:T(8,128)S(1)}, f32[1,2,7,128]{3,2,1,0:T(8,128)S(1)}, u32[]{:S(2)}, u32[]{:S(2)}) collective-permute-start(f32[1,2,7,128]{3,2,1,0:T(8,128)S(1)} %slice.229), channel_id=1, source_target_pairs={{1,0},{2,1},{3,2},{4,3},{5,4},{6,5},{7,6},{8,7},{9,8},{10,9},{11,1... | collective-permute-start | bytes 21512 | tf_op jit(solution)/shard_map/ppermute | solution.py:24
  93.2 7.9 %collective-permute-start.1 = (f32[1,2,7,128]{3,2,1,0:T(8,128)S(1)}, f32[1,2,7,128]{3,2,1,0:T(8,128)S(1)}, u32[]{:S(2)}, u32[]{:S(2)}) collective-permute-start(f32[1,2,7,128]{3,2,1,0:T(8,128)S(1)} %get-tuple-element.23), channel_id=1, source_target_pairs={{0,1},{1,2},{2,3},{3,4},{4,5},{5,6},{6,7},{7,8},{8,9},{9,10},{10,1... | collective-permute-start | bytes 21512 | tf_op jit(solution)/shard_map/ppermute | solution.py:24
  105.9 11.3 %all-to-all-start.3 = ((f32[16,1,4096]{2,1,0:T(1,128)}), f32[16,1,4096]{2,1,0:T(1,128)S(1)}, u32[]{:S(2)}, u32[]{:S(2)}) async-start(f32[16,1,4096]{2,1,0:T(1,128)} %all_to_all.61), calls=%async_computation.3 | async-start | bytes 524288 | tf_op jit(solution)/shard_map/all_to_all | solution.py:30
  118.3 12.1 %all-to-all-start.4 = ((f32[16,1,4096]{2,1,0:T(1,128)}), f32[16,1,4096]{2,1,0:T(1,128)S(1)}, u32[]{:S(2)}, u32[]{:S(2)}) async-start(f32[16,1,4096]{2,1,0:T(1,128)} %broadcast_in_dim.17), calls=%async_computation.4 | async-start | bytes 524288 | tf_op jit(solution)/shard_map/all_to_all | solution.py:32
  158.9 18.2 %copy-start.1 = (s32[8]{0:T(128)S(1)}, s32[8]{0:T(128)}, u32[]{:S(2)}) copy-start(s32[8]{0:T(128)} %param.4) | copy-start | bytes 100
  160.4 7.7 %collective-permute-start.3 = (f32[1,2,7,128]{3,2,1,0:T(8,128)S(1)}, f32[1,2,7,128]{3,2,1,0:T(8,128)S(1)}, u32[]{:S(2)}, u32[]{:S(2)}) collective-permute-start(f32[1,2,7,128]{3,2,1,0:T(8,128)S(1)} %slice.251), channel_id=1, source_target_pairs={{0,1},{1,2},{2,3},{3,4},{4,5},{5,6},{6,7},{7,8},{8,9},{9,10},{10,1... | collective-permute-start | bytes 21512 | tf_op jit(solution)/shard_map/ppermute | solution.py:24
